TPU v7x, 32 devices: a whole 2x2x4 slice. The times are simulated.
32 devices in a mesh: row: 8 (over z, x), col: 4 (over y, core).
Axes of the slice: x: 2, y: 2, z: 4, core: 2. Of those that a mesh axis runs over, the one named last changes fastest.
Arguments:
- tokens: bfloat16 [1024, 87040], P('col', 'row'), may hold values from -6 to 6
- condition: bfloat16 [128, 1024], P('row', 'col'), may hold values from -6 to 6
- scale_ids: int32 [128, 680], P('row'), may hold values from 0 to 9, never falling along the last dimension, each value on 1 to 256 neighbouring positions
- attention_triple_matrix: bfloat16 [1024, 3, 1024], P('row', None, 'col'), may hold values from -0.1875 to 0.1875
- attention_triple_offset: bfloat16 [3, 1024], P(None, 'col'), may hold values from -1.75 to 1.75
- qk_gain: float32 [16], P('col'), may hold values from 8 to 20
- w_proj: bfloat16 [1024, 1024], P('row', 'col'), may hold values from -0.75 to 0.75
- b_proj: bfloat16 [1024], P('col'), may hold values from -1.75 to 1.75
- w_fc1: bfloat16 [1024, 4096], P('row', 'col'), may hold values from -0.1875 to 0.1875
- b_fc1: bfloat16 [4096], P('col'), may hold values from -1.75 to 1.75
- w_fc2: bfloat16 [4096, 1024], P('col', 'row'), may hold values from -0.09375 to 0.09375
- b_fc2: bfloat16 [1024], P('col'), may hold values from -1.75 to 1.75
- w_ada: bfloat16 [6, 1024, 1024], P(None, 'row', 'col'), may hold values from -0.1875 to 0.1875
- b_ada: bfloat16 [6, 1024], P(None, 'col'), may hold values from -3 to 3
- out_grad: bfloat16 [1024, 87040], P('col', 'row'), may hold values from -6 to 6
Outputs:
- layer_out: bfloat16 [1024, 87040], P('col', 'row')
- grad_tokens: bfloat16 [1024, 87040], P('col', 'row')
- grad_condition: bfloat16 [128, 1024], P('row', 'col')
- grad_w_qkv: float32 [1024, 3, 1024], P('row', None, 'col')
- grad_b_qkv: float32 [3, 1024], P(None, 'col')
- grad_qk_gain: float32 [16], P('col')
- grad_w_proj: float32 [1024, 1024], P('row', 'col')
- grad_b_proj: float32 [1024], P('col')
- grad_w_fc1: float32 [1024, 4096], P('row', 'col')
- grad_b_fc1: float32 [4096], P('col')
- grad_w_fc2: float32 [4096, 1024], P('col', 'row')
- grad_b_fc2: float32 [1024], P('col')
- grad_w_ada: float32 [6, 1024, 1024], P(None, 'row', 'col')
- grad_b_ada: float32 [6, 1024], P(None, 'col')
Inputs may be any that keep to these rules, and one draw needn't show every extreme that they name: Along each image's 680 tokens scale_ids never falls and takes every value from 0 to 9; one scale of each image has exactly 256 tokens and none has more.
All inputs are finite; a program needn't handle non-finite values.
Results may differ from a plain program's by a relative error of at most 0.018.
The roundings to bfloat16 on the way count: a program that leaves them out, or rounds other values in their place, can miss the bound.
Values may be sent and summed in bfloat16 or wider, within the bound.
A program may use at most 768 MiB of HBM per device.

v0:
```python
import jax
import jax.numpy as jnp
from jax import lax
from jax.sharding import PartitionSpec as P

D = 1024
HEAD_DIM = 64
LENGTH = 680
IMG_MB = 4
MICRO = 4


exact_arithmetic_mode = lax.Precision.HIGHEST


def to_heads(activation):
    return lax.all_to_all(activation, "col", split_axis=2, concat_axis=0, tiled=True)


def to_tokens(activation):
    return lax.all_to_all(activation, "col", split_axis=0, concat_axis=2, tiled=True)


def to_features(activation):
    return lax.all_to_all(activation, "col", split_axis=2, concat_axis=0, tiled=True)


def standardized_entries(vector):
    centered = vector - jnp.mean(vector, axis=1, keepdims=True)
    inv_std = lax.rsqrt(jnp.mean(centered * centered, axis=1, keepdims=True) + 1e-06)
    return (centered * inv_std, inv_std)


def norm_back(incoming, normed, inv_std):
    average = jnp.mean(incoming, axis=1, keepdims=True)
    cross = jnp.mean(incoming * normed, axis=1, keepdims=True)
    return inv_std * (incoming - average - normed * cross)


def gelu_back(pre_act, incoming):
    _, pullback = jax.vjp(lambda inner: jax.nn.gelu(inner, approximate=True), pre_act)
    return pullback(incoming)[0]


def score_block(queries_low, keys_low, allowed):
    scores = jnp.einsum(
        "bqhd,bkhd->bhqk", queries_low, keys_low, preferred_element_type=jnp.float32
    )
    return jnp.where(allowed[:, None], scores, -1e30)


def shards(
    tokens,
    condition,
    scale_ids,
    attention_triple_matrix,
    attention_triple_offset,
    qk_gain,
    w_proj,
    b_proj,
    w_fc1,
    b_fc1,
    w_fc2,
    b_fc2,
    w_ada,
    b_ada,
    out_grad,
):
    row_qkv, row_proj, row_fc1, row_fc2, row_ada = (
        lax.all_gather(attention_triple_matrix, "row", axis=0, tiled=True),
        lax.all_gather(w_proj, "row", axis=0, tiled=True),
        lax.all_gather(w_fc1, "row", axis=0, tiled=True),
        lax.all_gather(w_fc2, "row", axis=1, tiled=True),
        lax.all_gather(w_ada, "row", axis=1, tiled=True),
    )
    groups = lax.axis_size("col")
    place = lax.axis_index("col")
    heads_here = qk_gain.shape[0]
    width_here = tokens.shape[0]
    block_rows = IMG_MB * LENGTH
    share = block_rows // groups
    head_shape = (IMG_MB, LENGTH, heads_here, HEAD_DIM)
    cond_float = condition.astype(jnp.float32)
    cond_all = lax.all_gather(
        jax.nn.silu(cond_float).astype(jnp.bfloat16), "col", axis=1, tiled=True
    )
    mod_part = (
        jnp.einsum("ic,scd->isd", cond_all, row_ada, preferred_element_type=jnp.float32)
        + b_ada.astype(jnp.float32)[None]
    )
    modulation = lax.all_gather(mod_part, "col", axis=2, tiled=True)
    gain_cols = qk_gain[None, None, :, None]
    complete_query_key_value, whole_proj, bias_proj, bias_two, whole_fc1, whole_fc2, bias_one = (
        lax.all_gather(row_qkv, "col", axis=2, tiled=True),
        lax.all_gather(row_proj, "col", axis=1, tiled=True),
        lax.all_gather(b_proj, "col", axis=0, tiled=True),
        lax.all_gather(b_fc2, "col", axis=0, tiled=True),
        lax.all_gather(row_fc1, "col", axis=1, tiled=True),
        lax.all_gather(row_fc2, "col", axis=0, tiled=True),
        lax.all_gather(b_fc1, "col", axis=0, tiled=True),
    )
    bias_proj = bias_proj.astype(jnp.float32)
    bias_two = bias_two.astype(jnp.float32)
    bias_one = bias_one.astype(jnp.float32)
    bias_heads = attention_triple_offset.astype(jnp.float32)[None]
    positions = place * share + jnp.arange(share, dtype=jnp.int32)
    image_of = positions // LENGTH
    one_hot = (image_of[:, None] == jnp.arange(IMG_MB, dtype=jnp.int32)[None, :]).astype(
        jnp.float32
    )

    def expand(table):
        return jnp.dot(one_hot, table, precision=exact_arithmetic_mode)

    def per_image(rows_array):
        return jnp.dot(one_hot.T, rows_array, precision=exact_arithmetic_mode)

    acc_fc1 = jnp.zeros(whole_fc1.shape, jnp.float32)
    acc_fc2 = jnp.zeros(whole_fc2.shape, jnp.float32)
    acc_b1 = jnp.zeros(bias_one.shape, jnp.float32)
    acc_b2 = jnp.zeros((D,), jnp.float32)
    acc_qkv = jnp.zeros(complete_query_key_value.shape, jnp.float32)
    acc_bqkv = jnp.zeros(attention_triple_offset.shape, jnp.float32)
    acc_gain = jnp.zeros(qk_gain.shape, jnp.float32)
    acc_proj = jnp.zeros(whole_proj.shape, jnp.float32)
    acc_bproj = jnp.zeros((D,), jnp.float32)
    pieces_out = []
    pieces_grad = []
    pieces_mod = []
    for micro_index in range(MICRO):
        first_row = micro_index * block_rows
        leading_picture = micro_index * IMG_MB
        tok_cols, grad_cols_in = (
            lax.all_to_all(
                tokens[:, first_row : first_row + block_rows],
                "col",
                split_axis=1,
                concat_axis=0,
                tiled=True,
            ),
            lax.all_to_all(
                out_grad[:, first_row : first_row + block_rows],
                "col",
                split_axis=1,
                concat_axis=0,
                tiled=True,
            ),
        )
        tok_in = tok_cols.astype(jnp.float32).T
        grad_in = grad_cols_in.astype(jnp.float32).T
        scale_rows = scale_ids[leading_picture : leading_picture + IMG_MB]
        mod_block = modulation[leading_picture : leading_picture + IMG_MB]
        shift_attn = expand(mod_block[:, 0])
        scale_attn = expand(mod_block[:, 1])
        gate_attn = expand(mod_block[:, 2])
        shift_ffn = expand(mod_block[:, 3])
        scale_ffn = expand(mod_block[:, 4])
        gate_ffn = expand(mod_block[:, 5])
        normed_one, inv_std_one = standardized_entries(tok_in)
        initial_standardize = (normed_one * (1.0 + scale_attn) + shift_attn).astype(jnp.bfloat16)
        query_key_value_rows = jnp.einsum(
            "gt,tpf->gpf",
            initial_standardize,
            complete_query_key_value,
            preferred_element_type=jnp.float32,
        )
        qkv_local = to_heads(query_key_value_rows) + bias_heads
        queries = qkv_local[:, 0].reshape(head_shape)
        keys_raw = qkv_local[:, 1].reshape(head_shape)
        values_raw = qkv_local[:, 2].reshape(head_shape)
        query_inv = lax.rsqrt(jnp.sum(queries * queries, axis=-1, keepdims=True) + 1e-06)
        key_inv = lax.rsqrt(jnp.sum(keys_raw * keys_raw, axis=-1, keepdims=True) + 1e-06)
        queries_unit = queries * query_inv
        keys_unit = keys_raw * key_inv
        queries_low = (queries_unit * gain_cols).astype(jnp.bfloat16)
        keys_low = keys_unit.astype(jnp.bfloat16)
        values_low = values_raw.astype(jnp.bfloat16)
        allowed = scale_rows[:, None, :] <= scale_rows[:, :, None]
        masked = score_block(queries_low, keys_low, allowed)
        row_max = jnp.max(masked, axis=-1, keepdims=True)
        log_total = row_max + jnp.log(jnp.sum(jnp.exp(masked - row_max), axis=-1, keepdims=True))
        attn_prob = jnp.exp(masked - log_total)
        attended = jnp.einsum(
            "bhqk,bkhd->bqhd",
            attn_prob.astype(jnp.bfloat16),
            values_low,
            preferred_element_type=jnp.float32,
        )
        attended = attended.reshape(block_rows, 1, width_here).astype(jnp.bfloat16)
        attn_rows = to_tokens(attended)[:, 0]
        branch_one = jnp.dot(attn_rows, whole_proj, preferred_element_type=jnp.float32) + bias_proj
        residual = tok_in + gate_attn * branch_one
        normed_two, inv_std_two = standardized_entries(residual)
        ln_two = (normed_two * (1.0 + scale_ffn) + shift_ffn).astype(jnp.bfloat16)
        pre_act = jnp.dot(ln_two, whole_fc1, preferred_element_type=jnp.float32) + bias_one
        hidden = jax.nn.gelu(pre_act, approximate=True).astype(jnp.bfloat16)
        branch_two = jnp.dot(hidden, whole_fc2, preferred_element_type=jnp.float32) + bias_two
        layer_block = residual + gate_ffn * branch_two
        pieces_out.append(layer_block.astype(jnp.bfloat16))
        d_gate_ffn = per_image(grad_in * branch_two)
        d_branch_two = (gate_ffn * grad_in).astype(jnp.bfloat16)
        acc_b2 = acc_b2 + jnp.sum(d_branch_two.astype(jnp.float32), axis=0)
        acc_fc2 = acc_fc2 + jnp.einsum(
            "rf,rd->fd", hidden, d_branch_two, preferred_element_type=jnp.float32
        )
        d_hidden = jnp.einsum(
            "rd,fd->rf", d_branch_two, whole_fc2, preferred_element_type=jnp.float32
        )
        d_pre = gelu_back(pre_act, d_hidden).astype(jnp.bfloat16)
        acc_fc1 = acc_fc1 + jnp.einsum(
            "rd,rf->df", ln_two, d_pre, preferred_element_type=jnp.float32
        )
        acc_b1 = acc_b1 + jnp.sum(d_pre.astype(jnp.float32), axis=0)
        d_back = jnp.einsum("rf,df->rd", d_pre, whole_fc1, preferred_element_type=jnp.float32)
        d_shift_ffn = per_image(d_back)
        d_scale_ffn = per_image(d_back * normed_two)
        d_residual = grad_in + norm_back(d_back * (1.0 + scale_ffn), normed_two, inv_std_two)
        d_gate_attn = per_image(d_residual * branch_one)
        d_branch_one = (gate_attn * d_residual).astype(jnp.bfloat16)
        acc_proj = acc_proj + jnp.einsum(
            "rd,re->de", attn_rows, d_branch_one, preferred_element_type=jnp.float32
        )
        acc_bproj = acc_bproj + jnp.sum(d_branch_one.astype(jnp.float32), axis=0)
        d_attn_rows = jnp.einsum(
            "re,de->rd", d_branch_one, whole_proj, preferred_element_type=jnp.float32
        ).astype(jnp.bfloat16)
        d_attended = to_features(d_attn_rows[:, None, :]).reshape(head_shape)
        masked = score_block(queries_low, keys_low, allowed)
        attn_prob = jnp.exp(masked - log_total)
        d_values = jnp.einsum(
            "bhqk,bqhd->bkhd",
            attn_prob.astype(jnp.bfloat16),
            d_attended,
            preferred_element_type=jnp.float32,
        )
        d_prob = jnp.einsum(
            "bqhd,bkhd->bhqk", d_attended, values_low, preferred_element_type=jnp.float32
        )
        d_scores = (
            attn_prob * (d_prob - jnp.sum(attn_prob * d_prob, axis=-1, keepdims=True))
        ).astype(jnp.bfloat16)
        d_queries_low = jnp.einsum(
            "bhqk,bkhd->bqhd", d_scores, keys_low, preferred_element_type=jnp.float32
        )
        d_keys_low = jnp.einsum(
            "bhqk,bqhd->bkhd", d_scores, queries_low, preferred_element_type=jnp.float32
        )
        acc_gain = acc_gain + jnp.sum(d_queries_low * queries_unit, axis=(0, 1, 3))
        d_query_unit = d_queries_low * gain_cols
        d_queries = query_inv * (
            d_query_unit
            - queries_unit * jnp.sum(d_query_unit * queries_unit, axis=-1, keepdims=True)
        )
        d_keys = key_inv * (
            d_keys_low - keys_unit * jnp.sum(d_keys_low * keys_unit, axis=-1, keepdims=True)
        )
        d_qkv = jnp.stack(
            [
                d_queries.reshape(block_rows, width_here),
                d_keys.reshape(block_rows, width_here),
                d_values.reshape(block_rows, width_here),
            ],
            axis=1,
        ).astype(jnp.bfloat16)
        acc_bqkv = acc_bqkv + jnp.sum(d_qkv.astype(jnp.float32), axis=0)
        query_key_value_grad_rows = to_tokens(d_qkv)
        acc_qkv = acc_qkv + jnp.einsum(
            "hi,hof->iof",
            initial_standardize,
            query_key_value_grad_rows,
            preferred_element_type=jnp.float32,
        )
        d_ln_one = jnp.einsum(
            "fcn,icn->fi",
            query_key_value_grad_rows,
            complete_query_key_value,
            preferred_element_type=jnp.float32,
        )
        d_shift_attn = per_image(d_ln_one)
        d_scale_attn = per_image(d_ln_one * normed_one)
        d_tokens = d_residual + norm_back(d_ln_one * (1.0 + scale_attn), normed_one, inv_std_one)
        pieces_grad.append(d_tokens.astype(jnp.bfloat16))
        pieces_mod.append(
            jnp.stack(
                [d_shift_attn, d_scale_attn, d_gate_attn, d_shift_ffn, d_scale_ffn, d_gate_ffn],
                axis=1,
            )
        )
    home = to_features(jnp.stack(pieces_out + pieces_grad, axis=1))
    layer_out = jnp.concatenate([home[:, index].T for index in range(MICRO)], axis=1)
    grad_tokens = jnp.concatenate([home[:, MICRO + index].T for index in range(MICRO)], axis=1)
    d_mod_part = jnp.concatenate(pieces_mod, axis=0)
    acc_qkv, acc_proj, acc_bproj, acc_b2, d_mod_sum, acc_fc1, acc_fc2, acc_b1 = (
        lax.psum_scatter(
            acc_qkv.astype(jnp.bfloat16), "col", scatter_dimension=2, tiled=True
        ).astype(jnp.float32),
        lax.psum_scatter(
            acc_proj.astype(jnp.bfloat16), "col", scatter_dimension=1, tiled=True
        ).astype(jnp.float32),
        lax.psum_scatter(
            acc_bproj.astype(jnp.bfloat16), "col", scatter_dimension=0, tiled=True
        ).astype(jnp.float32),
        lax.psum_scatter(
            acc_b2.astype(jnp.bfloat16), "col", scatter_dimension=0, tiled=True
        ).astype(jnp.float32),
        lax.psum_scatter(
            d_mod_part.astype(jnp.bfloat16), "col", scatter_dimension=2, tiled=True
        ).astype(jnp.float32),
        lax.psum_scatter(
            acc_fc1.astype(jnp.bfloat16), "col", scatter_dimension=1, tiled=True
        ).astype(jnp.float32),
        lax.psum_scatter(
            acc_fc2.astype(jnp.bfloat16), "col", scatter_dimension=0, tiled=True
        ).astype(jnp.float32),
        lax.psum_scatter(
            acc_b1.astype(jnp.bfloat16), "col", scatter_dimension=0, tiled=True
        ).astype(jnp.float32),
    )
    d_mod = d_mod_sum.astype(jnp.bfloat16)
    grad_ada = jnp.einsum("ic,isd->scd", cond_all, d_mod, preferred_element_type=jnp.float32)
    bias_ada = jnp.sum(d_mod.astype(jnp.float32), axis=0)
    d_soft = lax.psum_scatter(
        jnp.einsum("isd,scd->ic", d_mod, row_ada, preferred_element_type=jnp.float32).astype(
            jnp.bfloat16
        ),
        "col",
        scatter_dimension=1,
        tiled=True,
    ).astype(jnp.float32)
    _, silu_pull = jax.vjp(jax.nn.silu, cond_float)
    grad_condition = silu_pull(d_soft)[0].astype(jnp.bfloat16)
    grad_qkv, grad_proj, grad_fc1, grad_fc2, grad_ada = (
        lax.psum_scatter(
            acc_qkv.astype(jnp.bfloat16), "row", scatter_dimension=0, tiled=True
        ).astype(jnp.float32),
        lax.psum_scatter(
            acc_proj.astype(jnp.bfloat16), "row", scatter_dimension=0, tiled=True
        ).astype(jnp.float32),
        lax.psum_scatter(
            acc_fc1.astype(jnp.bfloat16), "row", scatter_dimension=0, tiled=True
        ).astype(jnp.float32),
        lax.psum_scatter(
            acc_fc2.astype(jnp.bfloat16), "row", scatter_dimension=1, tiled=True
        ).astype(jnp.float32),
        lax.psum_scatter(
            grad_ada.astype(jnp.bfloat16), "row", scatter_dimension=1, tiled=True
        ).astype(jnp.float32),
    )
    grad_bqkv, grad_gain, grad_bproj, grad_b1, grad_b2, grad_bada = lax.psum(
        (acc_bqkv, acc_gain, acc_bproj, acc_b1, acc_b2, bias_ada), "row"
    )
    return (
        layer_out,
        grad_tokens,
        grad_condition,
        grad_qkv,
        grad_bqkv,
        grad_gain,
        grad_proj,
        grad_bproj,
        grad_fc1,
        grad_b1,
        grad_fc2,
        grad_b2,
        grad_ada,
        grad_bada,
    )


def solution(mesh):
    placed = (
        P("col", "row"),
        P("row", "col"),
        P("row", None),
        P("row", None, "col"),
        P(None, "col"),
        P("col"),
        P("row", "col"),
        P("col"),
        P("row", "col"),
        P("col"),
        P("col", "row"),
        P("col"),
        P(None, "row", "col"),
        P(None, "col"),
        P("col", "row"),
    )
    return jax.shard_map(
        shards,
        mesh=mesh,
        in_specs=placed,
        out_specs=(
            P("col", "row"),
            P("col", "row"),
            P("row", "col"),
            P("row", None, "col"),
            P(None, "col"),
            P("col"),
            P("row", "col"),
            P("col"),
            P("row", "col"),
            P("col"),
            P("col", "row"),
            P("col"),
            P(None, "row", "col"),
            P(None, "col"),
        ),
        check_vma=False,
    )
```

profile of v0, /device:TPU:0, one launch (start us, length us, event | category | flops | bytes accessed | tf_op | source)
XLA Modules:
  0.0 3461.4 jit_solution(8351395032820483853)
XLA Ops:
  8.7 48.4 %all-gather.13.cloned.1.call-done = bf16[1024,3,256]{2,0,1:T(8,128)(2,1)} async-done(((bf16[128,3,256]{2,0,1:T(8,128)(2,1)}), bf16[1024,3,256]{2,0,1:T(8,128)(2,1)}) %all-gather.13.cloned.1.call-update) | async-done | bytes 1572880 | tf_op jit(solution)/shard_map/all_gather | solution.py:70
  71.6 16.5 all-to-all-done.9
  94.1 15.6 all-to-all-done.6
  115.9 17.4 all-to-all-done.3
  146.6 23.6 all-to-all-done
  199.3 19.1 all_gather.42
  227.6 18.2 all_gather.44
  315.2 111.0 %all-to-all-done.1 = f32[680,3,1024]{0,1,2:T(4,128)} async-done(((f32[680,3,1024]{0,1,2:T(4,128)}), f32[680,3,1024]{0,1,2:T(4,128)}, u32[]{:S(2)}, u32[]{:S(2)}) %all-to-all-start.1) | async-done | bytes 8355872 | tf_op jit(solution)/shard_map/all_to_all | solution.py:17
  432.6 33.3 all_gather.47
  496.3 130.5 %all-to-all-done.4 = f32[680,3,1024]{0,1,2:T(4,128)} async-done(((f32[680,3,1024]{0,1,2:T(4,128)}), f32[680,3,1024]{0,1,2:T(4,128)}, u32[]{:S(2)}, u32[]{:S(2)}) %all-to-all-start.4) | async-done | bytes 8355872 | tf_op jit(solution)/shard_map/all_to_all | solution.py:17
  659.7 111.7 %all-to-all-done.7 = f32[680,3,1024]{0,1,2:T(4,128)} async-done(((f32[680,3,1024]{0,1,2:T(4,128)}), f32[680,3,1024]{0,1,2:T(4,128)}, u32[]{:S(2)}, u32[]{:S(2)}) %all-to-all-start.7) | async-done | bytes 8355872 | tf_op jit(solution)/shard_map/all_to_all | solution.py:17
  778.0 138.9 %all-gather.1 = bf16[4,1,256]{2,1,0:T(2,128)(2,1)S(1)} all-gather(bf16[1,1,256]{2,1,0:T(2,128)(2,1)S(1)} %reshape.448), channel_id=1, replica_groups=mesh['row'=8,'col'=4] {'col'}, dimensions={0}, use_global_device_ids=true | all-gather | bytes 2560 | tf_op jit(solution)/shard_map/all_gather | solution.py:97
  1009.7 19.9 bitcast_add_fusion
  1158.4 17.0 select_reduce_fusion.1
  1189.6 16.8 fusion.130
  1223.0 16.2 reduce.14
  1247.2 15.5 select_reduce_fusion
  1277.1 15.6 select_reduce_fusion.3
  1337.9 16.2 fusion.131
  1396.8 16.0 fusion.128
  1455.2 16.0 fusion.129
  1725.1 50.7 %convert_reduce_fusion = (f32[4096]{0:T(1024)}, bf16[680,4096]{1,0:T(8,128)(2,1)}, f32[4096]{0:T(1024)}, bf16[680,4096]{1,0:T(8,128)(2,1)}, f32[4096]{0:T(1024)}...) fusion(f32[680,4096]{1,0:T(8,128)} %fusion.485, f32[4096]{0:T(1024)S(1)} %copy-done.279, ...), kind=kOutput, calls=%fused_computation.71 | convolution fusion | flops 5960482816 | bytes 110133248 | tf_op jit(solution)/shard_map/rd,fd->rf/dot_general | solution.py:206
  1989.9 16.3 fusion.132
  2006.2 27.7 multiply_reduce_fusion.3
  2034.0 28.6 multiply_convert_fusion.3
  2101.4 16.3 fusion.134
  2117.8 27.6 multiply_reduce_fusion.1
  2145.5 28.9 multiply_convert_fusion.1
  2212.9 16.2 fusion.133
  2229.2 27.7 multiply_reduce_fusion.2
  2256.9 28.6 multiply_convert_fusion.2
  2319.9 30.5 multiply_reduce_fusion
  2350.4 28.5 multiply_convert_fusion
  2560.6 16.2 fusion.135
  2622.9 22.2 all-to-all-done.20
  2673.0 40.5 %all-to-all-done.17 = bf16[2720,3,256]{2,1,0:T(4,128)(2,1)} async-done(((bf16[2720,3,256]{2,1,0:T(4,128)(2,1)}), bf16[2720,3,256]{2,1,0:T(4,128)(2,1)}, u32[]{:S(2)}, u32[]{:S(2)}) %all-to-all-start.17) | async-done | bytes 4177952 | tf_op jit(solution)/shard_map/all_to_all | solution.py:21
  2758.0 23.6 all-to-all-done.23
  2843.8 19.4 add_convert_fusion.2
  2906.5 26.7 add_convert_fusion
  2989.3 24.3 add_convert_fusion.1
  3034.3 17.7 copy.835
  3065.6 138.4 %all-reduce.4 = (bf16[1024]{0:T(1024)(128)(2,1)S(1)}, bf16[4096]{0:T(1024)(128)(2,1)S(1)}, bf16[1024]{0:T(1024)(128)(2,1)S(1)}) all-reduce(bf16[1024]{0:T(1024)(128)(2,1)S(1)} %add_convert_fusion.22, bf16[4096]{0:T(1024)(128)(2,1)S(1)} %add_convert_fusion.20, ...), channel_id=8, replica_groups=mesh['row'=8,'col'=4] {'col'}, use_global_device_ids=true, to_apply=%region_80.81.clone | all-reduce | flops 6144 | bytes 24576
  3213.8 36.7 %all-reduce.3 = (f32[3,256]{1,0:T(4,128)}, f32[4]{0:T(128)}, f32[256]{0:T(256)}, f32[1024]{0:T(1024)}, f32[256]{0:T(256)}, /*index=5*/f32[6,256]{1,0:T(8,128)}) all-reduce(f32[3,256]{1,0:T(4,128)S(1)} %add_add_fusion, f32[4]{0:T(128)S(1)} %add_add_fusion.1, ...), channel_id=1, replica_groups=mesh['row'=8,'col'=4] {'row'}, use_global_device_ids=true, to_apply=%region_68.69 | all-reduce | flops 3844 | bytes 30752 | tf_op jit(solution)/shard_map/psum | solution.py:349
  3256.1 23.7 copy.873
  3291.1 38.2 %fusion.466 = (bf16[2720,1,256]{2,1,0:T(2,128)(2,1)S(1)}, bf16[2720,1,256]{2,1,0:T(2,128)(2,1)S(1)}, bf16[2720,1,256]{2,1,0:T(2,128)(2,1)S(1)}, bf16[2720,1,256]...) fusion(bf16[2720,8,256]{2,1,0:T(8,128)(2,1)} %bitcast.1018), kind=kLoop, calls=%fused_computation.679 | loop fusion | bytes 22282240 | tf_op jit(solution)/shard_map/slice | solution.py:291
  3330.3 32.5 pad_maximum_fusion.1
  3375.8 32.1 pad_maximum_fusion
  3419.8 33.1 reduce-scatter.30.cloned.1.call-done
  (1172 shorter events, 1755.5 us)
Async XLA Ops:
  7.2 49.9 %all-gather.13.cloned.1.call-start = ((), (), s32[]{:S(2)}) async-start(), calls=%async_computation.37 | async-start | bytes 1769472 | tf_op jit(solution)/shard_map/all_gather | solution.py:70
  7.9 217.3 %all-gather.11.cloned.1.call-start = ((), (), s32[]{:S(2)}) async-start(), calls=%async_computation.36 | async-start | bytes 3538944 | tf_op jit(solution)/shard_map/all_gather | solution.py:74
  8.7 249.3 %all-gather.15.cloned.1.call-start = ((), (), s32[]{:S(2)}) async-start(), calls=%async_computation.38 | async-start | bytes 7864320 | tf_op jit(solution)/shard_map/all_gather | solution.py:94
  66.4 21.7 all-to-all-start.9
  88.1 21.7 all-to-all-start.6
  109.7 23.6 all-to-all-start.3
  133.3 36.9 %all-to-all-start = ((bf16[256,4,680]{0,2,1:T(8,128)(2,1)}), bf16[256,4,680]{0,2,1:T(8,128)(2,1)S(1)}, u32[]{:S(2)}, u32[]{:S(2)}) async-start(bf16[256,4,680]{0,2,1:T(8,128)(2,1)} %bitcast.1067), calls=%async_computation | async-start | bytes 2785280 | tf_op jit(solution)/shard_map/all_to_all | solution.py:134
  170.2 24.7 all-to-all-start.21
  173.8 294.7 %all-gather.19.cloned.1.call-start = ((), (), s32[]{:S(2)}) async-start(), calls=%async_computation.40 | async-start | bytes 2359296 | tf_op jit(solution)/shard_map/all_gather | solution.py:72
  195.0 25.4 all-to-all-start.18
  218.5 736.9 %copy-start.123 = (s32[680]{0:T(1024)}, s32[680]{0:T(1024)S(1)}, u32[]{:S(2)}) copy-start(s32[680]{0:T(1024)S(1)} %add_select_fusion) | copy-start | bytes 8164
  220.4 28.2 all-to-all-start.15
  245.8 709.6 %copy-start.150 = (f32[16,6,1024]{2,0,1:T(8,128)}, f32[16,6,1024]{2,0,1:T(8,128)S(1)}, u32[]{:S(2)}) copy-start(f32[16,6,1024]{2,0,1:T(8,128)S(1)} %all_gather.44) | copy-start | bytes 1179652
  248.6 33.0 all-to-all-start.12
  281.6 144.6 %all-to-all-start.1 = ((f32[680,3,1024]{0,1,2:T(4,128)}), f32[680,3,1024]{0,1,2:T(4,128)}, u32[]{:S(2)}, u32[]{:S(2)}) async-start(f32[680,3,1024]{0,1,2:T(4,128)} %copy.709), calls=%async_computation.1 | async-start | bytes 25165824 | tf_op jit(solution)/shard_map/all_to_all | solution.py:17
  288.1 661.5 %all-gather.23.cloned.1.call-start = ((), (), s32[]{:S(2)}) async-start(), calls=%async_computation.42 | async-start | bytes 2359296 | tf_op jit(solution)/shard_map/all_gather | solution.py:73
  426.2 200.6 %all-to-all-start.4 = ((f32[680,3,1024]{0,1,2:T(4,128)}), f32[680,3,1024]{0,1,2:T(4,128)}, u32[]{:S(2)}, u32[]{:S(2)}) async-start(f32[680,3,1024]{0,1,2:T(4,128)} %copy.726), calls=%async_computation.4 | async-start | bytes 25165824 | tf_op jit(solution)/shard_map/all_to_all | solution.py:17
  432.6 1099.8 %all-gather.17.cloned.1.call-start = ((), (), s32[]{:S(2)}) async-start(), calls=%async_computation.39 | async-start | bytes 2621440 | tf_op jit(solution)/shard_map/all_gather | solution.py:95
  465.9 1114.1 %all-gather.21.cloned.1.call-start = ((), (), s32[]{:S(2)}) async-start(), calls=%async_computation.41 | async-start | bytes 10485760 | tf_op jit(solution)/shard_map/all_gather | solution.py:98
  626.8 144.5 %all-to-all-start.7 = ((f32[680,3,1024]{0,1,2:T(4,128)}), f32[680,3,1024]{0,1,2:T(4,128)}, u32[]{:S(2)}, u32[]{:S(2)}) async-start(f32[680,3,1024]{0,1,2:T(4,128)} %copy.743), calls=%async_computation.7 | async-start | bytes 25165824 | tf_op jit(solution)/shard_map/all_to_all | solution.py:17
  659.7 263.4 %copy-start.299 = (bf16[1024]{0:T(1024)(128)(2,1)S(1)}, bf16[1024]{0:T(1024)(128)(2,1)}, u32[]{:S(2)}) copy-start(bf16[1024]{0:T(1024)(128)(2,1)} %param.24) | copy-start | bytes 6148
  659.7 269.2 %copy-start.268 = (s32[16,680]{1,0:T(8,128)S(1)}, s32[16,680]{1,0:T(8,128)}, u32[]{:S(2)}) copy-start(s32[16,680]{1,0:T(8,128)} %param.17) | copy-start | bytes 130564
  771.4 225.5 %all-to-all-start.10 = ((f32[680,3,1024]{0,1,2:T(4,128)}), f32[680,3,1024]{0,1,2:T(4,128)}, u32[]{:S(2)}, u32[]{:S(2)}) async-start(f32[680,3,1024]{0,1,2:T(4,128)} %copy.760), calls=%async_computation.10 | async-start | bytes 25165824 | tf_op jit(solution)/shard_map/all_to_all | solution.py:17
  777.9 813.4 %all-gather.25.cloned.1.call-start = ((), (), s32[]{:S(2)}) async-start(), calls=%async_computation.43 | async-start | bytes 10485760 | tf_op jit(solution)/shard_map/all_gather | solution.py:99
  1242.8 149.2 %all-to-all-start.8 = ((bf16[4,2,87040]{2,1,0:T(2,128)(2,1)}), bf16[4,2,87040]{2,1,0:T(2,128)(2,1)}, u32[]{:S(2)}, u32[]{:S(2)}) async-start(bf16[4,2,87040]{2,1,0:T(2,128)(2,1)} %reshape.485), calls=%async_computation.8 | async-start | bytes 2785280 | tf_op jit(solution)/shard_map/all_to_all | solution.py:21
  1392.0 58.7 %all-to-all-start.11 = ((bf16[4,2,87040]{2,1,0:T(2,128)(2,1)}), bf16[4,2,87040]{2,1,0:T(2,128)(2,1)}, u32[]{:S(2)}, u32[]{:S(2)}) async-start(bf16[4,2,87040]{2,1,0:T(2,128)(2,1)} %reshape.481), calls=%async_computation.11 | async-start | bytes 2785280 | tf_op jit(solution)/shard_map/all_to_all | solution.py:21
  1450.7 46.5 %all-to-all-start.2 = ((bf16[4,2,87040]{2,1,0:T(2,128)(2,1)}), bf16[4,2,87040]{2,1,0:T(2,128)(2,1)}, u32[]{:S(2)}, u32[]{:S(2)}) async-start(bf16[4,2,87040]{2,1,0:T(2,128)(2,1)} %reshape.493), calls=%async_computation.2 | async-start | bytes 2785280 | tf_op jit(solution)/shard_map/all_to_all | solution.py:21
  1497.2 30.9 all-to-all-start.5
  1857.2 116.9 %all-to-all-start.13 = ((bf16[4,2,87040]{2,1,0:T(2,128)(2,1)}), bf16[4,2,87040]{2,1,0:T(2,128)(2,1)}, u32[]{:S(2)}, u32[]{:S(2)}) async-start(bf16[4,2,87040]{2,1,0:T(2,128)(2,1)} %reshape.495), calls=%async_computation.13 | async-start | bytes 2785280 | tf_op jit(solution)/shard_map/all_to_all | solution.py:25
  1974.1 111.5 %all-to-all-start.19 = ((bf16[4,2,87040]{2,1,0:T(2,128)(2,1)}), bf16[4,2,87040]{2,1,0:T(2,128)(2,1)}, u32[]{:S(2)}, u32[]{:S(2)}) async-start(bf16[4,2,87040]{2,1,0:T(2,128)(2,1)} %reshape.487), calls=%async_computation.19 | async-start | bytes 2785280 | tf_op jit(solution)/shard_map/all_to_all | solution.py:25
  2085.6 111.5 %all-to-all-start.16 = ((bf16[4,2,87040]{2,1,0:T(2,128)(2,1)}), bf16[4,2,87040]{2,1,0:T(2,128)(2,1)}, u32[]{:S(2)}, u32[]{:S(2)}) async-start(bf16[4,2,87040]{2,1,0:T(2,128)(2,1)} %reshape.491), calls=%async_computation.16 | async-start | bytes 2785280 | tf_op jit(solution)/shard_map/all_to_all | solution.py:25
  2197.1 111.2 %all-to-all-start.22 = ((bf16[4,2,87040]{2,1,0:T(2,128)(2,1)}), bf16[4,2,87040]{2,1,0:T(2,128)(2,1)}, u32[]{:S(2)}, u32[]{:S(2)}) async-start(bf16[4,2,87040]{2,1,0:T(2,128)(2,1)} %reshape.483), calls=%async_computation.22 | async-start | bytes 2785280 | tf_op jit(solution)/shard_map/all_to_all | solution.py:25
  2464.3 112.5 %all-to-all-start.14 = ((bf16[2720,3,256]{2,1,0:T(4,128)(2,1)}), bf16[2720,3,256]{2,1,0:T(4,128)(2,1)}, u32[]{:S(2)}, u32[]{:S(2)}) async-start(bf16[2720,3,256]{2,1,0:T(4,128)(2,1)} %copy.787), calls=%async_computation.14 | async-start | bytes 11141120 | tf_op jit(solution)/shard_map/all_to_all | solution.py:21
  2576.8 68.2 %all-to-all-start.20 = ((bf16[2720,3,256]{2,1,0:T(4,128)(2,1)}), bf16[2720,3,256]{2,1,0:T(4,128)(2,1)}, u32[]{:S(2)}, u32[]{:S(2)}) async-start(bf16[2720,3,256]{2,1,0:T(4,128)(2,1)} %copy.817), calls=%async_computation.20 | async-start | bytes 11141120 | tf_op jit(solution)/shard_map/all_to_all | solution.py:21
  2645.1 68.5 %all-to-all-start.17 = ((bf16[2720,3,256]{2,1,0:T(4,128)(2,1)}), bf16[2720,3,256]{2,1,0:T(4,128)(2,1)}, u32[]{:S(2)}, u32[]{:S(2)}) async-start(bf16[2720,3,256]{2,1,0:T(4,128)(2,1)} %copy.802), calls=%async_computation.17 | async-start | bytes 11141120 | tf_op jit(solution)/shard_map/all_to_all | solution.py:21
  2713.5 68.1 %all-to-all-start.23 = ((bf16[2720,3,256]{2,1,0:T(4,128)(2,1)}), bf16[2720,3,256]{2,1,0:T(4,128)(2,1)}, u32[]{:S(2)}, u32[]{:S(2)}) async-start(bf16[2720,3,256]{2,1,0:T(4,128)(2,1)} %copy.832), calls=%async_computation.23 | async-start | bytes 11141120 | tf_op jit(solution)/shard_map/all_to_all | solution.py:21
  2718.7 214.5 %reduce-scatter.16.cloned.1.call-start = ((), (), s32[]{:S(2)}) async-start(), calls=%async_computation.44 | async-start | bytes 245760 | tf_op jit(solution)/shard_map/reduce_scatter | solution.py:306
  2809.0 128.4 %reduce-scatter.24.cloned.1.call-start = ((), (), s32[]{:S(2)}) async-start(), calls=%async_computation.48 | async-start | bytes 2621440 | tf_op jit(solution)/shard_map/reduce_scatter | solution.py:297
  2817.2 241.5 %reduce-scatter.20.cloned.1.call-start = ((), (), s32[]{:S(2)}) async-start(), calls=%async_computation.46 | async-start | bytes 7864320 | tf_op jit(solution)/shard_map/reduce_scatter | solution.py:294
  2863.2 196.3 %reduce-scatter.32.cloned.1.call-start = ((), (), s32[]{:S(2)}) async-start(), calls=%async_computation.52 | async-start | bytes 10485760 | tf_op jit(solution)/shard_map/reduce_scatter | solution.py:312
  2933.1 317.3 %reduce-scatter.18.cloned.1.call-start = ((), (), s32[]{:S(2)}) async-start(), calls=%async_computation.45 | async-start | bytes 40960 | tf_op jit(solution)/shard_map/reduce_scatter | solution.py:322
  2937.4 314.4 %reduce-scatter.26.cloned.1.call-start = ((), (), s32[]{:S(2)}) async-start(), calls=%async_computation.49 | async-start | bytes 589824 | tf_op jit(solution)/shard_map/reduce_scatter | solution.py:336
  2938.0 315.3 %reduce-scatter.36.cloned.1.call-start = ((), (), s32[]{:S(2)}) async-start(), calls=%async_computation.54 | async-start | bytes 3538944
  2961.7 329.4 %reduce-scatter.28.cloned.1.call-start = ((), (), s32[]{:S(2)}) async-start(), calls=%async_computation.50 | async-start | bytes 10485760 | tf_op jit(solution)/shard_map/reduce_scatter | solution.py:309
  3052.1 204.0 %all-to-all-start.24 = ((bf16[680,8,1024]{0,1,2:T(8,128)(2,1)}), bf16[680,8,1024]{0,1,2:T(8,128)(2,1)}, u32[]{:S(2)}, u32[]{:S(2)}) async-start(bf16[680,8,1024]{0,1,2:T(8,128)(2,1)} %copy.835), calls=%async_computation.24 | async-start | bytes 25165824 | tf_op jit(solution)/shard_map/all_to_all | solution.py:25
  3058.7 357.5 %reduce-scatter.22.cloned.1.call-start = ((), (), s32[]{:S(2)}) async-start(), calls=%async_computation.47 | async-start | bytes 1769472 | tf_op jit(solution)/shard_map/reduce_scatter | solution.py:333
  3059.4 358.4 %reduce-scatter.34.cloned.1.call-start = ((), (), s32[]{:S(2)}) async-start(), calls=%async_computation.53 | async-start | bytes 2359296
  3063.5 389.4 %reduce-scatter.30.cloned.1.call-start = ((), (), s32[]{:S(2)}) async-start(), calls=%async_computation.51 | async-start | bytes 2359296 | tf_op jit(solution)/shard_map/reduce_scatter | solution.py:339
  (319 other events, 5570.7 us)
Sparse Core Ops, SparseCore 0:
  10.2 46.8 all-gather.12
  59.3 59.3 all-gather.10
  120.2 65.2 all-gather.14
  187.4 50.6 all-gather.18
  290.7 50.5 all-gather.22
  466.0 34.0 all-gather.16
  501.7 103.3 all-gather.20
  949.8 56.6 all-gather.24
  2809.1 18.3 reduce-scatter.15
  2829.9 31.4 reduce-scatter.23
  2864.1 58.3 reduce-scatter.19
  2933.3 70.7 reduce-scatter.31
  3007.2 19.3 reduce-scatter.17
  3029.7 61.8 reduce-scatter.25
  3095.5 73.2 reduce-scatter.35
  3171.5 71.7 reduce-scatter.27
  3246.6 65.1 reduce-scatter.21
  3315.6 66.7 reduce-scatter.33
  3386.3 66.6 reduce-scatter.29
where the time goes:
time: 3480 us; the launch traced here: 3460 us
  matrix products  1010 us (29%)
  local copies, waits for them, and re-layouts  789 us (23%)
  waiting for transfers between devices  611 us (18%)
  other arithmetic  513 us (15%)
  blocking collectives  395 us (11%)
  starting transfers between devices  121 us (3%)
    all_to_all x4, waiting for transfers between devices, to_heads(): lax.all_to_all(activation, 'col', split_axis=2, concat_axis=0, tiled=True)  353 us
    unnamed x710, local copies, waits for them, and re-layouts  209 us
    all_gather x1, blocking collectives, shards(): lax.all_gather(b_fc2, 'col', axis=0, tiled=True)  139 us
    unnamed x1, blocking collectives  138 us
    convert_element_type x4, other arithmetic, shards(): d_scores = (attn_prob * (d_prob - jnp.sum(attn_prob * d_prob, axis=-1, ke...  115 us
    dot_general x4, matrix products, shards(): jnp.einsum('bqhd,bkhd->bhqk', d_attended, values_low, preferred_element_t...  114 us
    another operation x20, local copies, waits for them, and re-layouts, shards(): jnp.stack([d_queries.reshape(block_rows, width_here), d_keys.reshape(bloc...  88.7 us
    all_to_all x8, waiting for transfers between devices, to_tokens(): lax.all_to_all(activation, 'col', split_axis=0, concat_axis=2, tiled=True)  86.3 us
  transfers between devices with their start and end apart: 44, of which 13 were waited for; matrix products, arithmetic and copies ran while one was open for 52% of the time, Pallas kernels for 0%

commit v1 on v0

v1 whole, which is shorter than its diff:
```python
import functools
import jax
import jax.numpy as jnp
from jax import lax
from jax.sharding import PartitionSpec as P
from jax.experimental import pallas as pl
from jax.experimental.pallas import tpu as pltpu

HEAD_DIM = 64
PAIR = 2 * HEAD_DIM
NEG = -1024.0
FIRST_EXTRA = 16


def head_sums(values, left):
    first = jnp.sum(jnp.where(left, values, 0.0), axis=-1, keepdims=True)
    second = jnp.sum(jnp.where(left, 0.0, values), axis=-1, keepdims=True)
    return first, second


def unit_of(raw, left):
    first, second = head_sums(raw * raw, left)
    inverse = jnp.where(left, lax.rsqrt(first + 1e-06), lax.rsqrt(second + 1e-06))
    return raw * inverse, inverse


def nt(left_rows, right_rows):
    return lax.dot_general(
        left_rows, right_rows, (((1,), (1,)), ((), ())), preferred_element_type=jnp.float32
    )


def nn(left_rows, right_rows):
    return jnp.dot(left_rows, right_rows, preferred_element_type=jnp.float32)


def split_three(value):
    high = value.astype(jnp.bfloat16)
    rest = value - high.astype(jnp.float32)
    middle = rest.astype(jnp.bfloat16)
    lowest = (rest - middle.astype(jnp.float32)).astype(jnp.bfloat16)
    return high, middle, lowest


def forward_kernel(q_ref, k_ref, v_ref, gain_ref, qm_ref, km_ref, o_ref, lse_ref):
    lane = lax.broadcasted_iota(jnp.int32, q_ref.shape[-2:], 1)
    left = lane < HEAD_DIM
    q_unit, _ = unit_of(q_ref[0, 0], left)
    k_unit, _ = unit_of(k_ref[0, 0], left)
    q_low = (q_unit * gain_ref[...]).astype(jnp.bfloat16)
    k_low = k_unit.astype(jnp.bfloat16)
    v_low = v_ref[0, 0].astype(jnp.bfloat16)
    qm = qm_ref[0]
    km = km_ref[0]
    one = jnp.ones_like(v_low)
    results = []
    for head in range(2):
        mine = left if head == 0 else ~left
        scores = nt(jnp.where(mine, q_low, qm), jnp.where(mine, k_low, km))
        weights = jnp.exp(scores).astype(jnp.bfloat16)
        results.append(nn(weights, jnp.where(mine, v_low, one)))
    totals = jnp.where(left, results[1], results[0])
    lse_ref[0] = jnp.log(totals)
    swapped = pltpu.roll(totals, HEAD_DIM, 1)
    o_ref[0] = (jnp.where(left, results[0], results[1]) / swapped).astype(jnp.bfloat16)


def backward_kernel(
    q_ref, k_ref, v_ref, gain_ref, qm_ref, km_ref, o_ref, lse_ref, do_ref, d_ref, sums_ref
):
    shape = q_ref.shape[-2:]
    lane = lax.broadcasted_iota(jnp.int32, shape, 1)
    left = lane < HEAD_DIM
    spot = lane % HEAD_DIM
    gain = gain_ref[...]
    q_unit, q_inv = unit_of(q_ref[0, 0], left)
    k_unit, k_inv = unit_of(k_ref[0, 0], left)
    q_low = (q_unit * gain).astype(jnp.bfloat16)
    k_low = k_unit.astype(jnp.bfloat16)
    v_low = v_ref[0, 0].astype(jnp.bfloat16)
    d_out = do_ref[0]
    km = km_ref[0]

    def place(base, value):
        high, middle, lowest = split_three(value)
        base = jnp.where(spot == FIRST_EXTRA, high, base)
        base = jnp.where(spot == FIRST_EXTRA + 1, middle, base)
        return jnp.where(spot == FIRST_EXTRA + 2, lowest, base)

    qm = place(qm_ref[0], -lse_ref[0])
    product = d_out.astype(jnp.float32) * o_ref[0].astype(jnp.float32)
    first, second = head_sums(product, left)
    dm = place(jnp.zeros_like(d_out), -jnp.where(left, second, first))
    k_turned = k_low.astype(jnp.float32).T.astype(jnp.bfloat16)
    d_v, d_k, d_q = [], [], []
    for head in range(2):
        mine = left if head == 0 else ~left
        probs = jnp.exp(nt(jnp.where(mine, k_low, km), jnp.where(mine, q_low, qm)))
        d_v.append(nn(probs.astype(jnp.bfloat16), d_out))
        shifted = nt(jnp.where(mine, v_low, km), jnp.where(mine, d_out, dm))
        d_scores = (probs * shifted).astype(jnp.bfloat16)
        d_k.append(nn(d_scores, q_low))
        d_q.append(nn(k_turned[head * HEAD_DIM : (head + 1) * HEAD_DIM], d_scores))
    d_q_low = jnp.concatenate(d_q, axis=0).T
    d_k_low = jnp.where(left, d_k[0], d_k[1])
    d_values = jnp.where(left, d_v[0], d_v[1])
    turned = d_q_low * gain
    first, second = head_sums(turned * q_unit, left)
    d_queries = q_inv * (turned - q_unit * jnp.where(left, first, second))
    first, second = head_sums(d_k_low * k_unit, left)
    d_keys = k_inv * (d_k_low - k_unit * jnp.where(left, first, second))
    parts = []
    for index, value in enumerate((d_queries, d_keys, d_values)):
        rounded = value.astype(jnp.bfloat16)
        d_ref[index, 0] = rounded
        parts.append(jnp.sum(rounded.astype(jnp.float32), axis=0, keepdims=True))
    parts.append(jnp.sum(d_q_low * q_unit, axis=0, keepdims=True))
    parts.append(jnp.zeros((4, PAIR), jnp.float32))
    sums_ref[0] = jnp.concatenate(parts, axis=0)


def mask_lanes(ids):
    spot = jnp.arange(PAIR, dtype=jnp.int32) % HEAD_DIM
    rows = ids[:, :, None]
    queries = (rows == spot).astype(jnp.bfloat16)
    keys = jnp.where((rows > spot) & (spot < FIRST_EXTRA), NEG, 0.0)
    extra = (spot >= FIRST_EXTRA) & (spot < FIRST_EXTRA + 3)
    return queries, jnp.where(extra, 1.0, keys).astype(jnp.bfloat16)


def specs(length):
    def raw(which):
        return pl.BlockSpec((1, 1, length, PAIR), lambda b, h: (which, b, 0, h))

    gain = pl.BlockSpec((1, PAIR), lambda b, h: (0, h))
    lanes = pl.BlockSpec((1, length, PAIR), lambda b, h: (b, 0, 0))
    tokens = pl.BlockSpec((1, length, PAIR), lambda b, h: (b, 0, h))
    return [raw(0), raw(1), raw(2), gain, lanes, lanes], tokens


def attention_forward(qkv, gain_row, qm, km):
    _, images, length, width = qkv.shape
    ins, tokens = specs(length)
    return pl.pallas_call(
        forward_kernel,
        grid=(images, width // PAIR),
        in_specs=ins,
        out_specs=[tokens, tokens],
        out_shape=[
            jax.ShapeDtypeStruct((images, length, width), jnp.bfloat16),
            jax.ShapeDtypeStruct((images, length, width), jnp.float32),
        ],
        compiler_params=pltpu.CompilerParams(vmem_limit_bytes=48 << 20),
        cost_estimate=pl.CostEstimate(
            flops=4 * images * length * length * width * 2, bytes_accessed=images * length * width * 18, transcendentals=images * length * length * 16
        ),
        name="attention_forward",
    )(qkv, qkv, qkv, gain_row, qm, km)


def attention_backward(qkv, gain_row, qm, km, out, lse, d_out):
    _, images, length, width = qkv.shape
    ins, tokens = specs(length)
    return pl.pallas_call(
        backward_kernel,
        grid=(images, width // PAIR),
        in_specs=ins + [tokens, tokens, tokens],
        out_specs=[
            pl.BlockSpec((3, 1, length, PAIR), lambda b, h: (0, b, 0, h)),
            pl.BlockSpec((1, 8, PAIR), lambda b, h: (b, 0, h)),
        ],
        out_shape=[
            jax.ShapeDtypeStruct((3, images, length, width), jnp.bfloat16),
            jax.ShapeDtypeStruct((images, 8, width), jnp.float32),
        ],
        compiler_params=pltpu.CompilerParams(vmem_limit_bytes=56 << 20),
        cost_estimate=pl.CostEstimate(
            flops=10 * images * length * length * width * 2, bytes_accessed=images * length * width * 30, transcendentals=images * length * length * 16
        ),
        name="attention_backward",
    )(qkv, qkv, qkv, gain_row, qm, km, out, lse, d_out)


GELU_RATE = 0.7978845608
GELU_CUBE = 0.7978845608 * 0.044715
FFN_CHUNK = 512


def tile_of(count, want):
    best = 8
    for size in range(8, want + 1, 8):
        if count % size == 0:
            best = size
    return best


def side_by_side(ref):
    return jnp.concatenate([ref[index] for index in range(ref.shape[0])], axis=1)


class Images:
    def __init__(self, rows, length, images):
        start = pl.program_id(0) * rows
        self.first = start // length
        self.second = jnp.minimum((start + rows - 1) // length, images - 1)
        index = lax.broadcasted_iota(jnp.int32, (rows, 1), 0) + start
        self.early = index < (self.first + 1) * length

    def pick(self, table, which):
        return jnp.where(
            self.early,
            table[self.first, which : which + 1],
            table[self.second, which : which + 1],
        )

    def add(self, sums, which, value):
        early = jnp.sum(jnp.where(self.early, value, 0.0), axis=0, keepdims=True)
        late = jnp.sum(jnp.where(self.early, 0.0, value), axis=0, keepdims=True)
        sums[self.first, which : which + 1] += early
        sums[self.second, which : which + 1] += late


def standard_rows(value):
    centered = value - jnp.mean(value, axis=-1, keepdims=True)
    inv_std = lax.rsqrt(jnp.mean(centered * centered, axis=-1, keepdims=True) + 1e-06)
    return centered * inv_std, inv_std


def norm_back(incoming, normed, inv_std):
    average = jnp.mean(incoming, axis=-1, keepdims=True)
    cross = jnp.mean(incoming * normed, axis=-1, keepdims=True)
    return inv_std * (incoming - average - normed * cross)


def block_copies(parts, start, target, sem, row_blocks, col_blocks):
    height = target.shape[0] // row_blocks
    span = target.shape[1] // col_blocks
    for r in range(row_blocks):
        for c in range(col_blocks):
            pltpu.make_async_copy(
                parts.at[r * col_blocks + c, :, pl.ds(start, span)],
                target.at[pl.ds(r * height, height), pl.ds(c * span, span)],
                sem,
            ).start()


def wait_all(target, sem):
    pltpu.make_async_copy(target, target, sem).wait()


def ffn_kernel(
    blocks, length, images,
    x_ref, att_ref, g_ref, mod_ref, bias_proj_ref, bias_one_ref, bias_two_ref, parts_ref,
    out_ref, ln_ref, hidden_ref, d_two_ref, d_pre_ref, d_one_ref, d_res_ref, d_att_ref,
    sums_ref, sum_proj_ref, sum_one_ref, sum_two_ref,
    w_proj, w_one, w_two, slope, sems,
):
    rows = att_ref.shape[0]
    ff = w_one.shape[1]
    first_step = pl.program_id(0) == 0

    @pl.when(first_step)
    def _():
        part = w_proj.shape[1] // blocks[1]
        ff_part = ff // blocks[1]
        block_copies(parts_ref, 0, w_proj, sems.at[0], *blocks)
        block_copies(parts_ref, part, w_one, sems.at[1], *blocks)
        block_copies(parts_ref, part + ff_part, w_two, sems.at[2], *blocks)
        sums_ref[...] = jnp.zeros_like(sums_ref)
        sum_proj_ref[...] = jnp.zeros_like(sum_proj_ref)
        sum_one_ref[...] = jnp.zeros_like(sum_one_ref)
        sum_two_ref[...] = jnp.zeros_like(sum_two_ref)
        wait_all(w_proj, sems.at[0])
        wait_all(w_one, sems.at[1])
        wait_all(w_two, sems.at[2])

    here = Images(rows, length, images)
    gate_attn = here.pick(mod_ref, 2)
    branch_one = nn(att_ref[...], w_proj[...]) + bias_proj_ref[...]
    residual = side_by_side(x_ref).astype(jnp.float32) + gate_attn * branch_one
    normed, inv_std = standard_rows(residual)
    scale = 1.0 + here.pick(mod_ref, 4)
    ln_two = (normed * scale + here.pick(mod_ref, 3)).astype(jnp.bfloat16)
    ln_ref[...] = ln_two
    branch_two = jnp.broadcast_to(bias_two_ref[...], residual.shape)
    for start in range(0, ff, FFN_CHUNK):
        span = slice(start, start + FFN_CHUNK)
        pre = nn(ln_two, w_one[:, span]) + bias_one_ref[:, span]
        square = pre * pre
        turn = jnp.tanh(pre * (GELU_RATE + GELU_CUBE * square))
        half = 0.5 + 0.5 * turn
        value = pre * half
        slope[:, span] = half + value * (1.0 - turn) * (GELU_RATE + 3.0 * GELU_CUBE * square)
        low = value.astype(jnp.bfloat16)
        hidden_ref[:, span] = low
        branch_two += nt(low, w_two[:, span])
    gate_ffn = here.pick(mod_ref, 5)
    result = (residual + gate_ffn * branch_two).astype(jnp.bfloat16)
    part = out_ref.shape[2]
    for index in range(out_ref.shape[0]):
        out_ref[index] = result[:, index * part : (index + 1) * part]
    incoming = side_by_side(g_ref).astype(jnp.float32)
    here.add(sums_ref, 3, incoming * branch_two)
    d_two = (gate_ffn * incoming).astype(jnp.bfloat16)
    d_two_ref[...] = d_two
    sum_two_ref[...] += jnp.sum(d_two.astype(jnp.float32), axis=0, keepdims=True)
    d_back = jnp.zeros_like(residual)
    for start in range(0, ff, FFN_CHUNK):
        span = slice(start, start + FFN_CHUNK)
        d_pre = (nn(d_two, w_two[:, span]) * slope[:, span]).astype(jnp.bfloat16)
        d_pre_ref[:, span] = d_pre
        sum_one_ref[:, span] += jnp.sum(d_pre.astype(jnp.float32), axis=0, keepdims=True)
        d_back += nt(d_pre, w_one[:, span])
    here.add(sums_ref, 1, d_back)
    here.add(sums_ref, 2, d_back * normed)
    d_res = incoming + norm_back(d_back * scale, normed, inv_std)
    d_res_ref[...] = d_res
    here.add(sums_ref, 0, d_res * branch_one)
    d_one = (gate_attn * d_res).astype(jnp.bfloat16)
    d_one_ref[...] = d_one
    sum_proj_ref[...] += jnp.sum(d_one.astype(jnp.float32), axis=0, keepdims=True)
    d_att_ref[...] = nt(d_one, w_proj[...]).astype(jnp.bfloat16)


def ffn(x, attended, g, modulation, bias_proj, bias_one, bias_two, parts, blocks, length):
    groups, count, part = x.shape
    width = groups * part
    ff = bias_one.shape[1]
    images = modulation.shape[0]
    rows = tile_of(count, 272)
    f32, bf16 = jnp.float32, jnp.bfloat16
    pieces = pl.BlockSpec((groups, rows, part), lambda i: (0, i, 0))
    wide = pl.BlockSpec((rows, width), lambda i: (i, 0))
    tall = pl.BlockSpec((rows, ff), lambda i: (i, 0))

    def fixed(*shape):
        return pl.BlockSpec(shape, lambda i: (0,) * len(shape))

    def made(shape, dtype):
        return jax.ShapeDtypeStruct(shape, dtype)

    return pl.pallas_call(
        functools.partial(ffn_kernel, blocks, length, images),
        grid=(count // rows,),
        in_specs=[
            pieces, wide, pieces, fixed(images, 6, width), fixed(1, width), fixed(1, ff),
            fixed(1, width), pl.BlockSpec(memory_space=pl.ANY),
        ],
        out_specs=[
            pieces, wide, tall, wide, tall, wide, wide, wide,
            fixed(images, 4, width), fixed(1, width), fixed(1, ff), fixed(1, width),
        ],
        out_shape=[
            made((groups, count, part), bf16), made((count, width), bf16),
            made((count, ff), bf16), made((count, width), bf16), made((count, ff), bf16),
            made((count, width), bf16), made((count, width), f32), made((count, width), bf16),
            made((images, 4, width), f32), made((1, width), f32), made((1, ff), f32),
            made((1, width), f32),
        ],
        scratch_shapes=[
            pltpu.VMEM((width, width), bf16), pltpu.VMEM((width, ff), bf16),
            pltpu.VMEM((width, ff), bf16), pltpu.VMEM((rows, ff), f32),
            pltpu.SemaphoreType.DMA((3,)),
        ],
        compiler_params=pltpu.CompilerParams(vmem_limit_bytes=62 << 20),
        cost_estimate=pl.CostEstimate(
            flops=4 * count * width * (2 * ff + width),
            bytes_accessed=count * width * 20 + count * ff * 4 + width * (2 * ff + width) * 2,
            transcendentals=count * ff,
        ),
        name="ffn_both",
    )(x, attended, g, modulation, bias_proj, bias_one, bias_two, parts)


def cube_copies(parts, target, sem, row_blocks, col_blocks):
    height = target.shape[1] // row_blocks
    span = target.shape[2] // col_blocks
    for r in range(row_blocks):
        for c in range(col_blocks):
            pltpu.make_async_copy(
                parts.at[r * col_blocks + c],
                target.at[:, pl.ds(r * height, height), pl.ds(c * span, span)],
                sem,
            ).start()


def qkv_kernel(blocks, length, images, x_ref, mod_ref, bias_ref, parts_ref, ln_ref, qkv_ref, weights, sem):
    @pl.when(pl.program_id(0) == 0)
    def _():
        cube_copies(parts_ref, weights, sem.at[0], *blocks)
        wait_all(weights, sem.at[0])

    here = Images(ln_ref.shape[0], length, images)
    normed, _ = standard_rows(side_by_side(x_ref).astype(jnp.float32))
    ln_one = (normed * (1.0 + here.pick(mod_ref, 1)) + here.pick(mod_ref, 0)).astype(jnp.bfloat16)
    ln_ref[...] = ln_one
    for index in range(3):
        qkv_ref[index] = nn(ln_one, weights[index]) + bias_ref[index]


def qkv_forward(x, modulation, bias, parts, blocks, length):
    groups, count, part = x.shape
    width = groups * part
    images = modulation.shape[0]
    rows = tile_of(count, 544)
    return pl.pallas_call(
        functools.partial(qkv_kernel, blocks, length, images),
        grid=(count // rows,),
        in_specs=[
            pl.BlockSpec((groups, rows, part), lambda i: (0, i, 0)),
            pl.BlockSpec((images, 6, width), lambda i: (0, 0, 0)),
            pl.BlockSpec((3, 1, width), lambda i: (0, 0, 0)),
            pl.BlockSpec(memory_space=pl.ANY),
        ],
        out_specs=[
            pl.BlockSpec((rows, width), lambda i: (i, 0)),
            pl.BlockSpec((3, rows, width), lambda i: (0, i, 0)),
        ],
        out_shape=[
            jax.ShapeDtypeStruct((count, width), jnp.bfloat16),
            jax.ShapeDtypeStruct((3, count, width), jnp.float32),
        ],
        scratch_shapes=[
            pltpu.VMEM((3, width, width), jnp.bfloat16),
            pltpu.SemaphoreType.DMA((1,)),
        ],
        compiler_params=pltpu.CompilerParams(vmem_limit_bytes=48 << 20),
        cost_estimate=pl.CostEstimate(
            flops=6 * count * width * width,
            bytes_accessed=count * width * 16 + 6 * width * width,
            transcendentals=count,
        ),
        name="qkv_forward",
    )(x, modulation, bias, parts)


def input_kernel(
    blocks, length, images, d_ref, x_ref, res_ref, mod_ref, parts_ref, out_ref, sums_ref, weights, sem
):
    @pl.when(pl.program_id(0) == 0)
    def _():
        cube_copies(parts_ref, weights, sem.at[0], *blocks)
        sums_ref[...] = jnp.zeros_like(sums_ref)
        wait_all(weights, sem.at[0])

    here = Images(res_ref.shape[0], length, images)
    normed, inv_std = standard_rows(side_by_side(x_ref).astype(jnp.float32))
    d_ln = nt(d_ref[0], weights[0]) + nt(d_ref[1], weights[1]) + nt(d_ref[2], weights[2])
    here.add(sums_ref, 0, d_ln)
    here.add(sums_ref, 1, d_ln * normed)
    scale = 1.0 + here.pick(mod_ref, 1)
    result = (res_ref[...] + norm_back(d_ln * scale, normed, inv_std)).astype(jnp.bfloat16)
    part = out_ref.shape[2]
    for index in range(out_ref.shape[0]):
        out_ref[index] = result[:, index * part : (index + 1) * part]


def input_backward(d_qkv, x, d_res, modulation, parts, blocks, length):
    groups, count, part = x.shape
    width = groups * part
    images = modulation.shape[0]
    rows = tile_of(count, 544)
    pieces = pl.BlockSpec((groups, rows, part), lambda i: (0, i, 0))
    return pl.pallas_call(
        functools.partial(input_kernel, blocks, length, images),
        grid=(count // rows,),
        in_specs=[
            pl.BlockSpec((3, rows, width), lambda i: (0, i, 0)),
            pieces,
            pl.BlockSpec((rows, width), lambda i: (i, 0)),
            pl.BlockSpec((images, 6, width), lambda i: (0, 0, 0)),
            pl.BlockSpec(memory_space=pl.ANY),
        ],
        out_specs=[pieces, pl.BlockSpec((images, 2, width), lambda i: (0, 0, 0))],
        out_shape=[
            jax.ShapeDtypeStruct((groups, count, part), jnp.bfloat16),
            jax.ShapeDtypeStruct((images, 2, width), jnp.float32),
        ],
        scratch_shapes=[
            pltpu.VMEM((3, width, width), jnp.bfloat16),
            pltpu.SemaphoreType.DMA((1,)),
        ],
        compiler_params=pltpu.CompilerParams(vmem_limit_bytes=48 << 20),
        cost_estimate=pl.CostEstimate(
            flops=6 * count * width * width,
            bytes_accessed=count * width * 14 + 6 * width * width,
            transcendentals=count,
        ),
        name="input_backward",
    )(d_qkv, x, d_res, modulation, parts)


def turn_rows(source, target):
    total = source.shape[0]
    step = 640
    for start in range(0, total, step):
        size = min(step, total - start)
        target[:, start : start + size] = source[start : start + size, :].T


def ffn_grad_kernel(left_a, left_b, right_a, right_b, out_ref, turned):
    pair, tile = pl.program_id(0), pl.program_id(1)

    def write(value):
        value = value.astype(jnp.bfloat16)
        out_ref[...] = value.reshape(out_ref.shape)

    @pl.when((pair == 0) & (tile == 0))
    def _():
        turn_rows(left_a, turned)

    @pl.when((pair == 1) & (tile == 0))
    def _():
        turn_rows(left_b, turned)

    @pl.when(pair == 0)
    def _():
        write(nn(turned[...], right_a[...]))

    @pl.when(pair == 1)
    def _():
        write(nn(turned[...], right_b[...]))


def ffn_grads(left_a, right_a, left_b, right_b, blocks):
    row_blocks, col_blocks = blocks
    count, width = left_a.shape
    ff = right_a.shape[1]
    ff_part = ff // col_blocks
    span = min(512, ff_part)
    inner = ff_part // span
    tiles = ff // span
    height = width // row_blocks
    left = pl.BlockSpec((count, width), lambda p, j: (0, 0))
    return pl.pallas_call(
        ffn_grad_kernel,
        grid=(2, tiles),
        in_specs=[
            left,
            left,
            pl.BlockSpec((count, span), lambda p, j: (0, j * (1 - p) + (tiles - 1) * p)),
            pl.BlockSpec((count, span), lambda p, j: (0, j * p)),
        ],
        out_specs=pl.BlockSpec(
            (row_blocks, 1, height, span), lambda p, j: (0, j // inner, 0, p * inner + j % inner)
        ),
        out_shape=jax.ShapeDtypeStruct((row_blocks, col_blocks, height, 2 * ff_part), jnp.bfloat16),
        scratch_shapes=[pltpu.VMEM((width, count), jnp.bfloat16)],
        compiler_params=pltpu.CompilerParams(vmem_limit_bytes=56 << 20),
        cost_estimate=pl.CostEstimate(
            flops=4 * count * width * ff,
            bytes_accessed=count * width * 4 + count * ff * 4 + width * ff * 4,
            transcendentals=0,
        ),
        name="ffn_grads",
    )(left_a, left_b, right_a, right_b)


def attn_grad_kernel(left_a, left_b, right_a, right_b, out_ref, turned):
    which = pl.program_id(0)

    def write(value):
        height, part = out_ref.shape[2:]
        value = value.astype(jnp.bfloat16)
        for c in range(out_ref.shape[1]):
            piece = value[:, c * part : (c + 1) * part]
            out_ref[:, c] = piece.reshape(out_ref.shape[0], height, part)

    @pl.when(which == 0)
    def _():
        turn_rows(left_a, turned)
        write(nn(turned[...], right_a[...]))

    @pl.when(which == 1)
    def _():
        turn_rows(left_b, turned)

    @pl.when(which > 0)
    def _():
        write(nn(turned[...], right_b[0]))


def attn_grads(attended, d_one, ln_one, d_qkv, blocks):
    row_blocks, col_blocks = blocks
    count, width = attended.shape
    part = width // col_blocks
    height = width // row_blocks
    fixed = pl.BlockSpec((count, width), lambda p: (0, 0), pipeline_mode=pl.Buffered(1))
    return pl.pallas_call(
        attn_grad_kernel,
        grid=(4,),
        in_specs=[
            fixed,
            fixed,
            fixed,
            pl.BlockSpec((1, count, width), lambda p: (jnp.maximum(p - 1, 0), 0, 0)),
        ],
        out_specs=pl.BlockSpec((row_blocks, col_blocks, height, part), lambda p: (0, 0, 0, p)),
        out_shape=jax.ShapeDtypeStruct((row_blocks, col_blocks, height, 4 * part), jnp.bfloat16),
        scratch_shapes=[pltpu.VMEM((width, count), jnp.bfloat16)],
        compiler_params=pltpu.CompilerParams(vmem_limit_bytes=60 << 20),
        cost_estimate=pl.CostEstimate(
            flops=8 * count * width * width,
            bytes_accessed=count * width * 12 + width * width * 8,
            transcendentals=0,
        ),
        name="attn_grads",
    )(attended, ln_one, d_one, d_qkv)


def swap(pieces, axes):
    return lax.all_to_all(pieces, axes, split_axis=0, concat_axis=0, tiled=False)


def share(value, axes, count):
    return swap(jnp.broadcast_to(value[None], (count,) + value.shape), axes)


BOTH = ("row", "col")


def shards(
    tokens,
    condition,
    scale_ids,
    attention_triple_matrix,
    attention_triple_offset,
    qk_gain,
    w_proj,
    b_proj,
    w_fc1,
    b_fc1,
    w_fc2,
    b_fc2,
    w_ada,
    b_ada,
    out_grad,
):
    rows = lax.axis_size("row")
    groups = lax.axis_size("col")
    row = lax.axis_index("row")
    place = lax.axis_index("col")
    everyone = rows * groups
    part = tokens.shape[0]
    width = part * groups
    images_row, length = scale_ids.shape
    images = images_row // groups
    count = images * length
    block = w_proj.shape[0]
    ff_part = b_fc1.shape[0]
    hidden_width = ff_part * groups
    aligned = part % 128 == 0
    blocks = (rows, groups) if aligned else (1, 1)
    f32, bf16 = jnp.float32, jnp.bfloat16

    qkv_parts = lax.all_gather(attention_triple_matrix.transpose(1, 0, 2), BOTH)
    rest_parts = lax.all_gather(jnp.concatenate([w_proj, w_fc1, w_fc2.T], axis=1), BOTH)

    def whole(parts):
        parts = parts.reshape((rows, groups) + parts.shape[1:])
        return parts.transpose(0, 2, 1, 3).reshape(width, groups * parts.shape[-1])

    def spread(wide):
        cols = wide.shape[1] // groups
        pieces = wide.reshape(rows, block, groups, cols).transpose(0, 2, 1, 3)
        return pieces.reshape(everyone, block, cols)

    if not aligned:
        qkv_parts = jnp.stack([whole(qkv_parts[:, index]) for index in range(3)])[None]
        cut = part + ff_part
        rest_parts = jnp.concatenate(
            [
                whole(rest_parts[:, :, :part]),
                whole(rest_parts[:, :, part:cut]),
                whole(rest_parts[:, :, cut:]),
            ],
            axis=1,
        )[None]

    offsets = attention_triple_offset.astype(f32).reshape(-1)
    small = share(
        jnp.concatenate(
            [offsets, b_proj.astype(f32), b_fc1.astype(f32), b_fc2.astype(f32), qk_gain]
        ),
        "col",
        groups,
    )
    cuts = [3 * part, 4 * part, 4 * part + ff_part, 5 * part + ff_part]
    bias_qkv = small[:, : cuts[0]].reshape(groups, 3, part).transpose(1, 0, 2).reshape(3, 1, width)
    bias_proj = small[:, cuts[0] : cuts[1]].reshape(1, width)
    bias_one = small[:, cuts[1] : cuts[2]].reshape(1, hidden_width)
    bias_two = small[:, cuts[2] : cuts[3]].reshape(1, width)
    gain_row = jnp.repeat(small[:, cuts[3] :].reshape(-1), HEAD_DIM)[None]

    cond_float = condition.astype(f32)
    soft = jax.nn.silu(cond_float).astype(bf16)
    soft_all = (
        share(soft, BOTH, everyone)
        .reshape(rows, groups, images_row, part)
        .transpose(0, 2, 1, 3)
        .reshape(rows * images_row, width)
    )
    ada_block = w_ada.shape[1]
    soft_mine = lax.dynamic_slice(
        soft_all, (0, row * ada_block), (rows * images_row, ada_block)
    )
    mod_part = jnp.einsum("ic,scd->isd", soft_mine, w_ada, preferred_element_type=f32)
    mod_part = mod_part + jnp.where(row == 0, b_ada.astype(f32), 0.0)[None]
    modulation = swap(mod_part.reshape(everyone, images, 6, part), BOTH)
    modulation = (
        modulation.reshape(rows, groups, images, 6, part)
        .sum(axis=0)
        .transpose(1, 2, 0, 3)
        .reshape(images, 6, width)
    )

    def to_tokens(features):
        pieces = swap(features.T.reshape(groups, count, part), "col")
        return pieces if aligned else pieces.transpose(1, 0, 2).reshape(1, count, width)

    def to_features(pieces):
        if not aligned:
            pieces = pieces[0].reshape(count, groups, part).transpose(1, 0, 2)
        return swap(pieces, "col").reshape(groups * count, part).T

    tok_in = to_tokens(tokens)
    grad_in = to_tokens(out_grad)
    scale_rows = lax.dynamic_slice(scale_ids, (place * images, 0), (images, length))
    query_lanes, key_lanes = mask_lanes(scale_rows)

    ln_one, qkv = qkv_forward(tok_in, modulation, bias_qkv, qkv_parts, blocks, length)
    qkv = qkv.reshape(3, images, length, width)
    attended, log_sums = attention_forward(qkv, gain_row, query_lanes, key_lanes)
    attn_rows = attended.reshape(count, width)
    (
        layer_pieces,
        ln_two,
        hidden,
        d_two,
        d_pre,
        d_one,
        d_res,
        d_attended,
        mod_sums,
        sum_bproj,
        sum_b1,
        sum_b2,
    ) = ffn(
        tok_in,
        attn_rows,
        grad_in,
        modulation,
        bias_proj,
        bias_one,
        bias_two,
        rest_parts,
        blocks,
        length,
    )
    layer_out = to_features(layer_pieces)
    wide_ffn = ffn_grads(ln_two, d_pre, d_two, hidden, blocks)
    if aligned:
        wide_ffn = wide_ffn.reshape(everyone, block, 2 * ff_part)
    else:
        wide_ffn = wide_ffn[0, 0]
        wide_ffn = jnp.concatenate(
            [spread(wide_ffn[:, :hidden_width]), spread(wide_ffn[:, hidden_width:])], axis=2
        )
    wide_ffn = lax.psum_scatter(wide_ffn, BOTH, scatter_dimension=0, tiled=False).astype(f32)
    grad_fc1 = wide_ffn[:, :ff_part]
    grad_fc2 = wide_ffn[:, ff_part:].T

    d_qkv, head_totals = attention_backward(
        qkv,
        gain_row,
        query_lanes,
        key_lanes,
        attended,
        log_sums,
        d_attended.reshape(images, length, width),
    )
    d_qkv = d_qkv.reshape(3, count, width)
    wide_attn = attn_grads(attn_rows, d_one, ln_one, d_qkv, blocks)
    if aligned:
        wide_attn = wide_attn.reshape(everyone, block, 4 * part)
    else:
        wide_attn = wide_attn[0, 0]
        wide_attn = jnp.concatenate(
            [spread(wide_attn[:, index * width : (index + 1) * width]) for index in range(4)],
            axis=2,
        )
    wide_attn = lax.psum_scatter(wide_attn, BOTH, scatter_dimension=0, tiled=False).astype(f32)
    grad_proj = wide_attn[:, :part]
    grad_qkv = wide_attn[:, part:].reshape(block, 3, part)
    token_pieces, first_sums = input_backward(
        d_qkv, tok_in, d_res, modulation, qkv_parts, blocks, length
    )
    grad_tokens = to_features(token_pieces)

    head_totals = head_totals.sum(axis=0)
    totals = jnp.concatenate(
        [
            head_totals[:3].reshape(3, groups, part).transpose(1, 0, 2).reshape(groups, 3 * part),
            sum_bproj.reshape(groups, part),
            sum_b1.reshape(groups, ff_part),
            sum_b2.reshape(groups, part),
            head_totals[3].reshape(-1, HEAD_DIM).sum(axis=1).reshape(groups, -1),
        ],
        axis=1,
    )
    totals = jnp.broadcast_to(totals[None], (rows,) + totals.shape)
    totals = swap(totals.reshape(everyone, -1), BOTH).sum(axis=0)
    d_mod = jnp.concatenate([first_sums, mod_sums], axis=1).astype(bf16)
    d_mod = d_mod.reshape(images, 6, groups, part).transpose(2, 0, 1, 3)
    d_mod = jnp.broadcast_to(d_mod[None], (rows,) + d_mod.shape)
    d_mod = swap(d_mod.reshape((everyone,) + d_mod.shape[2:]), BOTH)
    d_mod = d_mod.reshape(everyone * images, 6, part)
    grad_ada = jnp.einsum("ic,isd->scd", soft_mine, d_mod, preferred_element_type=f32)
    grad_bada = jnp.sum(d_mod.astype(f32), axis=0)
    d_soft = jnp.einsum("isd,scd->ic", d_mod, w_ada, preferred_element_type=f32)
    d_soft = d_soft.reshape(rows, 1, images_row, ada_block)
    d_soft = jnp.broadcast_to(d_soft, (rows, groups, images_row, ada_block))
    d_soft = swap(d_soft.reshape(everyone, images_row, ada_block), BOTH)
    d_soft = d_soft.reshape(rows, groups, images_row, ada_block).sum(axis=1)
    d_soft = d_soft.transpose(1, 0, 2).reshape(images_row, width)
    d_soft = lax.dynamic_slice(d_soft, (0, place * part), (images_row, part))
    _, silu_pull = jax.vjp(jax.nn.silu, cond_float)
    grad_condition = silu_pull(d_soft)[0].astype(bf16)
    return (
        layer_out,
        grad_tokens,
        grad_condition,
        grad_qkv,
        totals[: cuts[0]].reshape(3, part),
        totals[cuts[3] :],
        grad_proj,
        totals[cuts[0] : cuts[1]],
        grad_fc1,
        totals[cuts[1] : cuts[2]],
        grad_fc2,
        totals[cuts[2] : cuts[3]],
        grad_ada,
        grad_bada,
    )


def solution(mesh):
    placed = (
        P("col", "row"),
        P("row", "col"),
        P("row", None),
        P("row", None, "col"),
        P(None, "col"),
        P("col"),
        P("row", "col"),
        P("col"),
        P("row", "col"),
        P("col"),
        P("col", "row"),
        P("col"),
        P(None, "row", "col"),
        P(None, "col"),
        P("col", "row"),
    )
    return jax.shard_map(
        shards,
        mesh=mesh,
        in_specs=placed,
        out_specs=(
            P("col", "row"),
            P("col", "row"),
            P("row", "col"),
            P("row", None, "col"),
            P(None, "col"),
            P("col"),
            P("row", "col"),
            P("col"),
            P("row", "col"),
            P("col"),
            P("col", "row"),
            P("col"),
            P(None, "row", "col"),
            P(None, "col"),
        ),
        check_vma=False,
    )
```

time: 3480 us -> 1110 us (0.32)
  matrix products: 1010 us -> 1.56 us
  local copies, waits for them, and re-layouts: 789 us -> 116 us
  other arithmetic: 513 us -> 12.4 us
  Pallas kernels: 0 us -> 484 us
  waiting for transfers between devices: 611 us -> 282 us
  blocking collectives: 395 us -> 145 us
  starting transfers between devices: 121 us -> 43.1 us
    dot_general x123 -> x3, matrix products: 1010 us -> 1.56 us  [the longest x1 1.04 us: shards(): jnp.einsum('ic,isd->scd', soft_mine, d_mod, preferred_element_type=f32)]
    pallas_call x0 -> x7, Pallas kernels: none -> 484 us  [the longest x1 155 us: ffn(): pl.pallas_call(functools.partial(ffn_kernel, blocks, length, images), gri...]
    all_to_all x25 -> x8, waiting for transfers between devices: 525 us -> 217 us  [swap(): lax.all_to_all(pieces, axes, split_axis=0, concat_axis=0, tiled=False)]
    all_gather x6 -> x0, blocking collectives: 220 us -> none  [the longest x1 139 us: shards(): lax.all_gather(b_fc2, 'col', axis=0, tiled=True)]
    unnamed x710 -> x49, local copies, waits for them, and re-layouts: 209 us -> 14.3 us
    convert_element_type x25 -> x6, other arithmetic: 185 us -> 4.51 us  [the longest x1 1.11 us: shards(): lax.psum_scatter(wide_ffn, BOTH, scatter_dimension=0, tiled=False)]
    another operation x37 -> x2, local copies, waits for them, and re-layouts: 168 us -> 0.15 us  [the longest x1 0.08 us: shards(): gain_row = jnp.repeat(small[:, cuts[3]:].reshape(-1), HEAD_DIM)[None]]
    all_to_all x0 -> x2, blocking collectives: none -> 145 us  [swap(): lax.all_to_all(pieces, axes, split_axis=0, concat_axis=0, tiled=False)]
  transfers between devices with their start and end apart: 44 -> 12, of which waited for: 13 -> 9; matrix products, arithmetic and copies ran while one was open for 52% -> 10% of each run, Pallas kernels for 0% -> 16%
where the time goes in v1:
time: 1110 us; the launch traced here: 1100 us
  Pallas kernels  484 us (44%)
  waiting for transfers between devices  282 us (25%)
  blocking collectives  145 us (13%)
  local copies, waits for them, and re-layouts  116 us (10%)
  starting transfers between devices  43.1 us (4%)
  between operations  14.6 us (1%)
  other arithmetic  12.4 us (1%)
    all_to_all x8, waiting for transfers between devices, swap(): lax.all_to_all(pieces, axes, split_axis=0, concat_axis=0, tiled=False)  217 us
    pallas_call x1, Pallas kernels, ffn(): pl.pallas_call(functools.partial(ffn_kernel, blocks, length, images), gri...  155 us
    all_to_all x2, blocking collectives, swap(): lax.all_to_all(pieces, axes, split_axis=0, concat_axis=0, tiled=False)  145 us
    pallas_call x1, Pallas kernels, attention_backward(): pl.pallas_call(backward_kernel, grid=(images, width // PAIR), in_specs=in...  115 us
    pallas_call x1, Pallas kernels, ffn_grads(): pl.pallas_call(ffn_grad_kernel, grid=(2, tiles), in_specs=[left, left, pl...  61.8 us
    pallas_call x1, Pallas kernels, attention_forward(): pl.pallas_call(forward_kernel, grid=(images, width // PAIR), in_specs=ins...  55.5 us
    all_gather x1, waiting for transfers between devices, shards(): lax.all_gather(jnp.concatenate([w_proj, w_fc1, w_fc2.T], axis=1), BOTH)  52.1 us
    all_to_all x8, starting transfers between devices, swap(): lax.all_to_all(pieces, axes, split_axis=0, concat_axis=0, tiled=False)  42.9 us
  transfers between devices with their start and end apart: 12, of which 9 were waited for; matrix products, arithmetic and copies ran while one was open for 10% of the time, Pallas kernels for 16%

profile of v1, /device:TPU:0, one launch (start us, length us, event | category | flops | bytes accessed | tf_op | source)
XLA Modules:
  0.0 1099.6 jit_solution(8934850299061372963)
XLA Ops:
  8.0 1.1 copy.112
  9.1 1.0 copy.111
  10.1 1.8 pad_maximum_fusion
  13.4 7.3 all-to-all-start.1
  24.8 9.1 all-to-all-done.1
  34.5 3.3 all-to-all-start.3
  39.1 1.0 copy.107
  40.2 1.5 all-to-all-done.3
  41.7 2.6 all-to-all-start.2
  44.3 8.2 copy.105
  52.6 17.9 %all-to-all-done.2 = f32[32,4,6,256]{3,1,2,0:T(4,128)S(1)} async-done(((f32[32,4,6,256]{3,1,2,0:T(4,128)}), f32[32,4,6,256]{3,1,2,0:T(4,128)S(1)}, u32[]{:S(2)}, u32[]{:S(2)}) %all-to-all-start.2) | async-done | bytes 786464 | tf_op jit(solution)/shard_map/all_to_all | solution.py:612
  70.5 5.2 all-to-all-start
  75.6 8.2 copy.110
  83.9 56.8 %all-to-all-done.x_ref = bf16[4,2720,256]{2,1,0:T(8,128)(2,1)} async-done(((bf16[4,2720,256]{2,1,0:T(8,128)(2,1)}), bf16[4,2720,256]{2,1,0:T(8,128)(2,1)}, u32[]{:S(2)}, u32[]{:S(2)}) %all-to-all-start) | async-done | bytes 5570592 | tf_op jit(solution)/shard_map/all_to_all | solution.py:612
  140.7 5.2 all-to-all-start.4
  150.2 28.2 %qkv_forward.1 = (bf16[2720,1024]{1,0:T(8,128)(2,1)S(1)}, f32[3,2720,1024]{2,1,0:T(8,128)}) custom-call(bf16[4,2720,256]{2,1,0:T(8,128)(2,1)} %all-to-all-done.x_ref, f32[4,6,1024]{2,1,0:T(8,128)S(1)} %copy.109.mod_ref, f32[3,1,1024]{2,1,0:T(1,128)S(1)} %reshape.189.bias_ref, bf16[32,3,128,256]{3,2,1,0:T(8,128)(2,1)} %bitcast.130), custom_call_target="tpu_custom_call" | custom-call | flops 17112760320 | bytes 50855936 | tf_op jit(solution)/shard_map/qkv_forward/pallas_call | solution.py:406
  178.4 2.4 copy-done.7
  180.8 55.5 %attention_forward.1 = (bf16[4,680,1024]{2,1,0:T(8,128)(2,1)}, f32[4,680,1024]{2,1,0:T(8,128)}) custom-call(f32[3,4,680,1024]{3,2,1,0:T(8,128)} %bitcast.94, f32[3,4,680,1024]{3,2,1,0:T(8,128)} %bitcast.95, f32[3,4,680,1024]{3,2,1,0:T(8,128)} %bitcast.96, f32[1,1024]{1,0:T(1,128)S(1)} %broadcast_in_dim_reshape.3.gain_ref, ...), custom_call_target="tpu_custom_call" | custom-call | flops 15151923200 | bytes 50135040 | tf_op jit(solution)/shard_map/attention_forward/pallas_call | solution.py:144
  236.2 52.1 %all-gather.7.cloned.1.call-done = bf16[4096,2304]{0,1:T(8,128)(2,1)} async-done(((bf16[128,2304]{0,1:T(8,128)(2,1)}), bf16[4096,2304]{0,1:T(8,128)(2,1)}) %all-gather.7.cloned.1.call-update) | async-done | bytes 18874384 | tf_op jit(solution)/shard_map/all_gather | solution.py:657
  288.3 22.8 %copy.113 = bf16[4096,2304]{1,0:T(8,128)(2,1)} copy(bf16[4096,2304]{0,1:T(8,128)(2,1)} %all-gather.7.cloned.1.call-done) | data formatting | bytes 37748736 | tf_op jit(solution)/shard_map/all_gather | solution.py:657
  311.1 154.7 %ffn_both.1 = (bf16[4,2720,256]{2,1,0:T(8,128)(2,1)}, bf16[2720,1024]{1,0:T(8,128)(2,1)}, bf16[2720,4096]{1,0:T(8,128)(2,1)}, bf16[2720,1024]{1,0:T(8,128)(2,1)}...) custom-call(bf16[4,2720,256]{2,1,0:T(8,128)(2,1)} %all-to-all-done.x, ...), custom_call_target="tpu_custom_call" | custom-call | flops 102676561920 | bytes 119144448 | tf_op jit(solution)/shard_map/ffn_both/pallas_call | solution.py:342
  465.9 115.5 %attention_backward.1 = (bf16[3,4,680,1024]{3,2,1,0:T(8,128)(2,1)}, f32[4,8,1024]{2,1,0:T(8,128)}) custom-call(f32[3,4,680,1024]{3,2,1,0:T(8,128)} %bitcast.97, f32[3,4,680,1024]{3,2,1,0:T(8,128)} %bitcast.98, f32[3,4,680,1024]{3,2,1,0:T(8,128)} %bitcast.99, f32[1,1024]{1,0:T(1,128)} %copy-done.6, bf16[4,680,128]{2,1,0:T(8,128)(2,1)} %copy-done.2, ...), custom_call_target="tpu_custom_call" | custom-call | flops 37879808000 | bytes 83558400 | tf_op jit(solution)/shard_map/attention_backward/pallas_call | solution.py:164
  581.4 35.0 %attn_grads.1 = bf16[8,4,128,1024]{3,2,1,0:T(8,128)(2,1)} custom-call(bf16[2720,1024]{1,0:T(8,128)(2,1)} %bitcast.133, bf16[2720,1024]{1,0:T(8,128)(2,1)} %copy-done.7, bf16[2720,1024]{1,0:T(8,128)(2,1)} %get-tuple-element.45.right_a, bf16[3,2720,1024]{2,1,0:T(8,128)(2,1)} %bitcast.134), custom_call_target="tpu_custom_call" | custom-call | flops 22817013760 | bytes 41811968 | tf_op jit(solution)/shard_map/attn_grads/pallas_call | solution.py:589
  616.4 12.0 %copy.121 = bf16[32,128,1024]{1,2,0:T(8,128)(2,1)} copy(bf16[32,128,1024]{2,1,0:T(8,128)(2,1)} %bitcast.105) | data formatting | bytes 16777216 | tf_op jit(solution)/shard_map/reshape | solution.py:785
  628.4 61.8 %ffn_grads.1 = bf16[8,4,128,2048]{3,2,1,0:T(8,128)(2,1)} custom-call(bf16[2720,1024]{1,0:T(8,128)(2,1)} %get-tuple-element.50.left_a, bf16[2720,1024]{1,0:T(8,128)(2,1)} %get-tuple-element.51.left_b, bf16[2720,4096]{1,0:T(8,128)(2,1)} %get-tuple-element.52.right_a, bf16[2720,4096]{1,0:T(8,128)(2,1)} %get-tuple-element.53.right_b), custom_call_target="tpu_custom_call" | custom-call | flops 45634027520 | bytes 72482816 | tf_op jit(solution)/shard_map/ffn_grads/pallas_call | solution.py:535
  690.2 22.6 %copy.122 = bf16[32,128,2048]{1,2,0:T(8,128)(2,1)} copy(bf16[32,128,2048]{2,1,0:T(8,128)(2,1)} %bitcast.104) | data formatting | bytes 33554432 | tf_op jit(solution)/shard_map/reshape | solution.py:763
  712.8 0.9 copy-done.5
  713.7 33.7 %input_backward.1 = (bf16[4,2720,256]{2,1,0:T(8,128)(2,1)S(1)}, f32[4,2,1024]{2,1,0:T(2,128)S(1)}) custom-call(bf16[3,2720,1024]{2,1,0:T(8,128)(2,1)} %bitcast.135, bf16[4,2720,256]{2,1,0:T(8,128)(2,1)} %all-to-all-done.x_ref, f32[2720,1024]{1,0:T(8,128)} %get-tuple-element.40.res_ref, f32[4,6,1024]{2,1,0:T(8,128)S(1)} %copy-done.5, ...), custom_call_target="tpu_custom_call" | custom-call | flops 17112760320 | bytes 45285376 | tf_op jit(solution)/shard_map/input_backward/pallas_call | solution.py:464
  747.4 2.5 copy-done.1
  750.9 10.4 all-to-all-start.7
  764.4 1.1 all_to_all.46
  765.5 10.5 all-to-all-done.7
  776.0 3.7 all-to-all-start.9
  780.2 11.2 %all-to-all-done.9 = f32[32,1,2308]{2,1,0:T(1,128)S(1)} async-done(((f32[32,1,2308]{2,1,0:T(1,128)}), f32[32,1,2308]{2,1,0:T(1,128)S(1)}, u32[]{:S(2)}, u32[]{:S(2)}) %all-to-all-start.9) | async-done | bytes 295456 | tf_op jit(solution)/shard_map/all_to_all | solution.py:612
  791.3 17.4 %all_to_all.58 = f32[32,16,128]{2,1,0:T(8,128)S(1)} all-to-all(f32[32,16,128]{2,1,0:T(8,128)S(1)} %bitcast.113), channel_id=1, replica_groups=mesh['row'=8,'col'=4] {'row','col'}, dimensions={0} | all-to-all | bytes 524288 | tf_op jit(solution)/shard_map/all_to_all | solution.py:612
  808.8 128.0 %all_to_all.59 = bf16[4,2720,256]{2,1,0:T(8,128)(2,1)} all-to-all(bf16[4,2720,256]{2,1,0:T(8,128)(2,1)} %copy-done.1), channel_id=1, replica_groups=mesh['row'=8,'col'=4] {'col'}, dimensions={0} | all-to-all | bytes 11141120 | tf_op jit(solution)/shard_map/all_to_all | solution.py:612
  936.8 5.3 all-to-all-start.5
  944.6 1.0 convolution_bitcast_fusion
  945.6 1.2 copy.127
  948.2 8.3 copy.117
  956.5 110.2 %all-to-all-done.5 = bf16[4,2720,256]{2,1,0:T(8,128)(2,1)} async-done(((bf16[4,2720,256]{2,1,0:T(8,128)(2,1)}), bf16[4,2720,256]{2,1,0:T(8,128)(2,1)}, u32[]{:S(2)}, u32[]{:S(2)}) %all-to-all-start.5) | async-done | bytes 5570592 | tf_op jit(solution)/shard_map/all_to_all | solution.py:612
  1066.7 8.3 copy.115
  1075.0 1.0 bitcast_convert_fusion.1
  1076.1 0.9 copy.124
  1077.7 12.1 %reduce-scatter.5.cloned.1.call-done = bf16[1,128,2048]{1,2,0:T(8,128)(2,1)} async-done(((bf16[32,128,2048]{1,2,0:T(8,128)(2,1)}), bf16[1,128,2048]{1,2,0:T(8,128)(2,1)}) %reduce-scatter.5.cloned.1.call-update) | async-done | bytes 524304 | tf_op jit(solution)/shard_map/reduce_scatter | solution.py:769
  1089.9 1.1 bitcast_convert_fusion
  1091.0 0.9 slice_bitcast_fusion
  1091.8 1.0 copy.126
  (117 shorter events, 21.7 us)
Async XLA Ops:
  7.2 31.5 %copy-start = (bf16[6,128,256]{2,1,0:T(8,128)(2,1)S(1)}, bf16[6,128,256]{2,1,0:T(8,128)(2,1)}, u32[]{:S(2)}) copy-start(bf16[6,128,256]{2,1,0:T(8,128)(2,1)} %param.27) | copy-start | bytes 1179652
  7.2 143.0 %all-gather.5.cloned.1.call-start = ((), (), s32[]{:S(2)}) async-start(), calls=%async_computation.14 | async-start | bytes 6488064 | tf_op jit(solution)/shard_map/all_gather | solution.py:656
  7.9 280.4 %all-gather.7.cloned.1.call-start = ((), (), s32[]{:S(2)}) async-start(), calls=%async_computation.15 | async-start | bytes 19464192 | tf_op jit(solution)/shard_map/all_gather | solution.py:657
  13.4 20.5 %all-to-all-start.1 = ((bf16[32,16,256]{2,1,0:T(8,128)(2,1)}), bf16[32,16,256]{2,1,0:T(8,128)(2,1)S(1)}, u32[]{:S(2)}, u32[]{:S(2)}) async-start(bf16[32,16,256]{2,1,0:T(8,128)(2,1)} %broadcast_in_dim.32), calls=%async_computation.1 | async-start | bytes 524288 | tf_op jit(solution)/shard_map/all_to_all | solution.py:612
  34.5 7.2 all-to-all-start.3
  37.9 0.7 copy-start.8
  41.7 28.8 %all-to-all-start.2 = ((f32[32,4,6,256]{3,1,2,0:T(4,128)}), f32[32,4,6,256]{3,1,2,0:T(4,128)S(1)}, u32[]{:S(2)}, u32[]{:S(2)}) async-start(f32[32,4,6,256]{3,1,2,0:T(4,128)} %copy.107), calls=%async_computation.2 | async-start | bytes 1572864 | tf_op jit(solution)/shard_map/all_to_all | solution.py:612
  70.5 70.2 %all-to-all-start = ((bf16[4,2720,256]{2,1,0:T(8,128)(2,1)}), bf16[4,2720,256]{2,1,0:T(8,128)(2,1)}, u32[]{:S(2)}, u32[]{:S(2)}) async-start(bf16[4,2720,256]{2,1,0:T(8,128)(2,1)} %bitcast.102), calls=%async_computation | async-start | bytes 11141120 | tf_op jit(solution)/shard_map/all_to_all | solution.py:612
  140.7 170.4 %all-to-all-start.4 = ((bf16[4,2720,256]{2,1,0:T(8,128)(2,1)}), bf16[4,2720,256]{2,1,0:T(8,128)(2,1)}, u32[]{:S(2)}, u32[]{:S(2)}) async-start(bf16[4,2720,256]{2,1,0:T(8,128)(2,1)} %bitcast.100), calls=%async_computation.4 | async-start | bytes 11141120 | tf_op jit(solution)/shard_map/all_to_all | solution.py:612
  145.9 929.2 %reduce-scatter.3.cloned.1.call-start = ((), (), s32[]{:S(2)}) async-start(), calls=%async_computation.12 | async-start | bytes 8650752 | tf_op jit(solution)/shard_map/reduce_scatter | solution.py:792
  147.2 33.6 %copy-start.2 = (bf16[4,680,128]{2,1,0:T(8,128)(2,1)}, bf16[4,680,128]{2,1,0:T(8,128)(2,1)S(1)}, u32[]{:S(2)}) copy-start(bf16[4,680,128]{2,1,0:T(8,128)(2,1)S(1)} %compare_convert_fusion.qm_ref) | copy-start | bytes 2088964
  147.8 33.0 %copy-start.3 = (bf16[4,680,128]{2,1,0:T(8,128)(2,1)}, bf16[4,680,128]{2,1,0:T(8,128)(2,1)S(1)}, u32[]{:S(2)}) copy-start(bf16[4,680,128]{2,1,0:T(8,128)(2,1)S(1)} %select_convert_fusion.km_ref) | copy-start | bytes 2088964
  148.1 32.7 %copy-start.6 = (f32[1,1024]{1,0:T(1,128)}, f32[1,1024]{1,0:T(1,128)S(1)}, u32[]{:S(2)}) copy-start(f32[1,1024]{1,0:T(1,128)S(1)} %broadcast_in_dim_reshape.3.gain_ref) | copy-start | bytes 12292
  150.1 28.2 %copy-start.4 = (f32[4,6,1024]{2,1,0:T(8,128)}, f32[4,6,1024]{2,1,0:T(8,128)S(1)}, u32[]{:S(2)}) copy-start(f32[4,6,1024]{2,1,0:T(8,128)S(1)} %copy.109.mod_ref) | copy-start | bytes 294916
  178.4 2.4 copy-start.7
  628.4 461.5 %reduce-scatter.5.cloned.1.call-start = ((), (), s32[]{:S(2)}) async-start(), calls=%async_computation.13 | async-start | bytes 17301504 | tf_op jit(solution)/shard_map/reduce_scatter | solution.py:769
  712.8 0.9 copy-start.5
  713.7 36.2 %copy-start.10 = (f32[4,4,1024]{2,1,0:T(4,128)S(1)}, f32[4,4,1024]{2,1,0:T(4,128)}, u32[]{:S(2)}) copy-start(f32[4,4,1024]{2,1,0:T(4,128)} %get-tuple-element.43) | copy-start | bytes 196612
  713.7 47.6 %copy-start.9 = (f32[4,8,1024]{2,1,0:T(8,128)S(1)}, f32[4,8,1024]{2,1,0:T(8,128)}, u32[]{:S(2)}) copy-start(f32[4,8,1024]{2,1,0:T(8,128)} %get-tuple-element.46) | copy-start | bytes 393220
  713.7 48.2 %copy-start.14 = (f32[1,1024]{1,0:T(1,128)S(1)}, f32[1,1024]{1,0:T(1,128)}, u32[]{:S(2)}) copy-start(f32[1,1024]{1,0:T(1,128)} %get-tuple-element.47) | copy-start | bytes 12292
  713.7 48.9 %copy-start.12 = (f32[1,4096]{1,0:T(1,128)S(1)}, f32[1,4096]{1,0:T(1,128)}, u32[]{:S(2)}) copy-start(f32[1,4096]{1,0:T(1,128)} %get-tuple-element.48) | copy-start | bytes 49156
  713.7 49.6 %copy-start.13 = (f32[1,1024]{1,0:T(1,128)S(1)}, f32[1,1024]{1,0:T(1,128)}, u32[]{:S(2)}) copy-start(f32[1,1024]{1,0:T(1,128)} %get-tuple-element.49) | copy-start | bytes 12292
  747.4 2.5 copy-start.1
  750.9 25.0 %all-to-all-start.7 = ((bf16[32,4,6,256]{3,1,2,0:T(4,128)(2,1)}), bf16[32,4,6,256]{3,1,2,0:T(4,128)(2,1)S(1)}, u32[]{:S(2)}, u32[]{:S(2)}) async-start(bf16[32,4,6,256]{3,1,2,0:T(4,128)(2,1)} %bitcast.26), calls=%async_computation.7 | async-start | bytes 786432 | tf_op jit(solution)/shard_map/all_to_all | solution.py:612
  776.0 15.4 %all-to-all-start.9 = ((f32[32,1,2308]{2,1,0:T(1,128)}), f32[32,1,2308]{2,1,0:T(1,128)S(1)}, u32[]{:S(2)}, u32[]{:S(2)}) async-start(f32[32,1,2308]{2,1,0:T(1,128)} %all_to_all.46), calls=%async_computation.10 | async-start | bytes 622592 | tf_op jit(solution)/shard_map/all_to_all | solution.py:612
  936.8 10.8 copy-start.11
  936.8 129.9 %all-to-all-start.5 = ((bf16[4,2720,256]{2,1,0:T(8,128)(2,1)}), bf16[4,2720,256]{2,1,0:T(8,128)(2,1)}, u32[]{:S(2)}, u32[]{:S(2)}) async-start(bf16[4,2720,256]{2,1,0:T(8,128)(2,1)} %get-tuple-element.36), calls=%async_computation.5 | async-start | bytes 11141120 | tf_op jit(solution)/shard_map/all_to_all | solution.py:612
Sparse Core Ops, SparseCore 0:
  10.9 83.9 all-gather.4
  96.4 191.8 all-gather.6
  628.5 157.5 reduce-scatter.2
  788.3 301.5 reduce-scatter.4

commit v2 on v1

--- a/solution.py
+++ b/solution.py
@@ -4,6 +4,7 @@
 from jax import lax
 from jax.sharding import PartitionSpec as P
 from jax.experimental import pallas as pl
+from jax.experimental.layout import Layout, with_layout_constraint
 from jax.experimental.pallas import tpu as pltpu
 
 HEAD_DIM = 64
@@ -556,56 +557,259 @@
     )(left_a, left_b, right_a, right_b)
 
 
-def attn_grad_kernel(left_a, left_b, right_a, right_b, out_ref, turned):
-    which = pl.program_id(0)
-
-    def write(value):
-        height, part = out_ref.shape[2:]
-        value = value.astype(jnp.bfloat16)
-        for c in range(out_ref.shape[1]):
-            piece = value[:, c * part : (c + 1) * part]
-            out_ref[:, c] = piece.reshape(out_ref.shape[0], height, part)
-
-    @pl.when(which == 0)
-    def _():
-        turn_rows(left_a, turned)
-        write(nn(turned[...], right_a[...]))
-
-    @pl.when(which == 1)
-    def _():
-        turn_rows(left_b, turned)
-
-    @pl.when(which > 0)
-    def _():
-        write(nn(turned[...], right_b[0]))
-
-
-def attn_grads(attended, d_one, ln_one, d_qkv, blocks):
-    row_blocks, col_blocks = blocks
+MESH = pl.DeviceIdType.MESH
+
+
+class Place:
+    def __init__(self):
+        row = lax.axis_index("row")
+        col = lax.axis_index("col")
+        self.z, self.x, self.y, self.k = row // 2, row % 2, col // 2, col % 2
+
+    def other(self, z=None, x=None, y=None, k=None):
+        z = self.z if z is None else z
+        x = self.x if x is None else x
+        y = self.y if y is None else y
+        k = self.k if k is None else k
+        return (z * 2 + x, y * 2 + k)
+
+    def partners(self):
+        near = [self.other(k=1 - self.k), self.other(x=1 - self.x), self.other(y=1 - self.y)]
+        return near + [self.other(z=(self.z + step) % 4) for step in (1, 2, 3)]
+
+    def meet(self):
+        barrier = pltpu.get_barrier_semaphore()
+        partners = self.partners()
+        for partner in partners:
+            pl.semaphore_signal(barrier, inc=1, device_id=partner, device_id_type=MESH)
+        pl.semaphore_wait(barrier, len(partners))
+
+
+def add_into(target, first, second):
+    for index in range(first.shape[0]):
+        value = first[index].astype(jnp.float32) + second[index].astype(jnp.float32)
+        target[index] = value.astype(target.dtype)
+
+
+def attn_grad_kernel(
+    att_ref, one_ref, ln_ref, d_ref, totals_ref, mod_ref,
+    out_ref, totals_out, mod_out,
+    left, turned, right, mine, core_in, after_core, x_in, after_x, z_in, summed, y_send, y_in,
+    t_core, t_x, t_z, t_y, t_sum, e_core, e_y, e_x,
+    load_sems, send_sems, recv_sems,
+):
+    at = Place()
+    loads = [
+        pltpu.make_async_copy(att_ref, left, load_sems.at[0]),
+        pltpu.make_async_copy(ln_ref, left, load_sems.at[1]),
+        pltpu.make_async_copy(one_ref, right.at[0], load_sems.at[2]),
+        pltpu.make_async_copy(d_ref.at[0], right.at[1], load_sems.at[3]),
+        pltpu.make_async_copy(d_ref.at[1], right.at[0], load_sems.at[4]),
+        pltpu.make_async_copy(d_ref.at[2], right.at[1], load_sems.at[5]),
+    ]
+    loads[0].start()
+    loads[2].start()
+    loads[3].start()
+    at.meet()
+    across = at.other(k=1 - at.k)
+    beside = at.other(x=1 - at.x)
+    over = at.other(y=1 - at.y)
+    ahead = [(at.z + step) % 4 for step in (1, 2, 3)]
+    sent = []
+
+    def send(flow, which, source, target, device):
+        copy = pltpu.make_async_remote_copy(
+            src_ref=source,
+            dst_ref=target,
+            send_sem=send_sems.at[flow, which],
+            recv_sem=recv_sems.at[flow, which],
+            device_id=device,
+            device_id_type=MESH,
+        )
+        copy.start()
+        sent.append(copy)
+        return copy
+
+    flights = {}
+
+    flights[4, 0] = send(4, 0, totals_ref.at[1 - at.k], t_core, across)
+    flights[5, 0] = send(5, 0, mod_ref.at[1 - at.k], e_core.at[at.k], across)
+
+    def small_one():
+        flights[4, 0].wait_recv()
+        for y in range(2):
+            t_core[y] = t_core[y] + totals_ref[at.k, y]
+        flights[4, 1] = send(4, 1, t_core, t_x, beside)
+        flights[5, 0].wait_recv()
+        for y in range(2):
+            e_core[at.k, y] = mod_ref[at.k, y]
+        flights[5, 1] = send(5, 1, e_core.at[:, 1 - at.y], e_y.at[at.y], over)
+
+    def small_two():
+        flights[4, 1].wait_recv()
+        for y in range(2):
+            t_z[at.z, y] = t_x[y] + t_core[y]
+        flights[4, 2] = [
+            send(4, 2 + index, t_z.at[at.z], t_z.at[at.z], at.other(z=z))
+            for index, z in enumerate(ahead)
+        ]
+        flights[5, 1].wait_recv()
+        for k in range(2):
+            e_y[at.y, k] = e_core[k, at.y]
+        flights[5, 2] = send(5, 2, e_y, e_x.at[at.x], beside)
+
+    def small_three():
+        for copy in flights[4, 2]:
+            copy.wait_recv()
+        for y in range(2):
+            t_sum[y] = (t_z[0, y] + t_z[1, y]) + (t_z[2, y] + t_z[3, y])
+        flights[4, 3] = send(4, 5, t_sum.at[1 - at.y], t_y, over)
+        flights[5, 2].wait_recv()
+        for y in range(2):
+            for k in range(2):
+                e_x[at.x, y, k] = e_y[y, k]
+        mod_out[at.z] = e_x[...]
+        flights[5, 3] = [
+            send(5, 3 + index, e_x, mod_out.at[at.z], at.other(z=z))
+            for index, z in enumerate(ahead)
+        ]
+
+    def small_four():
+        flights[4, 3].wait_recv()
+        totals_out[...] = t_sum[at.y] + t_y[...]
+        for copy in flights[5, 3]:
+            copy.wait_recv()
+
+    def compute(p):
+        for c in range(4):
+            span = slice(c * 256, (c + 1) * 256)
+            value = nn(turned[...], right[p % 2, :, span]).astype(jnp.bfloat16)
+            for r in range(8):
+                mine[p, c % 2, r % 2, r // 2, c // 2] = value[r * 128 : (r + 1) * 128]
+        flights[p, 0] = send(p, 0, mine.at[p, 1 - at.k], core_in.at[p], across)
+
+    def core_done(p):
+        flights[p, 0].wait_recv()
+        for x in range(2):
+            for z in range(4):
+                add_into(after_core.at[p, x, z], mine.at[p, at.k, x, z], core_in.at[p, x, z])
+        flights[p, 1] = send(p, 1, after_core.at[p, 1 - at.x], x_in.at[p], beside)
+
+    def x_done(p):
+        flights[p, 1].wait_recv()
+        for z in range(4):
+            add_into(after_x.at[p, z], after_core.at[p, at.x, z], x_in.at[p, z])
+        flights[p, 2] = [
+            send(p, 2 + index, after_x.at[p, z], z_in.at[p, index], at.other(z=z))
+            for index, z in enumerate(ahead)
+        ]
+
+    def z_done(p):
+        for copy in flights[p, 2]:
+            copy.wait_recv()
+        for y in range(2):
+            value = after_x[p, at.z, y].astype(jnp.float32)
+            for index in range(3):
+                value = value + z_in[p, index, y].astype(jnp.float32)
+            summed[p, y] = value
+        y_send[p] = summed[p, 1 - at.y].astype(jnp.bfloat16)
+        flights[p, 3] = send(p, 5, y_send.at[p], y_in.at[p], over)
+
+    def y_done(p):
+        flights[p, 3].wait_recv()
+        out_ref[p] = summed[p, at.y] + y_in[p].astype(jnp.float32)
+
+    loads[0].wait()
+    turn_rows(left, turned)
+    loads[1].start()
+    loads[2].wait()
+    compute(0)
+    loads[4].start()
+    small_one()
+    core_done(0)
+    loads[1].wait()
+    turn_rows(left, turned)
+    loads[3].wait()
+    compute(1)
+    loads[5].start()
+    core_done(1)
+    small_two()
+    x_done(0)
+    loads[4].wait()
+    compute(2)
+    core_done(2)
+    small_three()
+    loads[5].wait()
+    compute(3)
+    core_done(3)
+    x_done(1)
+    z_done(0)
+    small_four()
+    x_done(2)
+    z_done(1)
+    y_done(0)
+    x_done(3)
+    z_done(2)
+    y_done(1)
+    z_done(3)
+    y_done(2)
+    y_done(3)
+    for copy in sent:
+        copy.wait_send()
+
+
+def attn_grads_everywhere(attended, d_one, ln_one, d_qkv, totals, d_mod):
     count, width = attended.shape
-    part = width // col_blocks
-    height = width // row_blocks
-    fixed = pl.BlockSpec((count, width), lambda p: (0, 0), pipeline_mode=pl.Buffered(1))
+    f32, bf16 = jnp.float32, jnp.bfloat16
+    anywhere = pl.BlockSpec(memory_space=pl.ANY)
+    inside = pl.BlockSpec(memory_space=pltpu.VMEM)
+    images = d_mod.shape[2]
+    vec = totals.shape[2:]
+    tile = (128, 256)
     return pl.pallas_call(
         attn_grad_kernel,
-        grid=(4,),
-        in_specs=[
-            fixed,
-            fixed,
-            fixed,
-            pl.BlockSpec((1, count, width), lambda p: (jnp.maximum(p - 1, 0), 0, 0)),
-        ],
-        out_specs=pl.BlockSpec((row_blocks, col_blocks, height, part), lambda p: (0, 0, 0, p)),
-        out_shape=jax.ShapeDtypeStruct((row_blocks, col_blocks, height, 4 * part), jnp.bfloat16),
-        scratch_shapes=[pltpu.VMEM((width, count), jnp.bfloat16)],
-        compiler_params=pltpu.CompilerParams(vmem_limit_bytes=60 << 20),
+        in_specs=[anywhere] * 4 + [inside] * 2,
+        out_specs=[inside] * 3,
+        out_shape=[
+            jax.ShapeDtypeStruct((4,) + tile, f32),
+            jax.ShapeDtypeStruct(vec, f32),
+            jax.ShapeDtypeStruct((4, 2, 2, 2) + d_mod.shape[2:], bf16),
+        ],
+        scratch_shapes=[
+            pltpu.VMEM((count, width), bf16),
+            pltpu.VMEM((width, count), bf16),
+            pltpu.VMEM((2, count, width), bf16),
+            pltpu.VMEM((4, 2, 2, 4, 2) + tile, bf16),
+            pltpu.VMEM((4, 2, 4, 2) + tile, bf16),
+            pltpu.VMEM((4, 2, 4, 2) + tile, bf16),
+            pltpu.VMEM((4, 4, 2) + tile, bf16),
+            pltpu.VMEM((4, 4, 2) + tile, bf16),
+            pltpu.VMEM((4, 3, 2) + tile, bf16),
+            pltpu.VMEM((4, 2) + tile, f32),
+            pltpu.VMEM((4,) + tile, bf16),
+            pltpu.VMEM((4,) + tile, bf16),
+            pltpu.VMEM((2,) + vec, f32),
+            pltpu.VMEM((2,) + vec, f32),
+            pltpu.VMEM((4, 2) + vec, f32),
+            pltpu.VMEM(vec, f32),
+            pltpu.VMEM((2,) + vec, f32),
+            pltpu.VMEM((2, 2) + d_mod.shape[2:], bf16),
+            pltpu.VMEM((2, 2) + d_mod.shape[2:], bf16),
+            pltpu.VMEM((2, 2, 2) + d_mod.shape[2:], bf16),
+            pltpu.SemaphoreType.DMA((6,)),
+            pltpu.SemaphoreType.DMA((6, 6)),
+            pltpu.SemaphoreType.DMA((6, 6)),
+        ],
+        compiler_params=pltpu.CompilerParams(
+            vmem_limit_bytes=62 << 20, collective_id=1, has_side_effects=True
+        ),
         cost_estimate=pl.CostEstimate(
-            flops=8 * count * width * width,
+            flops=8 * count * width * width * 2,
             bytes_accessed=count * width * 12 + width * width * 8,
             transcendentals=0,
         ),
         name="attn_grads",
-    )(attended, ln_one, d_one, d_qkv)
+    )(attended, d_one, ln_one, d_qkv, totals, d_mod)
 
 
 def swap(pieces, axes):
@@ -617,6 +821,14 @@
 
 
 BOTH = ("row", "col")
+
+
+def row_major(value):
+    return with_layout_constraint(value, Layout(tuple(range(value.ndim))))
+
+
+def after(value, *others):
+    return lax.optimization_barrier((value,) + others)[0]
 
 
 def shards(
@@ -654,7 +866,9 @@
     f32, bf16 = jnp.float32, jnp.bfloat16
 
     qkv_parts = lax.all_gather(attention_triple_matrix.transpose(1, 0, 2), BOTH)
-    rest_parts = lax.all_gather(jnp.concatenate([w_proj, w_fc1, w_fc2.T], axis=1), BOTH)
+    rest_parts = lax.all_gather(
+        row_major(jnp.concatenate([w_proj, w_fc1, w_fc2.T], axis=1)), BOTH
+    )
 
     def whole(parts):
         parts = parts.reshape((rows, groups) + parts.shape[1:])
@@ -721,7 +935,7 @@
     def to_features(pieces):
         if not aligned:
             pieces = pieces[0].reshape(count, groups, part).transpose(1, 0, 2)
-        return swap(pieces, "col").reshape(groups * count, part).T
+        return swap(pieces, "col").reshape(groups * count, part)
 
     tok_in = to_tokens(tokens)
     grad_in = to_tokens(out_grad)
@@ -766,7 +980,9 @@
         wide_ffn = jnp.concatenate(
             [spread(wide_ffn[:, :hidden_width]), spread(wide_ffn[:, hidden_width:])], axis=2
         )
-    wide_ffn = lax.psum_scatter(wide_ffn, BOTH, scatter_dimension=0, tiled=False).astype(f32)
+    d_attended, wide_ffn = lax.optimization_barrier((d_attended, wide_ffn))
+    wide_ffn = row_major(lax.psum_scatter(wide_ffn, BOTH, scatter_dimension=0, tiled=False))
+    wide_ffn = wide_ffn.astype(f32)
     grad_fc1 = wide_ffn[:, :ff_part]
     grad_fc2 = wide_ffn[:, ff_part:].T
 
@@ -779,19 +995,8 @@
         log_sums,
         d_attended.reshape(images, length, width),
     )
+    d_qkv, layer_out = lax.optimization_barrier((d_qkv, layer_out))
     d_qkv = d_qkv.reshape(3, count, width)
-    wide_attn = attn_grads(attn_rows, d_one, ln_one, d_qkv, blocks)
-    if aligned:
-        wide_attn = wide_attn.reshape(everyone, block, 4 * part)
-    else:
-        wide_attn = wide_attn[0, 0]
-        wide_attn = jnp.concatenate(
-            [spread(wide_attn[:, index * width : (index + 1) * width]) for index in range(4)],
-            axis=2,
-        )
-    wide_attn = lax.psum_scatter(wide_attn, BOTH, scatter_dimension=0, tiled=False).astype(f32)
-    grad_proj = wide_attn[:, :part]
-    grad_qkv = wide_attn[:, part:].reshape(block, 3, part)
     token_pieces, first_sums = input_backward(
         d_qkv, tok_in, d_res, modulation, qkv_parts, blocks, length
     )
@@ -808,13 +1013,36 @@
         ],
         axis=1,
     )
-    totals = jnp.broadcast_to(totals[None], (rows,) + totals.shape)
-    totals = swap(totals.reshape(everyone, -1), BOTH).sum(axis=0)
     d_mod = jnp.concatenate([first_sums, mod_sums], axis=1).astype(bf16)
     d_mod = d_mod.reshape(images, 6, groups, part).transpose(2, 0, 1, 3)
-    d_mod = jnp.broadcast_to(d_mod[None], (rows,) + d_mod.shape)
-    d_mod = swap(d_mod.reshape((everyone,) + d_mod.shape[2:]), BOTH)
-    d_mod = d_mod.reshape(everyone * images, 6, part)
+    if aligned:
+        held = totals.shape[1]
+        totals = jnp.pad(totals, ((0, 0), (0, -held % 1024)))
+        totals = totals.reshape(2, 2, -1, 128).transpose(1, 0, 2, 3)
+        d_mod = d_mod.reshape(2, 2, images * 6, part).transpose(1, 0, 2, 3)
+        wide_attn, totals, d_mod = attn_grads_everywhere(
+            attn_rows, d_one, ln_one, d_qkv, totals, d_mod
+        )
+        d_mod, grad_tokens = lax.optimization_barrier((d_mod, grad_tokens))
+        totals = totals.reshape(-1)[:held]
+        d_mod = d_mod.reshape(everyone * images, 6, part)
+        grad_proj = wide_attn[0]
+        grad_qkv = wide_attn[1:].transpose(1, 0, 2)
+    else:
+        wide_attn = [
+            jnp.einsum("td,tf->df", one, two, preferred_element_type=f32).astype(bf16)
+            for one, two in [(attn_rows, d_one)] + [(ln_one, d_qkv[index]) for index in range(3)]
+        ]
+        wide_attn = jnp.concatenate([spread(wide) for wide in wide_attn], axis=2)
+        wide_attn = row_major(lax.psum_scatter(wide_attn, BOTH, scatter_dimension=0, tiled=False))
+        wide_attn = wide_attn.astype(f32)
+        grad_proj = wide_attn[:, :part]
+        grad_qkv = wide_attn[:, part:].reshape(block, 3, part)
+        totals = jnp.broadcast_to(totals[None], (rows,) + totals.shape)
+        totals = swap(totals.reshape(everyone, -1), BOTH).sum(axis=0)
+        d_mod = jnp.broadcast_to(d_mod[None], (rows,) + d_mod.shape)
+        d_mod = swap(d_mod.reshape((everyone,) + d_mod.shape[2:]), BOTH)
+        d_mod = d_mod.reshape(everyone * images, 6, part)
     grad_ada = jnp.einsum("ic,isd->scd", soft_mine, d_mod, preferred_element_type=f32)
     grad_bada = jnp.sum(d_mod.astype(f32), axis=0)
     d_soft = jnp.einsum("isd,scd->ic", d_mod, w_ada, preferred_element_type=f32)
@@ -827,8 +1055,8 @@
     _, silu_pull = jax.vjp(jax.nn.silu, cond_float)
     grad_condition = silu_pull(d_soft)[0].astype(bf16)
     return (
-        layer_out,
-        grad_tokens,
+        layer_out.T,
+        grad_tokens.T,
         grad_condition,
         grad_qkv,
         totals[: cuts[0]].reshape(3, part),

time: 1110 us -> 899 us (0.81)
  waiting for transfers between devices: 282 us -> 123 us
  Pallas kernels: 484 us -> 637 us
  blocking collectives: 145 us -> 0 us
  local copies, waits for them, and re-layouts: 116 us -> 62.3 us
    all_to_all x2 -> x0, blocking collectives: 145 us -> none  [swap(): lax.all_to_all(pieces, axes, split_axis=0, concat_axis=0, tiled=False)]
    pallas_call x1, Pallas kernels: 35 us -> 178 us  [attn_grads_everywhere(): pl.pallas_call(attn_grad_kernel, in_specs=[anywhere] * 4 + [inside] * 2,...]
    all_to_all x8, waiting for transfers between devices: 217 us -> 114 us  [swap(): lax.all_to_all(pieces, axes, split_axis=0, concat_axis=0, tiled=False)]
    reshape x5 -> x3, local copies, waits for them, and re-layouts: 51.7 us -> 1.29 us  [the longest x2 0.67 us: shards(): d_mod = d_mod.reshape(2, 2, images * 6, part).transpose(1, 0, 2, 3)]
    all_gather x1, waiting for transfers between devices: 52.1 us -> 8.26 us  [shards(): lax.all_gather(row_major(jnp.concatenate([w_proj, w_fc1, w_fc2.T], axis=1...]
    all_gather x1 -> x0, local copies, waits for them, and re-layouts: 22.8 us -> none  [shards(): lax.all_gather(jnp.concatenate([w_proj, w_fc1, w_fc2.T], axis=1), BOTH)]
    optimization_barrier x0 -> x2, local copies, waits for them, and re-layouts: none -> 16.6 us  [the longest x1 8.33 us: shards(): d_qkv, layer_out = lax.optimization_barrier((d_qkv, layer_out))]
    reduce_scatter x1, waiting for transfers between devices: 12.1 us -> 0.01 us  [shards(): lax.psum_scatter(wide_ffn, BOTH, scatter_dimension=0, tiled=False)]
  transfers between devices with their start and end apart: 12 -> 11, of which waited for: 9 -> 7; matrix products, arithmetic and copies ran while one was open for 10% -> 8% of each run, Pallas kernels for 16% -> 46%
where the time goes in v2:
time: 899 us; the launch traced here: 890 us
  Pallas kernels  637 us (71%)
  waiting for transfers between devices  123 us (14%)
  local copies, waits for them, and re-layouts  62.3 us (7%)
  starting transfers between devices  39.2 us (4%)
  between operations  14.7 us (2%)
  other arithmetic  12.1 us (1%)
    pallas_call x1, Pallas kernels, attn_grads_everywhere(): pl.pallas_call(attn_grad_kernel, in_specs=[anywhere] * 4 + [inside] * 2,...  178 us
    pallas_call x1, Pallas kernels, ffn(): pl.pallas_call(functools.partial(ffn_kernel, blocks, length, images), gri...  165 us
    pallas_call x1, Pallas kernels, attention_backward(): pl.pallas_call(backward_kernel, grid=(images, width // PAIR), in_specs=in...  115 us
    all_to_all x8, waiting for transfers between devices, swap(): lax.all_to_all(pieces, axes, split_axis=0, concat_axis=0, tiled=False)  114 us
    pallas_call x1, Pallas kernels, ffn_grads(): pl.pallas_call(ffn_grad_kernel, grid=(2, tiles), in_specs=[left, left, pl...  61.7 us
    pallas_call x1, Pallas kernels, attention_forward(): pl.pallas_call(forward_kernel, grid=(images, width // PAIR), in_specs=ins...  55.5 us
    all_to_all x8, starting transfers between devices, swap(): lax.all_to_all(pieces, axes, split_axis=0, concat_axis=0, tiled=False)  39.1 us
    pallas_call x1, Pallas kernels, input_backward(): pl.pallas_call(functools.partial(input_kernel, blocks, length, images), g...  33.8 us
  transfers between devices with their start and end apart: 11, of which 7 were waited for; matrix products, arithmetic and copies ran while one was open for 8% of the time, Pallas kernels for 46%

profile of v2, /device:TPU:0, one launch (start us, length us, event | category | flops | bytes accessed | tf_op | source)
XLA Modules:
  0.0 890.0 jit_solution(7775104726621958947)
XLA Ops:
  8.0 1.1 copy.94
  9.1 1.8 pad_maximum_fusion
  10.9 0.7 fusion.9
  11.7 0.7 broadcast_in_dim.45
  12.4 7.3 all-to-all-start.1
  23.8 8.1 all-to-all-done.1
  32.5 3.3 all-to-all-start.3
  37.1 1.0 copy.90
  38.2 1.5 all-to-all-done.3
  39.7 2.6 all-to-all-start.2
  42.3 8.2 copy.88
  50.6 19.3 %all-to-all-done.2 = f32[32,4,6,256]{3,1,2,0:T(4,128)S(1)} async-done(((f32[32,4,6,256]{3,1,2,0:T(4,128)}), f32[32,4,6,256]{3,1,2,0:T(4,128)S(1)}, u32[]{:S(2)}, u32[]{:S(2)}) %all-to-all-start.2) | async-done | bytes 786464 | tf_op jit(solution)/shard_map/all_to_all | solution.py:816
  69.9 5.1 all-to-all-start
  75.1 8.2 copy.93
  83.3 71.8 %all-to-all-done.x_ref = bf16[4,2720,256]{2,1,0:T(8,128)(2,1)} async-done(((bf16[4,2720,256]{2,1,0:T(8,128)(2,1)}), bf16[4,2720,256]{2,1,0:T(8,128)(2,1)}, u32[]{:S(2)}, u32[]{:S(2)}) %all-to-all-start) | async-done | bytes 5570592 | tf_op jit(solution)/shard_map/all_to_all | solution.py:816
  155.1 5.1 all-to-all-start.4
  160.3 0.8 constant_dynamic-slice_fusion
  164.6 28.1 %qkv_forward.1 = (bf16[2720,1024]{1,0:T(8,128)(2,1)S(1)}, f32[3,2720,1024]{2,1,0:T(8,128)}) custom-call(bf16[4,2720,256]{2,1,0:T(8,128)(2,1)} %all-to-all-done.x_ref, f32[4,6,1024]{2,1,0:T(8,128)S(1)} %copy.92.mod_ref, f32[3,1,1024]{2,1,0:T(1,128)S(1)} %reshape.183.bias_ref, bf16[32,3,128,256]{3,2,1,0:T(8,128)(2,1)} %bitcast.145), custom_call_target="tpu_custom_call" | custom-call | flops 17112760320 | bytes 50855936 | tf_op jit(solution)/shard_map/qkv_forward/pallas_call | solution.py:407
  192.7 2.4 copy-done.7
  195.2 55.5 %attention_forward.1 = (bf16[4,680,1024]{2,1,0:T(8,128)(2,1)}, f32[4,680,1024]{2,1,0:T(8,128)}) custom-call(f32[3,4,680,1024]{3,2,1,0:T(8,128)} %bitcast.108, f32[3,4,680,1024]{3,2,1,0:T(8,128)} %bitcast.109, f32[3,4,680,1024]{3,2,1,0:T(8,128)} %bitcast.110, f32[1,1024]{1,0:T(1,128)S(1)} %broadcast_in_dim_reshape.3.gain_ref, ...), custom_call_target="tpu_custom_call" | custom-call | flops 15151923200 | bytes 50135040 | tf_op jit(solution)/shard_map/attention_forward/pallas_call | solution.py:145
  250.6 6.3 all-to-all-done.4.g_ref
  256.9 8.3 all-gather.7.cloned.1.call-done
  265.2 165.0 %ffn_both.1 = (bf16[4,2720,256]{2,1,0:T(8,128)(2,1)}, bf16[2720,1024]{1,0:T(8,128)(2,1)}, bf16[2720,4096]{1,0:T(8,128)(2,1)}, bf16[2720,1024]{1,0:T(8,128)(2,1)}...) custom-call(bf16[4,2720,256]{2,1,0:T(8,128)(2,1)} %all-to-all-done.x, ...), custom_call_target="tpu_custom_call" | custom-call | flops 102676561920 | bytes 119144448 | tf_op jit(solution)/shard_map/ffn_both/pallas_call | solution.py:343
  430.2 61.7 %ffn_grads.1 = bf16[8,4,128,2048]{3,2,1,0:T(8,128)(2,1)} custom-call(bf16[2720,1024]{1,0:T(8,128)(2,1)} %get-tuple-element.47.left_a, bf16[2720,1024]{1,0:T(8,128)(2,1)} %get-tuple-element.48.left_b, bf16[2720,4096]{1,0:T(8,128)(2,1)} %get-tuple-element.49.right_a, bf16[2720,4096]{1,0:T(8,128)(2,1)} %get-tuple-element.50.right_b), custom_call_target="tpu_custom_call" | custom-call | flops 45634027520 | bytes 72482816 | tf_op jit(solution)/shard_map/ffn_grads/pallas_call | solution.py:536
  491.9 5.1 all-to-all-start.5
  497.1 115.5 %attention_backward.1 = (bf16[3,4,680,1024]{3,2,1,0:T(8,128)(2,1)}, f32[4,8,1024]{2,1,0:T(8,128)}) custom-call(f32[3,4,680,1024]{3,2,1,0:T(8,128)} %bitcast.111, f32[3,4,680,1024]{3,2,1,0:T(8,128)} %bitcast.112, f32[3,4,680,1024]{3,2,1,0:T(8,128)} %bitcast.113, f32[1,1024]{1,0:T(1,128)} %copy-done.6, bf16[4,680,128]{2,1,0:T(8,128)(2,1)} %copy-done.2, ...), custom_call_target="tpu_custom_call" | custom-call | flops 37879808000 | bytes 83558400 | tf_op jit(solution)/shard_map/attention_backward/pallas_call | solution.py:165
  612.6 0.9 reduce_sum.46
  617.2 6.6 all-to-all-done.5
  623.8 8.3 copy.96
  632.1 33.8 %input_backward.1 = (bf16[4,2720,256]{2,1,0:T(8,128)(2,1)S(1)}, f32[4,2,1024]{2,1,0:T(2,128)S(1)}) custom-call(bf16[3,2720,1024]{2,1,0:T(8,128)(2,1)} %bitcast.149, bf16[4,2720,256]{2,1,0:T(8,128)(2,1)} %all-to-all-done.x_ref, f32[2720,1024]{1,0:T(8,128)} %get-tuple-element.62.res_ref, f32[4,6,1024]{2,1,0:T(8,128)S(1)} %copy-done.5, ...), custom_call_target="tpu_custom_call" | custom-call | flops 17112760320 | bytes 45285376 | tf_op jit(solution)/shard_map/input_backward/pallas_call | solution.py:465
  666.0 2.4 copy-done.1
  669.2 5.4 all-to-all-start.6
  674.5 177.9 %attn_grads.1 = (f32[4,128,256]{2,1,0:T(8,128)}, f32[24,128]{1,0:T(8,128)}, bf16[4,2,2,2,24,256]{5,4,3,2,1,0:T(8,128)(2,1)}) custom-call(bf16[2720,1024]{1,0:T(8,128)(2,1)} %bitcast.148, bf16[2720,1024]{1,0:T(8,128)(2,1)} %get-tuple-element.55.one_ref, bf16[2720,1024]{1,0:T(8,128)(2,1)} %copy-done.7, bf16[3,2720,1024]{2,1,0:T(8,128)(2,1)} %bitcast.150, ...), custom_call_target="tpu_custom_call" | custom-call | flops 45634027520 | bytes 41811968 | tf_op jit(solution)/shard_map/attn_grads/pallas_call | solution.py:769
  853.7 1.2 slice.94
  854.9 1.3 slice_bitcast_fusion.6
  856.2 1.6 slice_bitcast_fusion.2
  857.7 1.8 slice_bitcast_fusion.1
  859.5 1.1 reshape.204
  861.0 0.7 broadcast_in_dim.53
  861.7 5.2 all-to-all-start.7
  866.9 1.3 slice_bitcast_fusion.7
  868.1 8.3 copy.100
  876.4 1.1 convolution_bitcast_fusion
  877.5 1.1 copy.105
  878.6 0.8 convert_reduce_fusion
  880.0 1.1 bitcast_convert_fusion
  881.2 0.9 slice_bitcast_fusion
  882.1 1.0 copy.104
  (103 shorter events, 16.9 us)
Async XLA Ops:
  7.2 29.5 %copy-start = (bf16[6,128,256]{2,1,0:T(8,128)(2,1)S(1)}, bf16[6,128,256]{2,1,0:T(8,128)(2,1)}, u32[]{:S(2)}) copy-start(bf16[6,128,256]{2,1,0:T(8,128)(2,1)} %param.27) | copy-start | bytes 1179652
  7.2 157.4 %all-gather.5.cloned.1.call-start = ((), (), s32[]{:S(2)}) async-start(), calls=%async_computation.10 | async-start | bytes 6488064 | tf_op jit(solution)/shard_map/all_gather | solution.py:868
  7.9 257.3 %all-gather.7.cloned.1.call-start = ((), (), s32[]{:S(2)}) async-start(), calls=%async_computation.11 | async-start | bytes 19464192 | tf_op jit(solution)/shard_map/all_gather | solution.py:869
  12.4 19.5 %all-to-all-start.1 = ((bf16[32,16,256]{2,1,0:T(8,128)(2,1)}), bf16[32,16,256]{2,1,0:T(8,128)(2,1)S(1)}, u32[]{:S(2)}, u32[]{:S(2)}) async-start(bf16[32,16,256]{2,1,0:T(8,128)(2,1)} %broadcast_in_dim.45), calls=%async_computation.1 | async-start | bytes 524288 | tf_op jit(solution)/shard_map/all_to_all | solution.py:816
  32.5 7.2 all-to-all-start.3
  35.9 0.7 copy-start.8
  39.7 30.2 %all-to-all-start.2 = ((f32[32,4,6,256]{3,1,2,0:T(4,128)}), f32[32,4,6,256]{3,1,2,0:T(4,128)S(1)}, u32[]{:S(2)}, u32[]{:S(2)}) async-start(f32[32,4,6,256]{3,1,2,0:T(4,128)} %copy.90), calls=%async_computation.2 | async-start | bytes 1572864 | tf_op jit(solution)/shard_map/all_to_all | solution.py:816
  69.9 85.2 %all-to-all-start = ((bf16[4,2720,256]{2,1,0:T(8,128)(2,1)}), bf16[4,2720,256]{2,1,0:T(8,128)(2,1)}, u32[]{:S(2)}, u32[]{:S(2)}) async-start(bf16[4,2720,256]{2,1,0:T(8,128)(2,1)} %bitcast.115), calls=%async_computation | async-start | bytes 11141120 | tf_op jit(solution)/shard_map/all_to_all | solution.py:816
  155.1 101.8 %all-to-all-start.4 = ((bf16[4,2720,256]{2,1,0:T(8,128)(2,1)}), bf16[4,2720,256]{2,1,0:T(8,128)(2,1)}, u32[]{:S(2)}, u32[]{:S(2)}) async-start(bf16[4,2720,256]{2,1,0:T(8,128)(2,1)} %bitcast.114), calls=%async_computation.4 | async-start | bytes 11141120 | tf_op jit(solution)/shard_map/all_to_all | solution.py:816
  160.3 719.8 %reduce-scatter.2.cloned.1.call-start = ((), (), s32[]{:S(2)}) async-start(), calls=%async_computation.9 | async-start | bytes 17301504 | tf_op jit(solution)/shard_map/reduce_scatter | solution.py:984
  161.6 33.6 %copy-start.2 = (bf16[4,680,128]{2,1,0:T(8,128)(2,1)}, bf16[4,680,128]{2,1,0:T(8,128)(2,1)S(1)}, u32[]{:S(2)}) copy-start(bf16[4,680,128]{2,1,0:T(8,128)(2,1)S(1)} %compare_convert_fusion.qm_ref) | copy-start | bytes 2088964
  162.2 33.0 %copy-start.3 = (bf16[4,680,128]{2,1,0:T(8,128)(2,1)}, bf16[4,680,128]{2,1,0:T(8,128)(2,1)S(1)}, u32[]{:S(2)}) copy-start(bf16[4,680,128]{2,1,0:T(8,128)(2,1)S(1)} %select_convert_fusion.km_ref) | copy-start | bytes 2088964
  162.5 32.7 %copy-start.6 = (f32[1,1024]{1,0:T(1,128)}, f32[1,1024]{1,0:T(1,128)S(1)}, u32[]{:S(2)}) copy-start(f32[1,1024]{1,0:T(1,128)S(1)} %broadcast_in_dim_reshape.3.gain_ref) | copy-start | bytes 12292
  164.5 28.2 %copy-start.4 = (f32[4,6,1024]{2,1,0:T(8,128)}, f32[4,6,1024]{2,1,0:T(8,128)S(1)}, u32[]{:S(2)}) copy-start(f32[4,6,1024]{2,1,0:T(8,128)S(1)} %copy.92.mod_ref) | copy-start | bytes 294916
  192.7 2.4 copy-start.7
  491.9 131.9 %all-to-all-start.5 = ((bf16[4,2720,256]{2,1,0:T(8,128)(2,1)}), bf16[4,2720,256]{2,1,0:T(8,128)(2,1)}, u32[]{:S(2)}, u32[]{:S(2)}) async-start(bf16[4,2720,256]{2,1,0:T(8,128)(2,1)} %get-tuple-element.53), calls=%async_computation.5 | async-start | bytes 11141120 | tf_op jit(solution)/shard_map/all_to_all | solution.py:816
  497.0 117.0 %copy-start.13 = (f32[1,1024]{1,0:T(1,128)S(1)}, f32[1,1024]{1,0:T(1,128)}, u32[]{:S(2)}) copy-start(f32[1,1024]{1,0:T(1,128)} %get-tuple-element.59) | copy-start | bytes 12292
  497.0 117.7 %copy-start.11 = (f32[1,4096]{1,0:T(1,128)S(1)}, f32[1,4096]{1,0:T(1,128)}, u32[]{:S(2)}) copy-start(f32[1,4096]{1,0:T(1,128)} %get-tuple-element.60) | copy-start | bytes 49156
  497.1 118.4 %copy-start.12 = (f32[1,1024]{1,0:T(1,128)S(1)}, f32[1,1024]{1,0:T(1,128)}, u32[]{:S(2)}) copy-start(f32[1,1024]{1,0:T(1,128)} %get-tuple-element.61) | copy-start | bytes 12292
  497.1 120.1 %copy-start.9 = (f32[4,4,1024]{2,1,0:T(4,128)S(1)}, f32[4,4,1024]{2,1,0:T(4,128)}, u32[]{:S(2)}) copy-start(f32[4,4,1024]{2,1,0:T(4,128)} %get-tuple-element.64) | copy-start | bytes 196612
  623.8 8.3 copy-start.5
  666.0 2.5 copy-start.1
  669.2 190.3 %all-to-all-start.6 = ((bf16[4,2720,256]{2,1,0:T(8,128)(2,1)}), bf16[4,2720,256]{2,1,0:T(8,128)(2,1)}, u32[]{:S(2)}, u32[]{:S(2)}) async-start(bf16[4,2720,256]{2,1,0:T(8,128)(2,1)} %copy-done.1), calls=%async_computation.6 | async-start | bytes 11141120 | tf_op jit(solution)/shard_map/all_to_all | solution.py:816
  861.7 17.7 %all-to-all-start.7 = ((f32[32,16,128]{2,1,0:T(8,128)}), f32[32,16,128]{2,1,0:T(8,128)S(1)}, u32[]{:S(2)}, u32[]{:S(2)}) async-start(f32[32,16,128]{2,1,0:T(8,128)} %bitcast.36), calls=%async_computation.7 | async-start | bytes 524288 | tf_op jit(solution)/shard_map/all_to_all | solution.py:816
  868.1 11.3 %copy-start.10 = (bf16[16,256]{1,0:T(8,128)(2,1)S(1)}, bf16[16,256]{1,0:T(8,128)(2,1)}, u32[]{:S(2)}) copy-start(bf16[16,256]{1,0:T(8,128)(2,1)} %param.16) | copy-start | bytes 24580
Sparse Core Ops, SparseCore 0:
  10.9 87.8 all-gather.4
  101.7 163.3 all-gather.6
  492.0 291.4 reduce-scatter.1

commit v3 on v2

--- a/solution.py
+++ b/solution.py
@@ -499,62 +499,43 @@
         target[:, start : start + size] = source[start : start + size, :].T
 
 
-def ffn_grad_kernel(left_a, left_b, right_a, right_b, out_ref, turned):
-    pair, tile = pl.program_id(0), pl.program_id(1)
-
-    def write(value):
-        value = value.astype(jnp.bfloat16)
-        out_ref[...] = value.reshape(out_ref.shape)
-
-    @pl.when((pair == 0) & (tile == 0))
+def plain_grad_kernel(left, right, out_ref, turned):
+    @pl.when(pl.program_id(0) == 0)
     def _():
-        turn_rows(left_a, turned)
-
-    @pl.when((pair == 1) & (tile == 0))
-    def _():
-        turn_rows(left_b, turned)
-
-    @pl.when(pair == 0)
-    def _():
-        write(nn(turned[...], right_a[...]))
-
-    @pl.when(pair == 1)
-    def _():
-        write(nn(turned[...], right_b[...]))
-
-
-def ffn_grads(left_a, right_a, left_b, right_b, blocks):
+        turn_rows(left, turned)
+
+    value = nn(turned[...], right[...]).astype(jnp.bfloat16)
+    out_ref[...] = value.reshape(out_ref.shape)
+
+
+def plain_grads(left, right, blocks):
     row_blocks, col_blocks = blocks
-    count, width = left_a.shape
-    ff = right_a.shape[1]
+    count, width = left.shape
+    ff = right.shape[1]
     ff_part = ff // col_blocks
     span = min(512, ff_part)
     inner = ff_part // span
-    tiles = ff // span
     height = width // row_blocks
-    left = pl.BlockSpec((count, width), lambda p, j: (0, 0))
     return pl.pallas_call(
-        ffn_grad_kernel,
-        grid=(2, tiles),
+        plain_grad_kernel,
+        grid=(ff // span,),
         in_specs=[
-            left,
-            left,
-            pl.BlockSpec((count, span), lambda p, j: (0, j * (1 - p) + (tiles - 1) * p)),
-            pl.BlockSpec((count, span), lambda p, j: (0, j * p)),
+            pl.BlockSpec((count, width), lambda j: (0, 0)),
+            pl.BlockSpec((count, span), lambda j: (0, j)),
         ],
         out_specs=pl.BlockSpec(
-            (row_blocks, 1, height, span), lambda p, j: (0, j // inner, 0, p * inner + j % inner)
+            (row_blocks, 1, height, span), lambda j: (0, j // inner, 0, j % inner)
         ),
-        out_shape=jax.ShapeDtypeStruct((row_blocks, col_blocks, height, 2 * ff_part), jnp.bfloat16),
+        out_shape=jax.ShapeDtypeStruct((row_blocks, col_blocks, height, ff_part), jnp.bfloat16),
         scratch_shapes=[pltpu.VMEM((width, count), jnp.bfloat16)],
         compiler_params=pltpu.CompilerParams(vmem_limit_bytes=56 << 20),
         cost_estimate=pl.CostEstimate(
-            flops=4 * count * width * ff,
-            bytes_accessed=count * width * 4 + count * ff * 4 + width * ff * 4,
+            flops=2 * count * width * ff,
+            bytes_accessed=count * width * 2 + count * ff * 2 + width * ff * 2,
             transcendentals=0,
         ),
-        name="ffn_grads",
-    )(left_a, left_b, right_a, right_b)
+        name="plain_grads",
+    )(left, right)
 
 
 MESH = pl.DeviceIdType.MESH
@@ -577,9 +558,9 @@
         near = [self.other(k=1 - self.k), self.other(x=1 - self.x), self.other(y=1 - self.y)]
         return near + [self.other(z=(self.z + step) % 4) for step in (1, 2, 3)]
 
-    def meet(self):
+    def meet(self, *more):
         barrier = pltpu.get_barrier_semaphore()
-        partners = self.partners()
+        partners = self.partners() + list(more)
         for partner in partners:
             pl.semaphore_signal(barrier, inc=1, device_id=partner, device_id_type=MESH)
         pl.semaphore_wait(barrier, len(partners))
@@ -591,25 +572,41 @@
         target[index] = value.astype(target.dtype)
 
 
-def attn_grad_kernel(
-    att_ref, one_ref, ln_ref, d_ref, totals_ref, mod_ref,
-    out_ref, totals_out, mod_out,
-    left, turned, right, mine, core_in, after_core, x_in, after_x, z_in, summed, y_send, y_in,
-    t_core, t_x, t_z, t_y, t_sum, e_core, e_y, e_x,
-    load_sems, send_sems, recv_sems,
-):
+def grad_kernel(small, *refs):
+    if small:
+        att_ref, one_ref, ln_ref, d_ref, totals_ref, mod_ref = refs[:6]
+        out_ref, totals_out, mod_out = refs[6:9]
+        refs = refs[9:]
+        t_core, t_x, t_z, t_y, t_sum, e_core, e_y, e_x = refs[:8]
+        refs = refs[8:]
+    else:
+        two_ref, hidden_ref, out_ref = refs[:3]
+        refs = refs[3:]
+    left, turned, right, mine, core_in, after_core, x_in, after_x = refs[:8]
+    z_in, summed, y_send, y_in, load_sems, send_sems, recv_sems = refs[8:]
     at = Place()
-    loads = [
-        pltpu.make_async_copy(att_ref, left, load_sems.at[0]),
-        pltpu.make_async_copy(ln_ref, left, load_sems.at[1]),
-        pltpu.make_async_copy(one_ref, right.at[0], load_sems.at[2]),
-        pltpu.make_async_copy(d_ref.at[0], right.at[1], load_sems.at[3]),
-        pltpu.make_async_copy(d_ref.at[1], right.at[0], load_sems.at[4]),
-        pltpu.make_async_copy(d_ref.at[2], right.at[1], load_sems.at[5]),
-    ]
-    loads[0].start()
-    loads[2].start()
-    loads[3].start()
+
+    def load(source, target, index):
+        copy = pltpu.make_async_copy(source, target, load_sems.at[index])
+        copy.start()
+        return copy
+
+    def load_right(p):
+        if small:
+            source = one_ref if p == 0 else d_ref.at[p - 1]
+            return [load(source, right.at[p % 2], 4 * p)]
+        part = hidden_ref.shape[1] // 4
+        return [
+            load(
+                hidden_ref.at[:, pl.ds(c * part + p * 256, 256)],
+                right.at[p % 2, :, pl.ds(c * 256, 256)],
+                4 * p + c,
+            )
+            for c in range(4)
+        ]
+
+    left_first = load(att_ref if small else two_ref, left, 16)
+    rights = [load_right(0), load_right(1)]
     at.meet()
     across = at.other(k=1 - at.k)
     beside = at.other(x=1 - at.x)
@@ -632,8 +629,9 @@
 
     flights = {}
 
-    flights[4, 0] = send(4, 0, totals_ref.at[1 - at.k], t_core, across)
-    flights[5, 0] = send(5, 0, mod_ref.at[1 - at.k], e_core.at[at.k], across)
+    def small_zero():
+        flights[4, 0] = send(4, 0, totals_ref.at[1 - at.k], t_core, across)
+        flights[5, 0] = send(5, 0, mod_ref.at[1 - at.k], e_core.at[at.k], across)
 
     def small_one():
         flights[4, 0].wait_recv()
@@ -693,6 +691,8 @@
         for x in range(2):
             for z in range(4):
                 add_into(after_core.at[p, x, z], mine.at[p, at.k, x, z], core_in.at[p, x, z])
+
+    def x_start(p):
         flights[p, 1] = send(p, 1, after_core.at[p, 1 - at.x], x_in.at[p], beside)
 
     def x_done(p):
@@ -719,97 +719,383 @@
         flights[p, 3].wait_recv()
         out_ref[p] = summed[p, at.y] + y_in[p].astype(jnp.float32)
 
-    loads[0].wait()
+    def right_ready(p):
+        for copy in rights[p]:
+            copy.wait()
+
+    hops = [small_zero, small_one, small_two, small_three, small_four]
+    if not small:
+        hops = [lambda: None] * 5
+    hops[0]()
+    left_first.wait()
     turn_rows(left, turned)
-    loads[1].start()
-    loads[2].wait()
+    if small:
+        left_second = load(ln_ref, left, 17)
+    right_ready(0)
     compute(0)
-    loads[4].start()
-    small_one()
+    rights.append(load_right(2))
+    hops[1]()
     core_done(0)
-    loads[1].wait()
-    turn_rows(left, turned)
-    loads[3].wait()
+    x_start(0)
+    if small:
+        left_second.wait()
+        turn_rows(left, turned)
+    right_ready(1)
     compute(1)
-    loads[5].start()
+    rights.append(load_right(3))
     core_done(1)
-    small_two()
+    hops[2]()
     x_done(0)
-    loads[4].wait()
+    x_start(1)
+    right_ready(2)
     compute(2)
     core_done(2)
-    small_three()
-    loads[5].wait()
+    hops[3]()
+    x_done(1)
+    x_start(2)
+    z_done(0)
+    right_ready(3)
     compute(3)
     core_done(3)
-    x_done(1)
-    z_done(0)
-    small_four()
+    hops[4]()
     x_done(2)
+    x_start(3)
     z_done(1)
     y_done(0)
-    x_done(3)
     z_done(2)
     y_done(1)
+    x_done(3)
+    y_done(2)
     z_done(3)
-    y_done(2)
     y_done(3)
     for copy in sent:
         copy.wait_send()
 
 
-def attn_grads_everywhere(attended, d_one, ln_one, d_qkv, totals, d_mod):
-    count, width = attended.shape
+def grads_everywhere(count, width, tensors, totals=None, d_mod=None):
+    f32, bf16 = jnp.float32, jnp.bfloat16
+    small = totals is not None
+    anywhere = pl.BlockSpec(memory_space=pl.ANY)
+    inside = pl.BlockSpec(memory_space=pltpu.VMEM)
+    tile = (128, 256)
+    vmem = pltpu.VMEM
+    outs = [jax.ShapeDtypeStruct((4,) + tile, f32)]
+    flows = []
+    if small:
+        vec, mod = totals.shape[2:], d_mod.shape[2:]
+        outs += [
+            jax.ShapeDtypeStruct(vec, f32),
+            jax.ShapeDtypeStruct((4, 2, 2, 2) + mod, bf16),
+        ]
+        flows = [
+            vmem((2,) + vec, f32),
+            vmem((2,) + vec, f32),
+            vmem((4, 2) + vec, f32),
+            vmem(vec, f32),
+            vmem((2,) + vec, f32),
+            vmem((2, 2) + mod, bf16),
+            vmem((2, 2) + mod, bf16),
+            vmem((2, 2, 2) + mod, bf16),
+        ]
+    return pl.pallas_call(
+        functools.partial(grad_kernel, small),
+        in_specs=[anywhere] * len(tensors) + [inside] * (2 if small else 0),
+        out_specs=[inside] * len(outs),
+        out_shape=outs,
+        scratch_shapes=flows
+        + [
+            vmem((count, width), bf16),
+            vmem((width, count), bf16),
+            vmem((2, count, width), bf16),
+            vmem((4, 2, 2, 4, 2) + tile, bf16),
+            vmem((4, 2, 4, 2) + tile, bf16),
+            vmem((4, 2, 4, 2) + tile, bf16),
+            vmem((4, 4, 2) + tile, bf16),
+            vmem((4, 4, 2) + tile, bf16),
+            vmem((4, 3, 2) + tile, bf16),
+            vmem((4, 2) + tile, f32),
+            vmem((4,) + tile, bf16),
+            vmem((4,) + tile, bf16),
+            pltpu.SemaphoreType.DMA((18,)),
+            pltpu.SemaphoreType.DMA((6, 6)),
+            pltpu.SemaphoreType.DMA((6, 6)),
+        ],
+        compiler_params=pltpu.CompilerParams(
+            vmem_limit_bytes=62 << 20, collective_id=1 if small else 3, has_side_effects=True
+        ),
+        cost_estimate=pl.CostEstimate(
+            flops=16 * count * width * width,
+            bytes_accessed=count * width * 12 + width * width * 8,
+            transcendentals=0,
+        ),
+        name="attn_grads" if small else "second_grads",
+    )(*tensors, *((totals, d_mod) if small else ()))
+
+
+class Sender:
+    def __init__(self, send_sems, recv_sems):
+        self.send_sems, self.recv_sems, self.copies = send_sems, recv_sems, []
+
+    def __call__(self, source, target, device):
+        used = len(self.copies)
+        copy = pltpu.make_async_remote_copy(
+            src_ref=source,
+            dst_ref=target,
+            send_sem=self.send_sems.at[used],
+            recv_sem=self.recv_sems.at[used],
+            device_id=device,
+            device_id_type=MESH,
+        )
+        copy.start()
+        self.copies.append(copy)
+        return copy
+
+    def finish(self):
+        for copy in self.copies:
+            copy.wait_send()
+
+
+START_COPIES = 41
+TURN = 640
+
+
+class Turner:
+    def __init__(self, source, target, held_in, held_out, sems, back=False):
+        self.source, self.target, self.back = source, target, back
+        self.held_in, self.held_out, self.sems = held_in, held_out, sems
+        self.total = source.shape[0 if back else 1] // TURN
+        self.done, self.loads, self.stores = 0, [], []
+        for _ in range(2):
+            self.load()
+
+    def slab(self, ref, index, by_rows):
+        span = pl.ds(index * TURN, TURN)
+        return ref.at[span] if by_rows else ref.at[:, span]
+
+    def load(self):
+        index = len(self.loads)
+        if index < self.total:
+            copy = pltpu.make_async_copy(
+                self.slab(self.source, index, self.back),
+                self.held_in.at[index % 2],
+                self.sems.at[index % 2],
+            )
+            copy.start()
+            self.loads.append(copy)
+
+    def run(self, steps):
+        for _ in range(min(steps, self.total - self.done)):
+            index = self.done
+            self.loads[index].wait()
+            if index >= 2:
+                self.stores[index - 2].wait()
+            self.held_out[index % 2] = self.held_in[index % 2].T
+            copy = pltpu.make_async_copy(
+                self.held_out.at[index % 2],
+                self.slab(self.target, index, not self.back),
+                self.sems.at[2 + index % 2],
+            )
+            copy.start()
+            self.stores.append(copy)
+            self.done += 1
+            self.load()
+
+    def finish(self):
+        self.run(self.total)
+        for copy in self.stores[-2:]:
+            copy.wait()
+
+
+def start_kernel(
+    tok_ref, shard_ref, grad_ref, soft_ref, vec_ref, ada_ref, bias_ref,
+    tok_out, parts_out, grad_out, mod_out, vec_out, soft_out,
+    s_col, x_send, x_rows, rows_in, partial, p_in, q_sum, z_in, y_send, n_y, k_send,
+    g_in, g_out, held,
+    send_sems, recv_sems, local_sems, g_sems,
+):
+    at = Place()
+    mine = at.y * 2 + at.k
+    turning = Turner(grad_ref, grad_out, g_in, g_out, g_sems)
+    own_load = pltpu.make_async_copy(tok_ref.at[mine], held.at[0], local_sems.at[0])
+    own_tokens = pltpu.make_async_copy(held.at[0], tok_out.at[mine], local_sems.at[2])
+    side_load = pltpu.make_async_copy(
+        tok_ref.at[at.y * 2 + 1 - at.k], held.at[1], local_sems.at[3]
+    )
+    own_shard = pltpu.make_async_copy(
+        shard_ref, parts_out.at[at.z, at.x, at.y, at.k], local_sems.at[1]
+    )
+    own_shard.start()
+    own_load.start()
+    side_load.start()
+    at.meet(at.other(y=1 - at.y, k=1 - at.k))
+    across = at.other(k=1 - at.k)
+    beside = at.other(x=1 - at.x)
+    over = at.other(y=1 - at.y)
+    ahead = [(at.z + step) % 4 for step in (1, 2, 3)]
+    send = Sender(send_sems, recv_sems)
+    length = tok_ref.shape[1] // 4
+    arrivals = []
+
+    def tokens_over(index):
+        span = pl.ds(index * length, length)
+        for k in (at.k, 1 - at.k):
+            source = tok_ref.at[(1 - at.y) * 2 + k, span]
+            arrivals.append(send(source, tok_out.at[mine, span], at.other(y=1 - at.y, k=k)))
+
+    zs, xs, ys = pl.ds(0, 4), pl.ds(0, 2), pl.ds(0, 2)
+
+    def forward(block, device):
+        return send(parts_out.at[block], parts_out.at[block], device)
+
+    def to_ahead(s):
+        return [forward((at.z, at.x, ys, at.k, s), at.other(z=z)) for z in ahead]
+
+    def all_in(copies):
+        for copy in copies:
+            copy.wait_recv()
+
+    shard_y = [
+        send(shard_ref.at[s], parts_out.at[at.z, at.x, at.y, at.k, s], over) for s in range(3)
+    ]
+    s_col[at.y, at.k] = soft_ref[...]
+    vec_out[at.y, at.k] = vec_ref[...]
+    soft_k = send(soft_ref, s_col.at[at.y, at.k], across)
+    vec_k = send(vec_ref, vec_out.at[at.y, at.k], across)
+    tokens_over(0)
+    soft_k.wait_recv()
+    vec_k.wait_recv()
+    soft_y = send(s_col.at[at.y], s_col.at[at.y], over)
+    vec_y = send(vec_out.at[at.y], vec_out.at[at.y], over)
+    own_shard.wait()
+    all_in(shard_y)
+    shard_z, shard_x, shard_k = [to_ahead(0)], [], []
+
+    def next_x(s):
+        all_in(shard_z[s])
+        shard_x.append(forward((zs, at.x, ys, at.k, s), beside))
+        if s < 2:
+            shard_z.append(to_ahead(s + 1))
+
+    def next_k(s):
+        shard_x[s].wait_recv()
+        shard_k.append(forward((zs, xs, ys, at.k, s), across))
+
+    own_load.wait()
+    own_tokens.start()
+    side_load.wait()
+    arrivals.append(send(held.at[1], tok_out.at[mine], across))
+    soft_y.wait_recv()
+    vec_y.wait_recv()
+    for z in range(4):
+        x_send[z] = s_col[z // 2, z % 2, 1 - at.x]
+        x_rows[at.x, z] = s_col[z // 2, z % 2, at.x]
+    soft_x = send(x_send, x_rows.at[at.x], beside)
+    tokens_over(1)
+    turning.run(1)
+    soft_x.wait_recv()
+    for x in range(2):
+        rows_in[at.z, x] = x_rows[x, at.z]
+    soft_z = [send(x_rows.at[xs, z], rows_in.at[at.z], at.other(z=z)) for z in ahead]
+    turning.run(2)
+    all_in(soft_z)
+    soft = jnp.concatenate([rows_in[r // 2, r % 2] for r in range(8)], axis=0)
+    soft_out[...] = soft
+    for part in range(6):
+        value = nn(soft, ada_ref[part])
+        for r in range(8):
+            partial[r % 2, r // 2, part] = value[r * 16 : (r + 1) * 16]
+    mod_x = send(partial.at[1 - at.x], p_in, beside)
+    tokens_over(2)
+    next_x(0)
+    turning.run(2)
+    mod_x.wait_recv()
+    for z in range(4):
+        for part in range(6):
+            q_sum[z, part] = partial[at.x, z, part] + p_in[z, part]
+    mod_z = [send(q_sum.at[z], z_in.at[at.z], at.other(z=z)) for z in ahead]
+    for part in range(6):
+        z_in[at.z, part] = q_sum[at.z, part]
+    turning.run(3)
+    next_x(1)
+    all_in(mod_z)
+    for part in range(6):
+        value = (z_in[0, part] + z_in[1, part]) + (z_in[2, part] + z_in[3, part])
+        value = value + bias_ref[part : part + 1]
+        for y in range(2):
+            y_send[y, part] = value[y * 8 : (y + 1) * 8]
+    mod_y = send(y_send.at[1 - at.y], n_y.at[at.y], over)
+    tokens_over(3)
+    for part in range(6):
+        n_y[at.y, part] = y_send[at.y, part]
+    next_k(0)
+    turning.run(2)
+    next_x(2)
+    mod_y.wait_recv()
+    for y in range(2):
+        for part in range(6):
+            for k in range(2):
+                k_send[k, y, part] = n_y[y, part, k * 4 : (k + 1) * 4]
+    mod_k = send(k_send.at[1 - at.k], mod_out.at[at.k], across)
+    for y in range(2):
+        for part in range(6):
+            mod_out[at.k, y, part] = k_send[at.k, y, part]
+    next_k(1)
+    turning.run(3)
+    next_k(2)
+    turning.finish()
+    mod_k.wait_recv()
+    all_in(arrivals)
+    all_in(shard_k)
+    own_tokens.wait()
+    send.finish()
+
+
+def start_everything(tok_pieces, shard, grad, soft, vec, w_ada, b_ada):
     f32, bf16 = jnp.float32, jnp.bfloat16
     anywhere = pl.BlockSpec(memory_space=pl.ANY)
     inside = pl.BlockSpec(memory_space=pltpu.VMEM)
-    images = d_mod.shape[2]
-    vec = totals.shape[2:]
-    tile = (128, 256)
+    six = (6, 16, 256)
+    vmem = pltpu.VMEM
     return pl.pallas_call(
-        attn_grad_kernel,
-        in_specs=[anywhere] * 4 + [inside] * 2,
-        out_specs=[inside] * 3,
+        start_kernel,
+        in_specs=[anywhere, inside, anywhere] + [inside] * 4,
+        out_specs=[anywhere, inside, anywhere] + [inside] * 3,
         out_shape=[
-            jax.ShapeDtypeStruct((4,) + tile, f32),
-            jax.ShapeDtypeStruct(vec, f32),
-            jax.ShapeDtypeStruct((4, 2, 2, 2) + d_mod.shape[2:], bf16),
+            jax.ShapeDtypeStruct(tok_pieces.shape, bf16),
+            jax.ShapeDtypeStruct((4, 2, 2, 2) + shard.shape, bf16),
+            jax.ShapeDtypeStruct(grad.shape[::-1], bf16),
+            jax.ShapeDtypeStruct((2, 2, 6, 4, 256), f32),
+            jax.ShapeDtypeStruct((2, 2) + vec.shape, f32),
+            jax.ShapeDtypeStruct((128, 128), bf16),
         ],
         scratch_shapes=[
-            pltpu.VMEM((count, width), bf16),
-            pltpu.VMEM((width, count), bf16),
-            pltpu.VMEM((2, count, width), bf16),
-            pltpu.VMEM((4, 2, 2, 4, 2) + tile, bf16),
-            pltpu.VMEM((4, 2, 4, 2) + tile, bf16),
-            pltpu.VMEM((4, 2, 4, 2) + tile, bf16),
-            pltpu.VMEM((4, 4, 2) + tile, bf16),
-            pltpu.VMEM((4, 4, 2) + tile, bf16),
-            pltpu.VMEM((4, 3, 2) + tile, bf16),
-            pltpu.VMEM((4, 2) + tile, f32),
-            pltpu.VMEM((4,) + tile, bf16),
-            pltpu.VMEM((4,) + tile, bf16),
-            pltpu.VMEM((2,) + vec, f32),
-            pltpu.VMEM((2,) + vec, f32),
-            pltpu.VMEM((4, 2) + vec, f32),
-            pltpu.VMEM(vec, f32),
-            pltpu.VMEM((2,) + vec, f32),
-            pltpu.VMEM((2, 2) + d_mod.shape[2:], bf16),
-            pltpu.VMEM((2, 2) + d_mod.shape[2:], bf16),
-            pltpu.VMEM((2, 2, 2) + d_mod.shape[2:], bf16),
-            pltpu.SemaphoreType.DMA((6,)),
-            pltpu.SemaphoreType.DMA((6, 6)),
-            pltpu.SemaphoreType.DMA((6, 6)),
+            vmem((2, 2) + soft.shape, bf16),
+            vmem((4, 16, 128), bf16),
+            vmem((2, 4, 16, 128), bf16),
+            vmem((4, 2, 16, 128), bf16),
+            vmem((2, 4) + six, f32),
+            vmem((4,) + six, f32),
+            vmem((4,) + six, f32),
+            vmem((4,) + six, f32),
+            vmem((2, 6, 8, 256), f32),
+            vmem((2, 6, 8, 256), f32),
+            vmem((2, 2, 6, 4, 256), f32),
+            vmem((2, grad.shape[0], TURN), bf16),
+            vmem((2, TURN, grad.shape[0]), bf16),
+            vmem((2,) + tok_pieces.shape[1:], bf16),
+            pltpu.SemaphoreType.DMA((START_COPIES,)),
+            pltpu.SemaphoreType.DMA((START_COPIES,)),
+            pltpu.SemaphoreType.DMA((4,)),
+            pltpu.SemaphoreType.DMA((4,)),
         ],
         compiler_params=pltpu.CompilerParams(
-            vmem_limit_bytes=62 << 20, collective_id=1, has_side_effects=True
+            vmem_limit_bytes=60 << 20, collective_id=2, has_side_effects=True
         ),
         cost_estimate=pl.CostEstimate(
-            flops=8 * count * width * width * 2,
-            bytes_accessed=count * width * 12 + width * width * 8,
-            transcendentals=0,
+            flops=100_000_000_000, bytes_accessed=30_000_000, transcendentals=0
         ),
-        name="attn_grads",
-    )(attended, d_one, ln_one, d_qkv, totals, d_mod)
+        name="start_exchange",
+    )(tok_pieces, shard, grad, soft, vec, w_ada, b_ada)
 
 
 def swap(pieces, axes):
@@ -861,11 +1147,10 @@
     block = w_proj.shape[0]
     ff_part = b_fc1.shape[0]
     hidden_width = ff_part * groups
-    aligned = part % 128 == 0
+    aligned = part == 256 and (rows, groups) == (8, 4)
     blocks = (rows, groups) if aligned else (1, 1)
     f32, bf16 = jnp.float32, jnp.bfloat16
 
-    qkv_parts = lax.all_gather(attention_triple_matrix.transpose(1, 0, 2), BOTH)
     rest_parts = lax.all_gather(
         row_major(jnp.concatenate([w_proj, w_fc1, w_fc2.T], axis=1)), BOTH
     )
@@ -879,7 +1164,39 @@
         pieces = wide.reshape(rows, block, groups, cols).transpose(0, 2, 1, 3)
         return pieces.reshape(everyone, block, cols)
 
-    if not aligned:
+    offsets = attention_triple_offset.astype(f32).reshape(-1)
+    vector = jnp.concatenate(
+        [offsets, b_proj.astype(f32), b_fc1.astype(f32), b_fc2.astype(f32), qk_gain]
+    )
+    ada_block = w_ada.shape[1]
+    cond_float = condition.astype(f32)
+    soft = jax.nn.silu(cond_float).astype(bf16)
+    def to_tokens(features):
+        pieces = swap(features.T.reshape(groups, count, part), "col")
+        return pieces if aligned else pieces.transpose(1, 0, 2).reshape(1, count, width)
+
+    def to_features(pieces):
+        if not aligned:
+            pieces = pieces[0].reshape(count, groups, part).transpose(1, 0, 2)
+        return swap(pieces, "col").reshape(groups * count, part)
+
+    if aligned:
+        held = vector.shape[0]
+        tok_in, qkv_parts, grad_in, modulation, small, soft_mine = start_everything(
+            tokens.T.reshape(groups, count, part),
+            attention_triple_matrix.transpose(1, 0, 2),
+            out_grad,
+            soft.reshape(images_row, 2, ada_block).transpose(1, 0, 2),
+            jnp.pad(vector, (0, -held % 1024)).reshape(-1, 128),
+            w_ada,
+            b_ada.astype(f32),
+        )
+        qkv_parts = qkv_parts.reshape(everyone, 3, block, part)
+        modulation = modulation.transpose(3, 2, 1, 0, 4).reshape(images, 6, width)
+        small = small.reshape(groups, -1)[:, :held]
+        grad_in = swap(grad_in.reshape(groups, count, part), "col")
+    else:
+        qkv_parts = lax.all_gather(attention_triple_matrix.transpose(1, 0, 2), BOTH)
         qkv_parts = jnp.stack([whole(qkv_parts[:, index]) for index in range(3)])[None]
         cut = part + ff_part
         rest_parts = jnp.concatenate(
@@ -891,14 +1208,28 @@
             axis=1,
         )[None]
 
-    offsets = attention_triple_offset.astype(f32).reshape(-1)
-    small = share(
-        jnp.concatenate(
-            [offsets, b_proj.astype(f32), b_fc1.astype(f32), b_fc2.astype(f32), qk_gain]
-        ),
-        "col",
-        groups,
-    )
+        small = share(vector, "col", groups)
+        soft_all = (
+            share(soft, BOTH, everyone)
+            .reshape(rows, groups, images_row, part)
+            .transpose(0, 2, 1, 3)
+            .reshape(rows * images_row, width)
+        )
+        soft_mine = lax.dynamic_slice(
+            soft_all, (0, row * ada_block), (rows * images_row, ada_block)
+        )
+        mod_part = jnp.einsum("ic,scd->isd", soft_mine, w_ada, preferred_element_type=f32)
+        mod_part = mod_part + jnp.where(row == 0, b_ada.astype(f32), 0.0)[None]
+        modulation = swap(mod_part.reshape(everyone, images, 6, part), BOTH)
+        modulation = (
+            modulation.reshape(rows, groups, images, 6, part)
+            .sum(axis=0)
+            .transpose(1, 2, 0, 3)
+            .reshape(images, 6, width)
+        )
+
+        tok_in = to_tokens(tokens)
+        grad_in = to_tokens(out_grad)
     cuts = [3 * part, 4 * part, 4 * part + ff_part, 5 * part + ff_part]
     bias_qkv = small[:, : cuts[0]].reshape(groups, 3, part).transpose(1, 0, 2).reshape(3, 1, width)
     bias_proj = small[:, cuts[0] : cuts[1]].reshape(1, width)
@@ -906,39 +1237,6 @@
     bias_two = small[:, cuts[2] : cuts[3]].reshape(1, width)
     gain_row = jnp.repeat(small[:, cuts[3] :].reshape(-1), HEAD_DIM)[None]
 
-    cond_float = condition.astype(f32)
-    soft = jax.nn.silu(cond_float).astype(bf16)
-    soft_all = (
-        share(soft, BOTH, everyone)
-        .reshape(rows, groups, images_row, part)
-        .transpose(0, 2, 1, 3)
-        .reshape(rows * images_row, width)
-    )
-    ada_block = w_ada.shape[1]
-    soft_mine = lax.dynamic_slice(
-        soft_all, (0, row * ada_block), (rows * images_row, ada_block)
-    )
-    mod_part = jnp.einsum("ic,scd->isd", soft_mine, w_ada, preferred_element_type=f32)
-    mod_part = mod_part + jnp.where(row == 0, b_ada.astype(f32), 0.0)[None]
-    modulation = swap(mod_part.reshape(everyone, images, 6, part), BOTH)
-    modulation = (
-        modulation.reshape(rows, groups, images, 6, part)
-        .sum(axis=0)
-        .transpose(1, 2, 0, 3)
-        .reshape(images, 6, width)
-    )
-
-    def to_tokens(features):
-        pieces = swap(features.T.reshape(groups, count, part), "col")
-        return pieces if aligned else pieces.transpose(1, 0, 2).reshape(1, count, width)
-
-    def to_features(pieces):
-        if not aligned:
-            pieces = pieces[0].reshape(count, groups, part).transpose(1, 0, 2)
-        return swap(pieces, "col").reshape(groups * count, part)
-
-    tok_in = to_tokens(tokens)
-    grad_in = to_tokens(out_grad)
     scale_rows = lax.dynamic_slice(scale_ids, (place * images, 0), (images, length))
     query_lanes, key_lanes = mask_lanes(scale_rows)
 
@@ -972,20 +1270,21 @@
         length,
     )
     layer_out = to_features(layer_pieces)
-    wide_ffn = ffn_grads(ln_two, d_pre, d_two, hidden, blocks)
     if aligned:
-        wide_ffn = wide_ffn.reshape(everyone, block, 2 * ff_part)
+        wide_one = plain_grads(ln_two, d_pre, blocks).reshape(everyone, block, ff_part)
+        wide_one, d_two = lax.optimization_barrier((wide_one, d_two))
     else:
-        wide_ffn = wide_ffn[0, 0]
-        wide_ffn = jnp.concatenate(
-            [spread(wide_ffn[:, :hidden_width]), spread(wide_ffn[:, hidden_width:])], axis=2
-        )
-    d_attended, wide_ffn = lax.optimization_barrier((d_attended, wide_ffn))
-    wide_ffn = row_major(lax.psum_scatter(wide_ffn, BOTH, scatter_dimension=0, tiled=False))
-    wide_ffn = wide_ffn.astype(f32)
-    grad_fc1 = wide_ffn[:, :ff_part]
-    grad_fc2 = wide_ffn[:, ff_part:].T
-
+        wide_one = spread(plain_grads(ln_two, d_pre, blocks)[0, 0])
+    wide_one = row_major(lax.psum_scatter(wide_one, BOTH, scatter_dimension=0, tiled=False))
+    grad_fc1 = wide_one.astype(f32)
+    if aligned:
+        (grad_fc2,) = grads_everywhere(count, width, (d_two, hidden))
+        grad_fc2 = grad_fc2.transpose(0, 2, 1).reshape(ff_part, block)
+        d_attended, grad_fc2 = lax.optimization_barrier((d_attended, grad_fc2))
+    else:
+        wide_two = spread(plain_grads(d_two, hidden, blocks)[0, 0])
+        wide_two = row_major(lax.psum_scatter(wide_two, BOTH, scatter_dimension=0, tiled=False))
+        grad_fc2 = wide_two.astype(f32).T
     d_qkv, head_totals = attention_backward(
         qkv,
         gain_row,
@@ -1020,8 +1319,8 @@
         totals = jnp.pad(totals, ((0, 0), (0, -held % 1024)))
         totals = totals.reshape(2, 2, -1, 128).transpose(1, 0, 2, 3)
         d_mod = d_mod.reshape(2, 2, images * 6, part).transpose(1, 0, 2, 3)
-        wide_attn, totals, d_mod = attn_grads_everywhere(
-            attn_rows, d_one, ln_one, d_qkv, totals, d_mod
+        wide_attn, totals, d_mod = grads_everywhere(
+            count, width, (attn_rows, d_one, ln_one, d_qkv), totals, d_mod
         )
         d_mod, grad_tokens = lax.optimization_barrier((d_mod, grad_tokens))
         totals = totals.reshape(-1)[:held]

time: 899 us -> 883 us (0.982)
  Pallas kernels: 637 us -> 774 us
  waiting for transfers between devices: 123 us -> 0.06 us
  local copies, waits for them, and re-layouts: 62.3 us -> 49.4 us
  starting transfers between devices: 39.2 us -> 30 us
    pallas_call x2 -> x4, Pallas kernels: 240 us -> 376 us  [the longest x2 227 us: grads_everywhere(): pl.pallas_call(functools.partial(grad_kernel, small), in_specs=[anywhere]...]
    all_to_all x8 -> x4, waiting for transfers between devices: 114 us -> 0.01 us  [swap(): lax.all_to_all(pieces, axes, split_axis=0, concat_axis=0, tiled=False)]
    all_to_all x8 -> x4, starting transfers between devices: 39.1 us -> 29.9 us  [swap(): lax.all_to_all(pieces, axes, split_axis=0, concat_axis=0, tiled=False)]
  transfers between devices with their start and end apart: 11 -> 6, of which waited for: 7 -> 0; matrix products, arithmetic and copies ran while one was open for 8% -> 6% of each run, Pallas kernels for 46% -> 66%
where the time goes in v3:
time: 883 us; the launch traced here: 879 us
  Pallas kernels  774 us (88%)
  local copies, waits for them, and re-layouts  49.4 us (6%)
  starting transfers between devices  30 us (3%)
  between operations  14.9 us (2%)
  other arithmetic  10.4 us (1%)
    pallas_call x2, Pallas kernels, grads_everywhere(): pl.pallas_call(functools.partial(grad_kernel, small), in_specs=[anywhere]...  227 us
    pallas_call x1, Pallas kernels, ffn(): pl.pallas_call(functools.partial(ffn_kernel, blocks, length, images), gri...  165 us
    pallas_call x1, Pallas kernels, start_everything(): pl.pallas_call(start_kernel, in_specs=[anywhere, inside, anywhere] + [ins...  117 us
    pallas_call x1, Pallas kernels, attention_backward(): pl.pallas_call(backward_kernel, grid=(images, width // PAIR), in_specs=in...  116 us
    pallas_call x1, Pallas kernels, attention_forward(): pl.pallas_call(forward_kernel, grid=(images, width // PAIR), in_specs=ins...  55.6 us
    pallas_call x1, Pallas kernels, input_backward(): pl.pallas_call(functools.partial(input_kernel, blocks, length, images), g...  33.7 us
    pallas_call x1, Pallas kernels, plain_grads(): pl.pallas_call(plain_grad_kernel, grid=(ff // span,), in_specs=[pl.BlockS...  31.4 us
    all_to_all x4, starting transfers between devices, swap(): lax.all_to_all(pieces, axes, split_axis=0, concat_axis=0, tiled=False)  29.9 us
  transfers between devices with their start and end apart: 6, of which 0 were waited for; matrix products, arithmetic and copies ran while one was open for 6% of the time, Pallas kernels for 66%

profile of v3, /device:TPU:0, one launch (start us, length us, event | category | flops | bytes accessed | tf_op | source)
XLA Modules:
  0.0 879.1 jit_solution(9159920107121192393)
XLA Ops:
  7.2 1.1 copy.72
  8.3 1.8 pad_maximum_fusion
  10.3 8.3 copy.68
  18.5 0.6 convert_element_type.45.bias_ref
  19.2 0.6 pad_bitcast_fusion.1.vec_ref
  19.8 0.6 bitcast_bitcast_fusion.soft_ref
  20.4 117.1 %start_exchange.1 = (bf16[4,2720,256]{2,1,0:T(8,128)(2,1)}, bf16[4,2,2,2,3,128,256]{6,5,4,3,2,1,0:T(8,128)(2,1)}, bf16[10880,256]{1,0:T(8,128)(2,1)}, f32[2,2,6,...) custom-call(bf16[4,2720,256]{2,1,0:T(8,128)(2,1)} %bitcast.116, ...), custom_call_target="tpu_custom_call" | custom-call | flops 99999997952 | bytes 30000000 | tf_op jit(solution)/shard_map/start_exchange/pallas_call | solution.py:1059
  137.6 5.2 all-to-all-start
  143.4 0.6 copy.90
  144.0 0.6 copy.91
  144.6 0.6 copy.92
  145.3 0.5 compare_convert_fusion.qm_ref
  145.8 0.5 select_convert_fusion.km_ref
  146.4 28.4 %qkv_forward.1 = (bf16[2720,1024]{1,0:T(8,128)(2,1)S(1)}, f32[3,2720,1024]{2,1,0:T(8,128)}) custom-call(bf16[4,2720,256]{2,1,0:T(8,128)(2,1)} %get-tuple-element.51.x_ref, f32[4,6,1024]{2,1,0:T(8,128)S(1)} %reshape.212.mod_ref, f32[3,1,1024]{2,1,0:T(1,128)S(1)} %reshape.177.bias_ref, bf16[32,3,128,256]{3,2,1,0:T(8,128)(2,1)} %bitcast.142), custom_call_target="tpu_custom_call" | custom-call | flops 17112760320 | bytes 50855936 | tf_op jit(solution)/shard_map/qkv_forward/pallas_call | solution.py:407
  174.9 2.4 copy-done.8
  177.3 55.6 %attention_forward.1 = (bf16[4,680,1024]{2,1,0:T(8,128)(2,1)}, f32[4,680,1024]{2,1,0:T(8,128)}) custom-call(f32[3,4,680,1024]{3,2,1,0:T(8,128)} %bitcast.104, f32[3,4,680,1024]{3,2,1,0:T(8,128)} %bitcast.105, f32[3,4,680,1024]{3,2,1,0:T(8,128)} %bitcast.106, f32[1,1024]{1,0:T(1,128)S(1)} %broadcast_in_dim_reshape.3.gain_ref, ...), custom_call_target="tpu_custom_call" | custom-call | flops 15151923200 | bytes 50135040 | tf_op jit(solution)/shard_map/attention_forward/pallas_call | solution.py:145
  232.9 164.9 %ffn_both.1 = (bf16[4,2720,256]{2,1,0:T(8,128)(2,1)}, bf16[2720,1024]{1,0:T(8,128)(2,1)}, bf16[2720,4096]{1,0:T(8,128)(2,1)}, bf16[2720,1024]{1,0:T(8,128)(2,1)}...) custom-call(bf16[4,2720,256]{2,1,0:T(8,128)(2,1)} %get-tuple-element, ...), custom_call_target="tpu_custom_call" | custom-call | flops 102676561920 | bytes 119144448 | tf_op jit(solution)/shard_map/ffn_both/pallas_call | solution.py:343
  397.7 31.4 %plain_grads.1 = bf16[8,4,128,1024]{3,2,1,0:T(8,128)(2,1)} custom-call(bf16[2720,1024]{1,0:T(8,128)(2,1)} %get-tuple-element.60.left, bf16[2720,4096]{1,0:T(8,128)(2,1)} %get-tuple-element.61.right), custom_call_target="tpu_custom_call" | custom-call | flops 22817013760 | bytes 36241408 | tf_op jit(solution)/shard_map/plain_grads/pallas_call | solution.py:519
  429.1 104.6 %second_grads.1 = f32[4,128,256]{2,1,0:T(8,128)} custom-call(bf16[2720,1024]{1,0:T(8,128)(2,1)} %get-tuple-element.63.refs_0_, bf16[2720,4096]{1,0:T(8,128)(2,1)} %get-tuple-element.64.refs_1_), custom_call_target="tpu_custom_call" | custom-call | flops 45634027520 | bytes 41811968 | tf_op jit(solution)/shard_map/second_grads/pallas_call | solution.py:800
  533.7 2.0 copy.74
  535.8 5.1 all-to-all-start.1
  540.9 115.5 %attention_backward.1 = (bf16[3,4,680,1024]{3,2,1,0:T(8,128)(2,1)}, f32[4,8,1024]{2,1,0:T(8,128)}) custom-call(f32[3,4,680,1024]{3,2,1,0:T(8,128)} %bitcast.107, f32[3,4,680,1024]{3,2,1,0:T(8,128)} %bitcast.108, f32[3,4,680,1024]{3,2,1,0:T(8,128)} %bitcast.109, f32[1,1024]{1,0:T(1,128)} %copy-done.7, bf16[4,680,128]{2,1,0:T(8,128)(2,1)} %copy-done.3, ...), custom_call_target="tpu_custom_call" | custom-call | flops 37879808000 | bytes 83558400 | tf_op jit(solution)/shard_map/attention_backward/pallas_call | solution.py:165
  656.5 0.9 reduce_sum.36
  657.9 0.7 reduce.13
  658.6 0.7 reduce.14
  659.3 0.7 reduce.15
  660.4 0.6 copy.103
  661.1 8.3 copy.75
  669.4 33.7 %input_backward.1 = (bf16[4,2720,256]{2,1,0:T(8,128)(2,1)S(1)}, f32[4,2,1024]{2,1,0:T(2,128)S(1)}) custom-call(bf16[3,2720,1024]{2,1,0:T(8,128)(2,1)} %bitcast.140, bf16[4,2720,256]{2,1,0:T(8,128)(2,1)} %get-tuple-element.51.x_ref, f32[2720,1024]{1,0:T(8,128)} %get-tuple-element.76.res_ref, f32[4,6,1024]{2,1,0:T(8,128)S(1)} %copy-done.6, ...), custom_call_target="tpu_custom_call" | custom-call | flops 17112760320 | bytes 45285376 | tf_op jit(solution)/shard_map/input_backward/pallas_call | solution.py:465
  703.1 2.4 copy-done.2
  705.6 0.6 copy.102
  706.3 5.3 all-to-all-start.2
  711.6 122.7 %attn_grads.1 = (f32[4,128,256]{2,1,0:T(8,128)}, f32[24,128]{1,0:T(8,128)}, bf16[4,2,2,2,24,256]{5,4,3,2,1,0:T(8,128)(2,1)}) custom-call(bf16[2720,1024]{1,0:T(8,128)(2,1)} %bitcast.138, bf16[2720,1024]{1,0:T(8,128)(2,1)} %get-tuple-element.69.refs_1_, bf16[2720,1024]{1,0:T(8,128)(2,1)} %copy-done.8, bf16[3,2720,1024]{2,1,0:T(8,128)(2,1)} %bitcast.141, ...), custom_call_target="tpu_custom_call" | custom-call | flops 45634027520 | bytes 41811968 | tf_op jit(solution)/shard_map/attn_grads/pallas_call | solution.py:800
  834.3 0.7 slice.75
  834.9 0.6 slice.76
  835.5 1.2 slice.92
  836.7 1.3 slice_bitcast_fusion.5
  838.0 1.6 slice_bitcast_fusion.1
  839.6 1.8 slice_bitcast_fusion
  841.3 1.1 reshape.200
  842.8 0.7 broadcast_in_dim.33
  843.6 14.2 %all-to-all-start.3 = ((f32[32,16,128]{2,1,0:T(8,128)}), f32[32,16,128]{2,1,0:T(8,128)S(1)}, u32[]{:S(2)}, u32[]{:S(2)}) async-start(f32[32,16,128]{2,1,0:T(8,128)} %bitcast.33), calls=%async_computation.3 | async-start | bytes 524288 | tf_op jit(solution)/shard_map/all_to_all | solution.py:1102
  857.8 1.3 slice_bitcast_fusion.6
  859.1 8.3 copy.79
  867.7 1.1 copy.83
  868.8 0.8 convert_reduce_fusion
  869.6 0.6 fusion.9
  870.3 1.8 bitcast_convert_fusion
  (107 shorter events, 2.5 us)
Async XLA Ops:
  7.2 138.1 %copy-start = (s32[16,680]{1,0:T(8,128)S(1)}, s32[16,680]{1,0:T(8,128)}, u32[]{:S(2)}) copy-start(s32[16,680]{1,0:T(8,128)} %param.17) | copy-start | bytes 130564
  7.2 225.7 %all-gather.3.cloned.1.call-start = ((), (), s32[]{:S(2)}) async-start(), calls=%async_computation.6 | async-start | bytes 19464192 | tf_op jit(solution)/shard_map/all_gather | solution.py:1154
  10.2 8.3 copy-start.20
  10.2 8.3 copy-start.17
  10.2 8.9 %copy-start.22 = (bf16[256]{0:T(256)(128)(2,1)S(1)}, bf16[256]{0:T(256)(128)(2,1)}, u32[]{:S(2)}) copy-start(bf16[256]{0:T(256)(128)(2,1)} %param.22) | copy-start | bytes 1540
  10.2 8.9 %copy-start.21 = (bf16[1024]{0:T(1024)(128)(2,1)S(1)}, bf16[1024]{0:T(1024)(128)(2,1)}, u32[]{:S(2)}) copy-start(bf16[1024]{0:T(1024)(128)(2,1)} %param.24) | copy-start | bytes 6148
  10.2 8.9 %copy-start.23 = (bf16[256]{0:T(256)(128)(2,1)S(1)}, bf16[256]{0:T(256)(128)(2,1)}, u32[]{:S(2)}) copy-start(bf16[256]{0:T(256)(128)(2,1)} %param.26) | copy-start | bytes 1540
  10.2 9.0 %copy-start.24 = (f32[4]{0:T(128)S(1)}, f32[4]{0:T(128)}, u32[]{:S(2)}) copy-start(f32[4]{0:T(128)} %param.20) | copy-start | bytes 52
  10.2 9.6 %copy-start.14 = (bf16[16,256]{1,0:T(8,128)(2,1)S(1)}, bf16[16,256]{1,0:T(8,128)(2,1)}, u32[]{:S(2)}) copy-start(bf16[16,256]{1,0:T(8,128)(2,1)} %param.16) | copy-start | bytes 24580
  137.6 5.3 copy-start.12
  137.6 5.4 copy-start.10
  137.6 95.3 %all-to-all-start = ((bf16[4,2720,256]{2,1,0:T(8,128)(2,1)}), bf16[4,2720,256]{2,1,0:T(8,128)(2,1)}, u32[]{:S(2)}, u32[]{:S(2)}) async-start(bf16[4,2720,256]{2,1,0:T(8,128)(2,1)} %bitcast.114), calls=%async_computation | async-start | bytes 11141120 | tf_op jit(solution)/shard_map/all_to_all | solution.py:1102
  142.8 727.4 %reduce-scatter.2.cloned.1.call-start = ((), (), s32[]{:S(2)}) async-start(), calls=%async_computation.5 | async-start | bytes 8650752 | tf_op jit(solution)/shard_map/reduce_scatter | solution.py:1278
  143.1 31.7 %copy-start.5 = (f32[4,6,1024]{2,1,0:T(8,128)}, f32[4,6,1024]{2,1,0:T(8,128)S(1)}, u32[]{:S(2)}) copy-start(f32[4,6,1024]{2,1,0:T(8,128)S(1)} %reshape.212.mod_ref) | copy-start | bytes 294916
  143.4 33.8 %copy-start.7 = (f32[1,1024]{1,0:T(1,128)}, f32[1,1024]{1,0:T(1,128)S(1)}, u32[]{:S(2)}) copy-start(f32[1,1024]{1,0:T(1,128)S(1)} %broadcast_in_dim_reshape.3.gain_ref) | copy-start | bytes 12292
  145.8 31.4 %copy-start.3 = (bf16[4,680,128]{2,1,0:T(8,128)(2,1)}, bf16[4,680,128]{2,1,0:T(8,128)(2,1)S(1)}, u32[]{:S(2)}) copy-start(bf16[4,680,128]{2,1,0:T(8,128)(2,1)S(1)} %compare_convert_fusion.qm_ref) | copy-start | bytes 2088964
  146.4 30.9 %copy-start.4 = (bf16[4,680,128]{2,1,0:T(8,128)(2,1)}, bf16[4,680,128]{2,1,0:T(8,128)(2,1)S(1)}, u32[]{:S(2)}) copy-start(bf16[4,680,128]{2,1,0:T(8,128)(2,1)S(1)} %select_convert_fusion.km_ref) | copy-start | bytes 2088964
  174.9 2.4 copy-start.8
  535.8 125.3 %all-to-all-start.1 = ((bf16[4,2720,256]{2,1,0:T(8,128)(2,1)}), bf16[4,2720,256]{2,1,0:T(8,128)(2,1)}, u32[]{:S(2)}, u32[]{:S(2)}) async-start(bf16[4,2720,256]{2,1,0:T(8,128)(2,1)} %get-tuple-element.67), calls=%async_computation.1 | async-start | bytes 11141120 | tf_op jit(solution)/shard_map/all_to_all | solution.py:1102
  540.9 117.0 %copy-start.19 = (f32[1,1024]{1,0:T(1,128)S(1)}, f32[1,1024]{1,0:T(1,128)}, u32[]{:S(2)}) copy-start(f32[1,1024]{1,0:T(1,128)} %get-tuple-element.73) | copy-start | bytes 12292
  540.9 117.7 %copy-start.16 = (f32[1,4096]{1,0:T(1,128)S(1)}, f32[1,4096]{1,0:T(1,128)}, u32[]{:S(2)}) copy-start(f32[1,4096]{1,0:T(1,128)} %get-tuple-element.74) | copy-start | bytes 49156
  540.9 118.4 %copy-start.18 = (f32[1,1024]{1,0:T(1,128)S(1)}, f32[1,1024]{1,0:T(1,128)}, u32[]{:S(2)}) copy-start(f32[1,1024]{1,0:T(1,128)} %get-tuple-element.75) | copy-start | bytes 12292
  540.9 120.1 %copy-start.11 = (f32[4,4,1024]{2,1,0:T(4,128)S(1)}, f32[4,4,1024]{2,1,0:T(4,128)}, u32[]{:S(2)}) copy-start(f32[4,4,1024]{2,1,0:T(4,128)} %get-tuple-element.78) | copy-start | bytes 196612
  661.1 8.3 copy-start.6
  703.1 2.4 copy-start.2
  706.3 135.1 %all-to-all-start.2 = ((bf16[4,2720,256]{2,1,0:T(8,128)(2,1)}), bf16[4,2720,256]{2,1,0:T(8,128)(2,1)}, u32[]{:S(2)}, u32[]{:S(2)}) async-start(bf16[4,2720,256]{2,1,0:T(8,128)(2,1)} %copy-done.2), calls=%async_computation.2 | async-start | bytes 11141120 | tf_op jit(solution)/shard_map/all_to_all | solution.py:1102
  711.6 131.0 %copy-start.9 = (bf16[6,128,256]{2,1,0:T(8,128)(2,1)S(1)}, bf16[6,128,256]{2,1,0:T(8,128)(2,1)}, u32[]{:S(2)}) copy-start(bf16[6,128,256]{2,1,0:T(8,128)(2,1)} %ada_ref.1) | copy-start | bytes 1179652
  843.6 26.0 %all-to-all-start.3 = ((f32[32,16,128]{2,1,0:T(8,128)}), f32[32,16,128]{2,1,0:T(8,128)S(1)}, u32[]{:S(2)}, u32[]{:S(2)}) async-start(f32[32,16,128]{2,1,0:T(8,128)} %bitcast.33), calls=%async_computation.3 | async-start | bytes 524288 | tf_op jit(solution)/shard_map/all_to_all | solution.py:1102
  857.8 14.3 %copy-start.1 = (s32[16,680]{1,0:T(8,128)S(1)}, s32[16,680]{1,0:T(8,128)}, u32[]{:S(2)}) copy-start(s32[16,680]{1,0:T(8,128)} %param.17) | copy-start | bytes 130564
  859.1 8.3 copy-start.13
  859.1 10.6 %copy-start.15 = (bf16[16,256]{1,0:T(8,128)(2,1)S(1)}, bf16[16,256]{1,0:T(8,128)(2,1)}, u32[]{:S(2)}) copy-start(bf16[16,256]{1,0:T(8,128)(2,1)} %param.16) | copy-start | bytes 24580
Sparse Core Ops, SparseCore 0:
  11.5 168.3 all-gather.2
  429.3 163.8 reduce-scatter.1

commit v4 on v3

--- a/solution.py
+++ b/solution.py
@@ -89,17 +89,16 @@
         return jnp.where(spot == FIRST_EXTRA + 2, lowest, base)
 
     qm = place(qm_ref[0], -lse_ref[0])
-    product = d_out.astype(jnp.float32) * o_ref[0].astype(jnp.float32)
-    first, second = head_sums(product, left)
-    dm = place(jnp.zeros_like(d_out), -jnp.where(left, second, first))
+    zero = jnp.zeros_like(d_out)
     k_turned = k_low.astype(jnp.float32).T.astype(jnp.bfloat16)
     d_v, d_k, d_q = [], [], []
     for head in range(2):
         mine = left if head == 0 else ~left
         probs = jnp.exp(nt(jnp.where(mine, k_low, km), jnp.where(mine, q_low, qm)))
         d_v.append(nn(probs.astype(jnp.bfloat16), d_out))
-        shifted = nt(jnp.where(mine, v_low, km), jnp.where(mine, d_out, dm))
-        d_scores = (probs * shifted).astype(jnp.bfloat16)
+        product = probs * nt(v_low, jnp.where(mine, d_out, zero))
+        expected = jnp.sum(product, axis=0, keepdims=True)
+        d_scores = (product - probs * expected).astype(jnp.bfloat16)
         d_k.append(nn(d_scores, q_low))
         d_q.append(nn(k_turned[head * HEAD_DIM : (head + 1) * HEAD_DIM], d_scores))
     d_q_low = jnp.concatenate(d_q, axis=0).T
@@ -184,13 +183,14 @@
 
 GELU_RATE = 0.7978845608
 GELU_CUBE = 0.7978845608 * 0.044715
-FFN_CHUNK = 512
-
-
-def tile_of(count, want):
+FFN_CHUNK = 1024
+
+
+def tile_of(count, length, want):
     best = 8
     for size in range(8, want + 1, 8):
-        if count % size == 0:
+        halves = size % 16 == 0 and length % (size // 2) == 0
+        if count % size == 0 and (length % size == 0 or halves):
             best = size
     return best
 
@@ -201,24 +201,19 @@
 
 class Images:
     def __init__(self, rows, length, images):
+        self.unit = rows if length % rows == 0 else rows // 2
         start = pl.program_id(0) * rows
-        self.first = start // length
-        self.second = jnp.minimum((start + rows - 1) // length, images - 1)
-        index = lax.broadcasted_iota(jnp.int32, (rows, 1), 0) + start
-        self.early = index < (self.first + 1) * length
-
-    def pick(self, table, which):
-        return jnp.where(
-            self.early,
-            table[self.first, which : which + 1],
-            table[self.second, which : which + 1],
-        )
-
-    def add(self, sums, which, value):
-        early = jnp.sum(jnp.where(self.early, value, 0.0), axis=0, keepdims=True)
-        late = jnp.sum(jnp.where(self.early, 0.0, value), axis=0, keepdims=True)
-        sums[self.first, which : which + 1] += early
-        sums[self.second, which : which + 1] += late
+        self.spans = [(first, first + self.unit) for first in range(0, rows, self.unit)]
+        self.which = [(start + first) // length for first, _ in self.spans]
+
+    def pick(self, table, column):
+        parts = [table[image, column : column + 1] for image in self.which]
+        shape = (self.unit, parts[0].shape[1])
+        return jnp.concatenate([jnp.broadcast_to(part, shape) for part in parts], axis=0)
+
+    def add(self, sums, column, value):
+        for image, (first, last) in zip(self.which, self.spans):
+            sums[image, column : column + 1] += jnp.sum(value[first:last], axis=0, keepdims=True)
 
 
 def standard_rows(value):
@@ -272,8 +267,6 @@
         sum_one_ref[...] = jnp.zeros_like(sum_one_ref)
         sum_two_ref[...] = jnp.zeros_like(sum_two_ref)
         wait_all(w_proj, sems.at[0])
-        wait_all(w_one, sems.at[1])
-        wait_all(w_two, sems.at[2])
 
     here = Images(rows, length, images)
     gate_attn = here.pick(mod_ref, 2)
@@ -283,6 +276,12 @@
     scale = 1.0 + here.pick(mod_ref, 4)
     ln_two = (normed * scale + here.pick(mod_ref, 3)).astype(jnp.bfloat16)
     ln_ref[...] = ln_two
+
+    @pl.when(first_step)
+    def _():
+        wait_all(w_one, sems.at[1])
+        wait_all(w_two, sems.at[2])
+
     branch_two = jnp.broadcast_to(bias_two_ref[...], residual.shape)
     for start in range(0, ff, FFN_CHUNK):
         span = slice(start, start + FFN_CHUNK)
@@ -328,7 +327,7 @@
     width = groups * part
     ff = bias_one.shape[1]
     images = modulation.shape[0]
-    rows = tile_of(count, 272)
+    rows = tile_of(count, length, 272)
     f32, bf16 = jnp.float32, jnp.bfloat16
     pieces = pl.BlockSpec((groups, rows, part), lambda i: (0, i, 0))
     wide = pl.BlockSpec((rows, width), lambda i: (i, 0))
@@ -403,7 +402,7 @@
     groups, count, part = x.shape
     width = groups * part
     images = modulation.shape[0]
-    rows = tile_of(count, 544)
+    rows = tile_of(count, length, 272)
     return pl.pallas_call(
         functools.partial(qkv_kernel, blocks, length, images),
         grid=(count // rows,),
@@ -460,7 +459,7 @@
     groups, count, part = x.shape
     width = groups * part
     images = modulation.shape[0]
-    rows = tile_of(count, 544)
+    rows = tile_of(count, length, 272)
     pieces = pl.BlockSpec((groups, rows, part), lambda i: (0, i, 0))
     return pl.pallas_call(
         functools.partial(input_kernel, blocks, length, images),
@@ -541,6 +540,67 @@
 MESH = pl.DeviceIdType.MESH
 
 
+TURN = 640
+
+
+class Turner:
+    def __init__(self, source, target, held_in, held_out, sems, back=False, shift=0, ahead=None):
+        self.source, self.target, self.back = source, target, back
+        self.held_in, self.held_out, self.sems = held_in, held_out, sems
+        self.total = source.shape[0 if back else 1] // TURN
+        self.done, self.settled, self.loads, self.stores, self.shift = 0, 0, [], [], shift
+        self.limit = self.total if ahead is None else ahead
+        for _ in range(2):
+            self.load()
+
+    def slab(self, ref, index, by_rows):
+        span = pl.ds(pl.multiple_of((index + self.shift) % self.total * TURN, TURN), TURN)
+        return ref.at[span] if by_rows else ref.at[:, span]
+
+    def load(self):
+        index = len(self.loads)
+        if index < min(self.limit, self.total):
+            copy = pltpu.make_async_copy(
+                self.slab(self.source, index, self.back),
+                self.held_in.at[index % 2],
+                self.sems.at[index % 2],
+            )
+            copy.start()
+            self.loads.append(copy)
+
+    def run(self, steps):
+        for _ in range(min(steps, self.total - self.done)):
+            index = self.done
+            self.loads[index].wait()
+            if index - 2 >= self.settled:
+                self.stores[index - 2].wait()
+                self.settled = index - 1
+            self.held_out[index % 2] = self.held_in[index % 2].T
+            copy = pltpu.make_async_copy(
+                self.held_out.at[index % 2],
+                self.slab(self.target, index, not self.back),
+                self.sems.at[2 + index % 2],
+            )
+            copy.start()
+            self.stores.append(copy)
+            self.done += 1
+            self.load()
+
+    def release(self):
+        self.limit = self.total
+        while len(self.loads) < min(self.done + 2, self.total):
+            self.load()
+
+    def settle(self):
+        for copy in self.stores[self.settled :]:
+            copy.wait()
+        self.settled = len(self.stores)
+
+    def finish(self):
+        self.run(self.total)
+        self.settle()
+
+
 class Place:
     def __init__(self):
         row = lax.axis_index("row")
@@ -566,6 +626,29 @@
         pl.semaphore_wait(barrier, len(partners))
 
 
+class Sender:
+    def __init__(self, send_sems, recv_sems):
+        self.send_sems, self.recv_sems, self.copies = send_sems, recv_sems, []
+
+    def __call__(self, source, target, device):
+        used = len(self.copies)
+        copy = pltpu.make_async_remote_copy(
+            src_ref=source,
+            dst_ref=target,
+            send_sem=self.send_sems.at[used],
+            recv_sem=self.recv_sems.at[used],
+            device_id=device,
+            device_id_type=MESH,
+        )
+        copy.start()
+        self.copies.append(copy)
+        return copy
+
+    def finish(self):
+        for copy in self.copies:
+            copy.wait_send()
+
+
 def add_into(target, first, second):
     for index in range(first.shape[0]):
         value = first[index].astype(jnp.float32) + second[index].astype(jnp.float32)
@@ -574,14 +657,17 @@
 
 def grad_kernel(small, *refs):
     if small:
-        att_ref, one_ref, ln_ref, d_ref, totals_ref, mod_ref = refs[:6]
-        out_ref, totals_out, mod_out = refs[6:9]
-        refs = refs[9:]
+        att_ref, one_ref, ln_ref, d_ref, tok_ref, layer_ref, totals_ref, mod_ref, ada_ref = refs[:9]
+        out_ref, totals_out, mod_out, soft_out, tok_in, tok_out, layer_out = refs[9:16]
+        refs = refs[16:]
+        g_own, g_z, g_x, g_turn, g_y, g_sum, g_k, soft_sems = refs[:8]
+        refs = refs[8:]
         t_core, t_x, t_z, t_y, t_sum, e_core, e_y, e_x = refs[:8]
+        turn_in, turn_out, turn_sems, more_sems = refs[8:12]
+        refs = refs[12:]
+    else:
+        two_ref, hidden_ref, two_left_ref, pre_ref, out_ref, wide_ref, stage, stage_sems = refs[:8]
         refs = refs[8:]
-    else:
-        two_ref, hidden_ref, out_ref = refs[:3]
-        refs = refs[3:]
     left, turned, right, mine, core_in, after_core, x_in, after_x = refs[:8]
     z_in, summed, y_send, y_in, load_sems, send_sems, recv_sems = refs[8:]
     at = Place()
@@ -595,6 +681,10 @@
         if small:
             source = one_ref if p == 0 else d_ref.at[p - 1]
             return [load(source, right.at[p % 2], 4 * p)]
+        if p >= 4:
+            width = right.shape[2]
+            source = pre_ref.at[:, pl.ds((p - 4) * width, width)]
+            return [load(source, right.at[p % 2], 16 + p)]
         part = hidden_ref.shape[1] // 4
         return [
             load(
@@ -605,9 +695,11 @@
             for c in range(4)
         ]
 
+    if small:
+        layer = Turner(layer_ref, layer_out, turn_in.at[0], turn_out.at[0], turn_sems.at[0], back=True)
     left_first = load(att_ref if small else two_ref, left, 16)
     rights = [load_right(0), load_right(1)]
-    at.meet()
+    at.meet(at.other(y=1 - at.y, k=1 - at.k))
     across = at.other(k=1 - at.k)
     beside = at.other(x=1 - at.x)
     over = at.other(y=1 - at.y)
@@ -678,19 +770,82 @@
         for copy in flights[5, 3]:
             copy.wait_recv()
 
+    soft_flights = []
+
+    def soft_send(source, target, device):
+        used = len(soft_flights)
+        copy = pltpu.make_async_remote_copy(
+            src_ref=source,
+            dst_ref=target,
+            send_sem=soft_sems.at[0, used],
+            recv_sem=soft_sems.at[1, used],
+            device_id=device,
+            device_id_type=MESH,
+        )
+        copy.start()
+        sent.append(copy)
+        soft_flights.append(copy)
+
+    def soft_one():
+        share = jnp.zeros((128, 128), jnp.float32)
+        for part in range(6):
+            rows = []
+            for r in range(8):
+                for c in range(4):
+                    rows.append(mod_out[r // 2, r % 2, c // 2, c % 2, part * 4 : part * 4 + 4])
+            share = share + nt(jnp.concatenate(rows, axis=0), ada_ref[part])
+        for r in range(8):
+            g_own[r // 2, r % 2] = share[r * 16 : (r + 1) * 16]
+        for z in ahead:
+            soft_send(g_own.at[z], g_z.at[at.z], at.other(z=z))
+        for x in range(2):
+            g_z[at.z, x] = g_own[at.z, x]
+
+    def soft_two():
+        for copy in soft_flights[:3]:
+            copy.wait_recv()
+        for z in range(4):
+            g_x[at.x, z] = g_z[z, at.x]
+        soft_send(g_z.at[pl.ds(0, 4), 1 - at.x], g_x.at[at.x], beside)
+
+    def soft_three():
+        soft_flights[3].wait_recv()
+        for z in range(4):
+            for x in range(2):
+                g_turn[z // 2, z % 2, x] = g_x[x, z]
+        soft_send(g_turn.at[1 - at.y], g_y, over)
+
+    def soft_four():
+        soft_flights[4].wait_recv()
+        for k in range(2):
+            for x in range(2):
+                g_sum[k, x] = g_turn[at.y, k, x] + g_y[k, x]
+        soft_send(g_sum.at[1 - at.k], g_k, across)
+
+    def soft_five():
+        soft_flights[5].wait_recv()
+        for x in range(2):
+            soft_out[x] = g_sum[at.k, x] + g_k[x]
+
     def compute(p):
         for c in range(4):
             span = slice(c * 256, (c + 1) * 256)
             value = nn(turned[...], right[p % 2, :, span]).astype(jnp.bfloat16)
             for r in range(8):
-                mine[p, c % 2, r % 2, r // 2, c // 2] = value[r * 128 : (r + 1) * 128]
+                z, x, y = r // 2, r % 2, c // 2
+                where = (x, z, y) if small else ((x, y, z), (y, x, z))[p % 2]
+                mine[(p, c % 2) + where] = value[r * 128 : (r + 1) * 128]
         flights[p, 0] = send(p, 0, mine.at[p, 1 - at.k], core_in.at[p], across)
 
     def core_done(p):
         flights[p, 0].wait_recv()
-        for x in range(2):
-            for z in range(4):
-                add_into(after_core.at[p, x, z], mine.at[p, at.k, x, z], core_in.at[p, x, z])
+        for one in range(mine.shape[2]):
+            for two in range(mine.shape[3]):
+                add_into(
+                    after_core.at[p, one, two],
+                    mine.at[p, at.k, one, two],
+                    core_in.at[p, one, two],
+                )
 
     def x_start(p):
         flights[p, 1] = send(p, 1, after_core.at[p, 1 - at.x], x_in.at[p], beside)
@@ -719,75 +874,247 @@
         flights[p, 3].wait_recv()
         out_ref[p] = summed[p, at.y] + y_in[p].astype(jnp.float32)
 
+    def axes(p):
+        return ((at.x, beside), (at.y, over))[:: 1 if p % 2 == 0 else -1]
+
+    def first_start(p):
+        place, partner = axes(p)[0]
+        flights[p, 1] = send(p, 1, after_core.at[p, 1 - place], x_in.at[p], partner)
+
+    def first_done(p):
+        flights[p, 1].wait_recv()
+        for index in range(2):
+            add_into(after_x.at[p, index], after_core.at[p, axes(p)[0][0], index], x_in.at[p, index])
+        place, partner = axes(p)[1]
+        flights[p, 2] = send(p, 2, after_x.at[p, 1 - place], y_in.at[p], partner)
+
+    def second_done(p):
+        flights[p, 2].wait_recv()
+        add_into(y_send.at[p], after_x.at[p, axes(p)[1][0]], y_in.at[p])
+        flights[p, 3] = [
+            send(p, 3 + index, y_send.at[p, z], z_in.at[p, index], at.other(z=z))
+            for index, z in enumerate(ahead)
+        ]
+
+    def third_done(p):
+        for copy in flights[p, 3]:
+            copy.wait_recv()
+        value = y_send[p, at.z].astype(jnp.float32)
+        for index in range(3):
+            value = value + z_in[p, index].astype(jnp.float32)
+        out_ref[p] = value
+
+    arrivals = []
+
+    def tokens_from(c, index):
+        length = tok_ref.shape[1] // 4
+        here = pl.ds(index * length, length)
+        there = pl.ds(pl.multiple_of((at.y * 2 + at.k) * tok_ref.shape[1] + index * length, 8), length)
+        return tok_ref.at[c, here], tok_in.at[there]
+
+    def tokens_over(index):
+        for step, k in enumerate((at.k, 1 - at.k)):
+            source, target = tokens_from((1 - at.y) * 2 + k, index)
+            copy = pltpu.make_async_remote_copy(
+                src_ref=source,
+                dst_ref=target,
+                send_sem=more_sems.at[0, 2 * index + step],
+                recv_sem=more_sems.at[1, 2 * index + step],
+                device_id=at.other(y=1 - at.y, k=k),
+                device_id_type=MESH,
+            )
+            copy.start()
+            arrivals.append(copy)
+            sent.append(copy)
+
+    def tokens_across():
+        count = tok_ref.shape[1]
+        copy = pltpu.make_async_remote_copy(
+            src_ref=tok_ref.at[at.y * 2 + 1 - at.k],
+            dst_ref=tok_in.at[pl.ds(pl.multiple_of((at.y * 2 + at.k) * count, 8), count)],
+            send_sem=more_sems.at[0, 8],
+            recv_sem=more_sems.at[1, 8],
+            device_id=across,
+            device_id_type=MESH,
+        )
+        copy.start()
+        sent.append(copy)
+        return copy
+
+    def own_tokens():
+        count = tok_ref.shape[1]
+        held = left.at[:, pl.ds(0, tok_ref.shape[2])]
+        load(tok_ref.at[at.y * 2 + at.k], held, 18).wait()
+        place = pl.ds(pl.multiple_of((at.y * 2 + at.k) * count, 8), count)
+        load(held, tok_in.at[place], 19).wait()
+
     def right_ready(p):
         for copy in rights[p]:
             copy.wait()
 
-    hops = [small_zero, small_one, small_two, small_three, small_four]
-    if not small:
-        hops = [lambda: None] * 5
-    hops[0]()
+    writes = []
+
+    def plain(c):
+        right_ready(4 + c)
+        if c >= 2:
+            writes[c - 2].wait()
+        for part in range(4):
+            span = slice(part * 256, (part + 1) * 256)
+            value = nn(turned[...], right[c % 2, :, span]).astype(jnp.bfloat16)
+            for r in range(8):
+                stage[c % 2, r, :, span] = value[r * 128 : (r + 1) * 128]
+        copy = pltpu.make_async_copy(stage.at[c % 2], wide_ref.at[:, c], stage_sems.at[c % 2])
+        copy.start()
+        writes.append(copy)
+        if c < 2:
+            rights.append(load_right(6 + c))
+
     left_first.wait()
-    turn_rows(left, turned)
     if small:
+        small_zero()
+        from_across = tokens_across()
+        tokens_over(0)
+        turn_rows(left, turned)
         left_second = load(ln_ref, left, 17)
-    right_ready(0)
-    compute(0)
-    rights.append(load_right(2))
-    hops[1]()
-    core_done(0)
-    x_start(0)
-    if small:
+        right_ready(0)
+        compute(0)
+        rights.append(load_right(2))
+        small_one()
+        tokens_over(1)
+        core_done(0)
+        x_start(0)
+        layer.run(4)
         left_second.wait()
         turn_rows(left, turned)
-    right_ready(1)
-    compute(1)
-    rights.append(load_right(3))
-    core_done(1)
-    hops[2]()
-    x_done(0)
-    x_start(1)
-    right_ready(2)
-    compute(2)
-    core_done(2)
-    hops[3]()
-    x_done(1)
-    x_start(2)
-    z_done(0)
-    right_ready(3)
-    compute(3)
-    core_done(3)
-    hops[4]()
-    x_done(2)
-    x_start(3)
-    z_done(1)
-    y_done(0)
-    z_done(2)
-    y_done(1)
-    x_done(3)
-    y_done(2)
-    z_done(3)
-    y_done(3)
+        right_ready(1)
+        compute(1)
+        rights.append(load_right(3))
+        core_done(1)
+        small_two()
+        x_done(0)
+        x_start(1)
+        tokens_over(2)
+        layer.run(4)
+        own_tokens()
+        from_across.wait_recv()
+        right_ready(2)
+        compute(2)
+        core_done(2)
+        small_three()
+        x_done(1)
+        x_start(2)
+        tokens_over(3)
+        z_done(0)
+        right_ready(3)
+        compute(3)
+        core_done(3)
+        small_four()
+        soft_one()
+        x_done(2)
+        x_start(3)
+        layer.run(5)
+        soft_two()
+        layer.run(4)
+        soft_three()
+        half = layer.total // 2
+        turned_tokens = Turner(
+            tok_in, tok_out, turn_in.at[1], turn_out.at[1], turn_sems.at[1],
+            back=True, shift=at.y * (half + 1), ahead=half,
+        )
+        z_done(1)
+        y_done(0)
+        turned_tokens.run(half)
+        soft_four()
+        z_done(2)
+        y_done(1)
+        for copy in arrivals:
+            copy.wait_recv()
+        turned_tokens.release()
+        soft_five()
+        x_done(3)
+        turned_tokens.finish()
+        layer.finish()
+        y_done(2)
+        z_done(3)
+        y_done(3)
+    else:
+        turn_rows(left, turned)
+        left_second = load(two_left_ref, left, 17)
+        right_ready(0)
+        compute(0)
+        rights.append(load_right(2))
+        core_done(0)
+        first_start(0)
+        right_ready(1)
+        compute(1)
+        rights.append(load_right(3))
+        core_done(1)
+        first_start(1)
+        right_ready(2)
+        compute(2)
+        rights.append(load_right(4))
+        core_done(2)
+        first_done(0)
+        first_start(2)
+        first_done(1)
+        right_ready(3)
+        compute(3)
+        rights.append(load_right(5))
+        core_done(3)
+        first_start(3)
+        left_second.wait()
+        turn_rows(left, turned)
+        second_done(0)
+        second_done(1)
+        plain(0)
+        first_done(2)
+        third_done(0)
+        plain(1)
+        third_done(1)
+        first_done(3)
+        second_done(2)
+        plain(2)
+        second_done(3)
+        third_done(2)
+        plain(3)
+        third_done(3)
+        writes[2].wait()
+        writes[3].wait()
     for copy in sent:
         copy.wait_send()
 
 
-def grads_everywhere(count, width, tensors, totals=None, d_mod=None):
+def grads_everywhere(count, width, tensors, pieces=None, layer=None, totals=None, d_mod=None, w_ada=None):
     f32, bf16 = jnp.float32, jnp.bfloat16
     small = totals is not None
     anywhere = pl.BlockSpec(memory_space=pl.ANY)
     inside = pl.BlockSpec(memory_space=pltpu.VMEM)
     tile = (128, 256)
+    cube = (2, 4, 2) if small else (2, 2, 4)
     vmem = pltpu.VMEM
     outs = [jax.ShapeDtypeStruct((4,) + tile, f32)]
-    flows = []
-    if small:
+    flows = [vmem((2, 8, 128, width), bf16), pltpu.SemaphoreType.DMA((2,))]
+    if not small:
+        outs += [jax.ShapeDtypeStruct((8, 4, 128, width), bf16)]
+    else:
         vec, mod = totals.shape[2:], d_mod.shape[2:]
         outs += [
             jax.ShapeDtypeStruct(vec, f32),
             jax.ShapeDtypeStruct((4, 2, 2, 2) + mod, bf16),
+            jax.ShapeDtypeStruct((2, 16, 128), f32),
+            jax.ShapeDtypeStruct(layer.shape, bf16),
+            jax.ShapeDtypeStruct(layer.shape[::-1], bf16),
+            jax.ShapeDtypeStruct(layer.shape[::-1], bf16),
         ]
         flows = [
+            vmem((4, 2, 16, 128), f32),
+            vmem((4, 2, 16, 128), f32),
+            vmem((2, 4, 16, 128), f32),
+            vmem((2, 2, 2, 16, 128), f32),
+            vmem((2, 2, 16, 128), f32),
+            vmem((2, 2, 16, 128), f32),
+            vmem((2, 16, 128), f32),
+            pltpu.SemaphoreType.DMA((2, 6)),
             vmem((2,) + vec, f32),
             vmem((2,) + vec, f32),
             vmem((4, 2) + vec, f32),
@@ -796,27 +1123,31 @@
             vmem((2, 2) + mod, bf16),
             vmem((2, 2) + mod, bf16),
             vmem((2, 2, 2) + mod, bf16),
+            vmem((2, 2, TURN, layer.shape[1]), bf16),
+            vmem((2, 2, layer.shape[1], TURN), bf16),
+            pltpu.SemaphoreType.DMA((2, 4)),
+            pltpu.SemaphoreType.DMA((2, 9)),
         ]
     return pl.pallas_call(
         functools.partial(grad_kernel, small),
-        in_specs=[anywhere] * len(tensors) + [inside] * (2 if small else 0),
-        out_specs=[inside] * len(outs),
+        in_specs=[anywhere] * (len(tensors) + 2 * small) + [inside] * (3 * small),
+        out_specs=[inside] * (4 if small else 1) + [anywhere] * (3 if small else 1),
         out_shape=outs,
         scratch_shapes=flows
         + [
             vmem((count, width), bf16),
             vmem((width, count), bf16),
             vmem((2, count, width), bf16),
-            vmem((4, 2, 2, 4, 2) + tile, bf16),
-            vmem((4, 2, 4, 2) + tile, bf16),
-            vmem((4, 2, 4, 2) + tile, bf16),
-            vmem((4, 4, 2) + tile, bf16),
-            vmem((4, 4, 2) + tile, bf16),
-            vmem((4, 3, 2) + tile, bf16),
-            vmem((4, 2) + tile, f32),
-            vmem((4,) + tile, bf16),
-            vmem((4,) + tile, bf16),
-            pltpu.SemaphoreType.DMA((18,)),
+            vmem((4, 2) + cube + tile, bf16),
+            vmem((4,) + cube + tile, bf16),
+            vmem((4,) + cube + tile, bf16),
+            vmem((4,) + cube[1:] + tile, bf16),
+            vmem((4,) + cube[1:] + tile, bf16),
+            vmem((4, 3) + ((2,) if small else ()) + tile, bf16),
+            vmem((4, 2 if small else 1) + tile, f32),
+            vmem((4,) + (() if small else (4,)) + tile, bf16),
+            vmem((4,) + (() if small else (4,)) + tile, bf16),
+            pltpu.SemaphoreType.DMA((24,)),
             pltpu.SemaphoreType.DMA((6, 6)),
             pltpu.SemaphoreType.DMA((6, 6)),
         ],
@@ -829,117 +1160,52 @@
             transcendentals=0,
         ),
         name="attn_grads" if small else "second_grads",
-    )(*tensors, *((totals, d_mod) if small else ()))
-
-
-class Sender:
-    def __init__(self, send_sems, recv_sems):
-        self.send_sems, self.recv_sems, self.copies = send_sems, recv_sems, []
-
-    def __call__(self, source, target, device):
-        used = len(self.copies)
-        copy = pltpu.make_async_remote_copy(
-            src_ref=source,
-            dst_ref=target,
-            send_sem=self.send_sems.at[used],
-            recv_sem=self.recv_sems.at[used],
-            device_id=device,
-            device_id_type=MESH,
-        )
-        copy.start()
-        self.copies.append(copy)
-        return copy
-
-    def finish(self):
-        for copy in self.copies:
-            copy.wait_send()
+    )(*tensors, *((pieces, layer, totals, d_mod, w_ada) if small else ()))
 
 
 START_COPIES = 41
-TURN = 640
-
-
-class Turner:
-    def __init__(self, source, target, held_in, held_out, sems, back=False):
-        self.source, self.target, self.back = source, target, back
-        self.held_in, self.held_out, self.sems = held_in, held_out, sems
-        self.total = source.shape[0 if back else 1] // TURN
-        self.done, self.loads, self.stores = 0, [], []
-        for _ in range(2):
-            self.load()
-
-    def slab(self, ref, index, by_rows):
-        span = pl.ds(index * TURN, TURN)
-        return ref.at[span] if by_rows else ref.at[:, span]
-
-    def load(self):
-        index = len(self.loads)
-        if index < self.total:
-            copy = pltpu.make_async_copy(
-                self.slab(self.source, index, self.back),
-                self.held_in.at[index % 2],
-                self.sems.at[index % 2],
-            )
-            copy.start()
-            self.loads.append(copy)
-
-    def run(self, steps):
-        for _ in range(min(steps, self.total - self.done)):
-            index = self.done
-            self.loads[index].wait()
-            if index >= 2:
-                self.stores[index - 2].wait()
-            self.held_out[index % 2] = self.held_in[index % 2].T
-            copy = pltpu.make_async_copy(
-                self.held_out.at[index % 2],
-                self.slab(self.target, index, not self.back),
-                self.sems.at[2 + index % 2],
-            )
-            copy.start()
-            self.stores.append(copy)
-            self.done += 1
-            self.load()
-
-    def finish(self):
-        self.run(self.total)
-        for copy in self.stores[-2:]:
-            copy.wait()
 
 
 def start_kernel(
     tok_ref, shard_ref, grad_ref, soft_ref, vec_ref, ada_ref, bias_ref,
-    tok_out, parts_out, grad_out, mod_out, vec_out, soft_out,
+    tok_out, parts_out, grad_out, tok_turned, mod_out, vec_out, soft_out,
     s_col, x_send, x_rows, rows_in, partial, p_in, q_sum, z_in, y_send, n_y, k_send,
-    g_in, g_out, held,
-    send_sems, recv_sems, local_sems, g_sems,
+    t_in, t_out, g_in, g_out, held,
+    send_sems, recv_sems, local_sems, t_sems, g_sems,
 ):
     at = Place()
     mine = at.y * 2 + at.k
     turning = Turner(grad_ref, grad_out, g_in, g_out, g_sems)
-    own_load = pltpu.make_async_copy(tok_ref.at[mine], held.at[0], local_sems.at[0])
+    count = tok_turned.shape[0] // 4
+
+    def piece(c, start, size):
+        return tok_turned.at[pl.ds(pl.multiple_of(c * count + start, 8), size)]
+
+    own_load = pltpu.make_async_copy(piece(mine, 0, count), held.at[0], local_sems.at[0])
     own_tokens = pltpu.make_async_copy(held.at[0], tok_out.at[mine], local_sems.at[2])
     side_load = pltpu.make_async_copy(
-        tok_ref.at[at.y * 2 + 1 - at.k], held.at[1], local_sems.at[3]
+        piece(at.y * 2 + 1 - at.k, 0, count), held.at[1], local_sems.at[3]
     )
     own_shard = pltpu.make_async_copy(
         shard_ref, parts_out.at[at.z, at.x, at.y, at.k], local_sems.at[1]
     )
     own_shard.start()
-    own_load.start()
-    side_load.start()
+    first = Turner(
+        tok_ref, tok_turned, t_in, t_out, t_sems, shift=(1 - at.y) * (tok_ref.shape[1] // TURN // 2)
+    )
     at.meet(at.other(y=1 - at.y, k=1 - at.k))
     across = at.other(k=1 - at.k)
     beside = at.other(x=1 - at.x)
     over = at.other(y=1 - at.y)
     ahead = [(at.z + step) % 4 for step in (1, 2, 3)]
     send = Sender(send_sems, recv_sems)
-    length = tok_ref.shape[1] // 4
+    length = count // 4
     arrivals = []
 
     def tokens_over(index):
         span = pl.ds(index * length, length)
         for k in (at.k, 1 - at.k):
-            source = tok_ref.at[(1 - at.y) * 2 + k, span]
+            source = piece((1 - at.y) * 2 + k, index * length, length)
             arrivals.append(send(source, tok_out.at[mine, span], at.other(y=1 - at.y, k=k)))
 
     zs, xs, ys = pl.ds(0, 4), pl.ds(0, 2), pl.ds(0, 2)
@@ -961,6 +1227,8 @@
     vec_out[at.y, at.k] = vec_ref[...]
     soft_k = send(soft_ref, s_col.at[at.y, at.k], across)
     vec_k = send(vec_ref, vec_out.at[at.y, at.k], across)
+    first.run(9)
+    first.settle()
     tokens_over(0)
     soft_k.wait_recv()
     vec_k.wait_recv()
@@ -980,6 +1248,9 @@
         shard_x[s].wait_recv()
         shard_k.append(forward((zs, xs, ys, at.k, s), across))
 
+    first.finish()
+    own_load.start()
+    side_load.start()
     own_load.wait()
     own_tokens.start()
     side_load.wait()
@@ -1050,7 +1321,7 @@
     send.finish()
 
 
-def start_everything(tok_pieces, shard, grad, soft, vec, w_ada, b_ada):
+def start_everything(tokens, shard, grad, soft, vec, w_ada, b_ada):
     f32, bf16 = jnp.float32, jnp.bfloat16
     anywhere = pl.BlockSpec(memory_space=pl.ANY)
     inside = pl.BlockSpec(memory_space=pltpu.VMEM)
@@ -1059,11 +1330,12 @@
     return pl.pallas_call(
         start_kernel,
         in_specs=[anywhere, inside, anywhere] + [inside] * 4,
-        out_specs=[anywhere, inside, anywhere] + [inside] * 3,
+        out_specs=[anywhere, inside, anywhere, anywhere] + [inside] * 3,
         out_shape=[
-            jax.ShapeDtypeStruct(tok_pieces.shape, bf16),
+            jax.ShapeDtypeStruct((4, tokens.shape[1] // 4, tokens.shape[0]), bf16),
             jax.ShapeDtypeStruct((4, 2, 2, 2) + shard.shape, bf16),
             jax.ShapeDtypeStruct(grad.shape[::-1], bf16),
+            jax.ShapeDtypeStruct(tokens.shape[::-1], bf16),
             jax.ShapeDtypeStruct((2, 2, 6, 4, 256), f32),
             jax.ShapeDtypeStruct((2, 2) + vec.shape, f32),
             jax.ShapeDtypeStruct((128, 128), bf16),
@@ -1080,11 +1352,14 @@
             vmem((2, 6, 8, 256), f32),
             vmem((2, 6, 8, 256), f32),
             vmem((2, 2, 6, 4, 256), f32),
+            vmem((2, tokens.shape[0], TURN), bf16),
+            vmem((2, TURN, tokens.shape[0]), bf16),
             vmem((2, grad.shape[0], TURN), bf16),
             vmem((2, TURN, grad.shape[0]), bf16),
-            vmem((2,) + tok_pieces.shape[1:], bf16),
+            vmem((2, tokens.shape[1] // 4, tokens.shape[0]), bf16),
             pltpu.SemaphoreType.DMA((START_COPIES,)),
             pltpu.SemaphoreType.DMA((START_COPIES,)),
+            pltpu.SemaphoreType.DMA((4,)),
             pltpu.SemaphoreType.DMA((4,)),
             pltpu.SemaphoreType.DMA((4,)),
         ],
@@ -1095,7 +1370,7 @@
             flops=100_000_000_000, bytes_accessed=30_000_000, transcendentals=0
         ),
         name="start_exchange",
-    )(tok_pieces, shard, grad, soft, vec, w_ada, b_ada)
+    )(tokens, shard, grad, soft, vec, w_ada, b_ada)
 
 
 def swap(pieces, axes):
@@ -1182,8 +1457,8 @@
 
     if aligned:
         held = vector.shape[0]
-        tok_in, qkv_parts, grad_in, modulation, small, soft_mine = start_everything(
-            tokens.T.reshape(groups, count, part),
+        tok_in, qkv_parts, grad_in, _, modulation, small, soft_mine = start_everything(
+            tokens,
             attention_triple_matrix.transpose(1, 0, 2),
             out_grad,
             soft.reshape(images_row, 2, ada_block).transpose(1, 0, 2),
@@ -1269,22 +1544,21 @@
         blocks,
         length,
     )
-    layer_out = to_features(layer_pieces)
     if aligned:
-        wide_one = plain_grads(ln_two, d_pre, blocks).reshape(everyone, block, ff_part)
-        wide_one, d_two = lax.optimization_barrier((wide_one, d_two))
+        grad_fc2, wide_one = grads_everywhere(count, width, (d_two, hidden, ln_two, d_pre))
+        grad_fc2 = grad_fc2.transpose(0, 2, 1).reshape(ff_part, block)
+        wide_one = wide_one.reshape(everyone, block, ff_part)
+        wide_one, d_attended, layer_pieces = lax.optimization_barrier(
+            (wide_one, d_attended, layer_pieces)
+        )
     else:
         wide_one = spread(plain_grads(ln_two, d_pre, blocks)[0, 0])
-    wide_one = row_major(lax.psum_scatter(wide_one, BOTH, scatter_dimension=0, tiled=False))
-    grad_fc1 = wide_one.astype(f32)
-    if aligned:
-        (grad_fc2,) = grads_everywhere(count, width, (d_two, hidden))
-        grad_fc2 = grad_fc2.transpose(0, 2, 1).reshape(ff_part, block)
-        d_attended, grad_fc2 = lax.optimization_barrier((d_attended, grad_fc2))
-    else:
         wide_two = spread(plain_grads(d_two, hidden, blocks)[0, 0])
         wide_two = row_major(lax.psum_scatter(wide_two, BOTH, scatter_dimension=0, tiled=False))
         grad_fc2 = wide_two.astype(f32).T
+    wide_one = row_major(lax.psum_scatter(wide_one, BOTH, scatter_dimension=0, tiled=False))
+    grad_fc1 = wide_one.astype(f32)
+    layer_out = to_features(layer_pieces)
     d_qkv, head_totals = attention_backward(
         qkv,
         gain_row,
@@ -1299,7 +1573,6 @@
     token_pieces, first_sums = input_backward(
         d_qkv, tok_in, d_res, modulation, qkv_parts, blocks, length
     )
-    grad_tokens = to_features(token_pieces)
 
     head_totals = head_totals.sum(axis=0)
     totals = jnp.concatenate(
@@ -1318,16 +1591,26 @@
         held = totals.shape[1]
         totals = jnp.pad(totals, ((0, 0), (0, -held % 1024)))
         totals = totals.reshape(2, 2, -1, 128).transpose(1, 0, 2, 3)
-        d_mod = d_mod.reshape(2, 2, images * 6, part).transpose(1, 0, 2, 3)
-        wide_attn, totals, d_mod = grads_everywhere(
-            count, width, (attn_rows, d_one, ln_one, d_qkv), totals, d_mod
+        d_mod = d_mod.reshape(2, 2, images, 6, part).transpose(1, 0, 3, 2, 4)
+        d_mod = d_mod.reshape(2, 2, 6 * images, part)
+        wide_attn, totals, d_mod, d_soft, _, grad_tokens, layer_out = grads_everywhere(
+            count,
+            width,
+            (attn_rows, d_one, ln_one, d_qkv),
+            token_pieces,
+            layer_out,
+            totals,
+            d_mod,
+            w_ada,
         )
-        d_mod, grad_tokens = lax.optimization_barrier((d_mod, grad_tokens))
         totals = totals.reshape(-1)[:held]
+        d_mod = d_mod.reshape(everyone, 6, images, part).transpose(0, 2, 1, 3)
         d_mod = d_mod.reshape(everyone * images, 6, part)
         grad_proj = wide_attn[0]
         grad_qkv = wide_attn[1:].transpose(1, 0, 2)
     else:
+        grad_tokens = to_features(token_pieces).T
+        layer_out = layer_out.T
         wide_attn = [
             jnp.einsum("td,tf->df", one, two, preferred_element_type=f32).astype(bf16)
             for one, two in [(attn_rows, d_one)] + [(ln_one, d_qkv[index]) for index in range(3)]
@@ -1344,18 +1627,21 @@
         d_mod = d_mod.reshape(everyone * images, 6, part)
     grad_ada = jnp.einsum("ic,isd->scd", soft_mine, d_mod, preferred_element_type=f32)
     grad_bada = jnp.sum(d_mod.astype(f32), axis=0)
-    d_soft = jnp.einsum("isd,scd->ic", d_mod, w_ada, preferred_element_type=f32)
-    d_soft = d_soft.reshape(rows, 1, images_row, ada_block)
-    d_soft = jnp.broadcast_to(d_soft, (rows, groups, images_row, ada_block))
-    d_soft = swap(d_soft.reshape(everyone, images_row, ada_block), BOTH)
-    d_soft = d_soft.reshape(rows, groups, images_row, ada_block).sum(axis=1)
-    d_soft = d_soft.transpose(1, 0, 2).reshape(images_row, width)
-    d_soft = lax.dynamic_slice(d_soft, (0, place * part), (images_row, part))
+    if aligned:
+        d_soft = d_soft.transpose(1, 0, 2).reshape(images_row, part)
+    else:
+        d_soft = jnp.einsum("isd,scd->ic", d_mod, w_ada, preferred_element_type=f32)
+        d_soft = d_soft.reshape(rows, 1, images_row, ada_block)
+        d_soft = jnp.broadcast_to(d_soft, (rows, groups, images_row, ada_block))
+        d_soft = swap(d_soft.reshape(everyone, images_row, ada_block), BOTH)
+        d_soft = d_soft.reshape(rows, groups, images_row, ada_block).sum(axis=1)
+        d_soft = d_soft.transpose(1, 0, 2).reshape(images_row, width)
+        d_soft = lax.dynamic_slice(d_soft, (0, place * part), (images_row, part))
     _, silu_pull = jax.vjp(jax.nn.silu, cond_float)
     grad_condition = silu_pull(d_soft)[0].astype(bf16)
     return (
-        layer_out.T,
-        grad_tokens.T,
+        layer_out,
+        grad_tokens,
         grad_condition,
         grad_qkv,
         totals[: cuts[0]].reshape(3, part),

time: 883 us -> 743 us (0.84)
  Pallas kernels: 774 us -> 664 us
  local copies, waits for them, and re-layouts: 49.4 us -> 29 us
  starting transfers between devices: 30 us -> 10.6 us
    pallas_call x2, Pallas kernels: 227 us -> 183 us  [grads_everywhere(): pl.pallas_call(functools.partial(grad_kernel, small), in_specs=[anywhere]...]
    pallas_call x1 -> x0, Pallas kernels: 31.4 us -> none  [plain_grads(): pl.pallas_call(plain_grad_kernel, grid=(ff // span,), in_specs=[pl.BlockS...]
    pallas_call x1, Pallas kernels: 165 us -> 138 us  [ffn(): pl.pallas_call(functools.partial(ffn_kernel, blocks, length, images), gri...]
    all_to_all x4 -> x2, starting transfers between devices: 29.9 us -> 10.5 us  [swap(): lax.all_to_all(pieces, axes, split_axis=0, concat_axis=0, tiled=False)]
    optimization_barrier x2 -> x0, local copies, waits for them, and re-layouts: 16.6 us -> none  [the longest x1 8.32 us: shards(): d_qkv, layer_out = lax.optimization_barrier((d_qkv, layer_out))]
  transfers between devices with their start and end apart: 6 -> 4, of which waited for: 0 -> 1; matrix products, arithmetic and copies ran while one was open for 6% -> 3% of each run, Pallas kernels for 66% -> 60%
where the time goes in v4:
time: 743 us; the launch traced here: 734 us
  Pallas kernels  664 us (89%)
  local copies, waits for them, and re-layouts  29 us (4%)
  between operations  15 us (2%)
  other arithmetic  14 us (2%)
  starting transfers between devices  10.6 us (1%)
    pallas_call x2, Pallas kernels, grads_everywhere(): pl.pallas_call(functools.partial(grad_kernel, small), in_specs=[anywhere]...  183 us
    pallas_call x1, Pallas kernels, ffn(): pl.pallas_call(functools.partial(ffn_kernel, blocks, length, images), gri...  138 us
    pallas_call x1, Pallas kernels, attention_backward(): pl.pallas_call(backward_kernel, grid=(images, width // PAIR), in_specs=in...  116 us
    pallas_call x1, Pallas kernels, start_everything(): pl.pallas_call(start_kernel, in_specs=[anywhere, inside, anywhere] + [ins...  114 us
    pallas_call x1, Pallas kernels, attention_forward(): pl.pallas_call(forward_kernel, grid=(images, width // PAIR), in_specs=ins...  55.4 us
    pallas_call x1, Pallas kernels, input_backward(): pl.pallas_call(functools.partial(input_kernel, blocks, length, images), g...  30.1 us
    pallas_call x1, Pallas kernels, qkv_forward(): pl.pallas_call(functools.partial(qkv_kernel, blocks, length, images), gri...  28 us
    unnamed x63, local copies, waits for them, and re-layouts  17.1 us
  transfers between devices with their start and end apart: 4, of which 1 were waited for; matrix products, arithmetic and copies ran while one was open for 3% of the time, Pallas kernels for 60%

profile of v4, /device:TPU:0, one launch (start us, length us, event | category | flops | bytes accessed | tf_op | source)
XLA Modules:
  0.0 734.5 jit_solution(9429114833506187794)
XLA Ops:
  7.2 1.1 copy.37
  8.3 1.8 pad_maximum_fusion
  10.2 0.7 reshape.190
  10.9 1.3 convert_element_type.46.bias_ref
  12.2 0.7 constant_dynamic-update-slice_fusion.9
  12.8 0.7 constant_dynamic-update-slice_fusion.8
  13.5 0.7 constant_dynamic-update-slice_fusion.7
  14.2 0.7 constant_dynamic-update-slice_fusion.6
  14.8 0.6 pad_bitcast_fusion.1.vec_ref
  15.4 1.3 bitcast_bitcast_fusion.soft_ref
  16.7 113.9 %start_exchange.1 = (bf16[4,2720,256]{2,1,0:T(8,128)(2,1)}, bf16[4,2,2,2,3,128,256]{6,5,4,3,2,1,0:T(8,128)(2,1)}, bf16[10880,256]{1,0:T(8,128)(2,1)}, bf16[10880...) custom-call(bf16[256,10880]{1,0:T(8,128)(2,1)} %tok_ref.1, ...), custom_call_target="tpu_custom_call" | custom-call | flops 99999997952 | bytes 30000000 | tf_op jit(solution)/shard_map/start_exchange/pallas_call | solution.py:1330
  130.7 5.2 all-to-all-start
  136.5 0.6 copy.56
  137.1 0.6 copy.58
  137.7 0.6 copy.57
  139.0 0.5 select_convert_fusion.km_ref
  139.5 28.0 %qkv_forward.1 = (bf16[2720,1024]{1,0:T(8,128)(2,1)S(1)}, f32[3,2720,1024]{2,1,0:T(8,128)}) custom-call(bf16[4,2720,256]{2,1,0:T(8,128)(2,1)} %get-tuple-element.53.x_ref, f32[4,6,1024]{2,1,0:T(8,128)S(1)} %reshape.194.mod_ref, f32[3,1,1024]{2,1,0:T(1,128)S(1)} %reshape.162.bias_ref, bf16[32,3,128,256]{3,2,1,0:T(8,128)(2,1)} %bitcast.132), custom_call_target="tpu_custom_call" | custom-call | flops 17112760320 | bytes 50855936 | tf_op jit(solution)/shard_map/qkv_forward/pallas_call | solution.py:406
  167.6 2.4 copy-done.8
  170.0 55.4 %attention_forward.1 = (bf16[4,680,1024]{2,1,0:T(8,128)(2,1)}, f32[4,680,1024]{2,1,0:T(8,128)}) custom-call(f32[3,4,680,1024]{3,2,1,0:T(8,128)} %bitcast.97, f32[3,4,680,1024]{3,2,1,0:T(8,128)} %bitcast.98, f32[3,4,680,1024]{3,2,1,0:T(8,128)} %bitcast.99, f32[1,1024]{1,0:T(1,128)S(1)} %broadcast_in_dim_reshape.3.gain_ref, ...), custom_call_target="tpu_custom_call" | custom-call | flops 15151923200 | bytes 50135040 | tf_op jit(solution)/shard_map/attention_forward/pallas_call | solution.py:144
  225.5 138.1 %ffn_both.1 = (bf16[4,2720,256]{2,1,0:T(8,128)(2,1)}, bf16[2720,1024]{1,0:T(8,128)(2,1)}, bf16[2720,4096]{1,0:T(8,128)(2,1)}, bf16[2720,1024]{1,0:T(8,128)(2,1)}...) custom-call(bf16[4,2720,256]{2,1,0:T(8,128)(2,1)} %get-tuple-element, ...), custom_call_target="tpu_custom_call" | custom-call | flops 102676561920 | bytes 119144448 | tf_op jit(solution)/shard_map/ffn_both/pallas_call | solution.py:342
  363.5 86.8 %second_grads.1 = (f32[4,128,256]{2,1,0:T(8,128)}, bf16[8,4,128,1024]{3,2,1,0:T(8,128)(2,1)}) custom-call(bf16[2720,1024]{1,0:T(8,128)(2,1)} %get-tuple-element.63.refs_0_, bf16[2720,4096]{1,0:T(8,128)(2,1)} %get-tuple-element.64.refs_1_, bf16[2720,1024]{1,0:T(8,128)(2,1)} %get-tuple-element.65.refs_2_, bf16[2720,4096]{1,0:T(8,128)(2,1)} %get-tuple-element.66.refs_3_), custom_call_target="tpu_custom_call" | custom-call | flops 45634027520 | bytes 41811968 | tf_op jit(solution)/shard_map/second_grads/pallas_call | solution.py:1131
  450.4 5.3 all-to-all-start.1
  455.8 115.8 %attention_backward.1 = (bf16[3,4,680,1024]{3,2,1,0:T(8,128)(2,1)}, f32[4,8,1024]{2,1,0:T(8,128)}) custom-call(f32[3,4,680,1024]{3,2,1,0:T(8,128)} %bitcast.100, f32[3,4,680,1024]{3,2,1,0:T(8,128)} %bitcast.101, f32[3,4,680,1024]{3,2,1,0:T(8,128)} %bitcast.102, f32[1,1024]{1,0:T(1,128)} %copy-done.6, bf16[4,680,128]{2,1,0:T(8,128)(2,1)} %copy-done.2, ...), custom_call_target="tpu_custom_call" | custom-call | flops 37879808000 | bytes 83558400 | tf_op jit(solution)/shard_map/attention_backward/pallas_call | solution.py:164
  571.6 0.9 reduce_sum.27
  573.0 0.7 reduce.14
  573.7 0.7 reduce.15
  574.4 0.7 reduce.16
  575.5 0.6 copy.69
  576.1 1.0 copy.45
  577.1 1.5 all-to-all-done.1
  578.6 30.1 %input_backward.1 = (bf16[4,2720,256]{2,1,0:T(8,128)(2,1)S(1)}, f32[4,2,1024]{2,1,0:T(2,128)S(1)}) custom-call(bf16[3,2720,1024]{2,1,0:T(8,128)(2,1)} %bitcast.130, bf16[4,2720,256]{2,1,0:T(8,128)(2,1)} %get-tuple-element.53.x_ref, f32[2720,1024]{1,0:T(8,128)} %get-tuple-element.74.res_ref, f32[4,6,1024]{2,1,0:T(8,128)S(1)} %copy-done.5, ...), custom_call_target="tpu_custom_call" | custom-call | flops 17112760320 | bytes 45285376 | tf_op jit(solution)/shard_map/input_backward/pallas_call | solution.py:464
  608.7 2.5 copy-done.7
  611.3 0.6 copy.50.refs_7_
  612.0 95.9 %attn_grads.1 = (f32[4,128,256]{2,1,0:T(8,128)}, f32[24,128]{1,0:T(8,128)}, bf16[4,2,2,2,24,256]{5,4,3,2,1,0:T(8,128)(2,1)}, f32[2,16,128]{2,1,0:T(8,128)}, bf16...) custom-call(bf16[2720,1024]{1,0:T(8,128)(2,1)} %bitcast.128, ...), custom_call_target="tpu_custom_call" | custom-call | flops 45634027520 | bytes 41811968 | tf_op jit(solution)/shard_map/attn_grads/pallas_call | solution.py:1131
  707.9 1.1 reshape.187
  709.6 1.2 copy.48
  710.8 0.7 slice.75
  711.5 0.6 slice.76
  712.1 1.2 slice.92
  713.2 0.8 convert_reduce_fusion
  714.0 0.6 slice_bitcast_fusion.6
  714.6 0.6 slice_bitcast_fusion.5
  715.2 0.6 fusion.7
  715.8 0.7 slice_bitcast_fusion.1
  716.5 0.8 slice_bitcast_fusion
  717.3 1.9 bitcast_convert_fusion
  719.2 5.5 copy.81
  724.7 2.5 copy.82
  (97 shorter events, 2.8 us)
Async XLA Ops:
  7.2 131.2 %copy-start = (s32[16,680]{1,0:T(8,128)S(1)}, s32[16,680]{1,0:T(8,128)}, u32[]{:S(2)}) copy-start(s32[16,680]{1,0:T(8,128)} %param.17) | copy-start | bytes 130564
  7.2 218.3 %all-gather.3.cloned.1.call-start = ((), (), s32[]{:S(2)}) async-start(), calls=%async_computation.4 | async-start | bytes 19464192 | tf_op jit(solution)/shard_map/all_gather | solution.py:1429
  130.7 5.3 copy-start.13
  130.7 5.4 copy-start.11
  130.7 94.7 %all-to-all-start = ((bf16[4,2720,256]{2,1,0:T(8,128)(2,1)}), bf16[4,2720,256]{2,1,0:T(8,128)(2,1)}, u32[]{:S(2)}, u32[]{:S(2)}) async-start(bf16[4,2720,256]{2,1,0:T(8,128)(2,1)} %bitcast.104), calls=%async_computation | async-start | bytes 11141120 | tf_op jit(solution)/shard_map/all_to_all | solution.py:1377
  136.0 581.3 %reduce-scatter.2.cloned.1.call-start = ((), (), s32[]{:S(2)}) async-start(), calls=%async_computation.3 | async-start | bytes 8650752 | tf_op jit(solution)/shard_map/reduce_scatter | solution.py:1559
  136.3 31.3 %copy-start.4 = (f32[4,6,1024]{2,1,0:T(8,128)}, f32[4,6,1024]{2,1,0:T(8,128)S(1)}, u32[]{:S(2)}) copy-start(f32[4,6,1024]{2,1,0:T(8,128)S(1)} %reshape.194.mod_ref) | copy-start | bytes 294916
  136.5 33.4 %copy-start.6 = (f32[1,1024]{1,0:T(1,128)}, f32[1,1024]{1,0:T(1,128)S(1)}, u32[]{:S(2)}) copy-start(f32[1,1024]{1,0:T(1,128)S(1)} %broadcast_in_dim_reshape.3.gain_ref) | copy-start | bytes 12292
  139.0 31.0 %copy-start.2 = (bf16[4,680,128]{2,1,0:T(8,128)(2,1)}, bf16[4,680,128]{2,1,0:T(8,128)(2,1)S(1)}, u32[]{:S(2)}) copy-start(bf16[4,680,128]{2,1,0:T(8,128)(2,1)S(1)} %compare_convert_fusion.qm_ref) | copy-start | bytes 2088964
  139.5 30.5 %copy-start.3 = (bf16[4,680,128]{2,1,0:T(8,128)(2,1)}, bf16[4,680,128]{2,1,0:T(8,128)(2,1)S(1)}, u32[]{:S(2)}) copy-start(bf16[4,680,128]{2,1,0:T(8,128)(2,1)S(1)} %select_convert_fusion.km_ref) | copy-start | bytes 2088964
  167.6 2.4 copy-start.8
  450.3 5.3 copy-start.12
  450.4 128.3 %all-to-all-start.1 = ((bf16[4,2720,256]{2,1,0:T(8,128)(2,1)}), bf16[4,2720,256]{2,1,0:T(8,128)(2,1)}, u32[]{:S(2)}, u32[]{:S(2)}) async-start(bf16[4,2720,256]{2,1,0:T(8,128)(2,1)} %get-tuple-element.72), calls=%async_computation.1 | async-start | bytes 11141120 | tf_op jit(solution)/shard_map/all_to_all | solution.py:1377
  455.7 117.3 %copy-start.20 = (f32[1,1024]{1,0:T(1,128)S(1)}, f32[1,1024]{1,0:T(1,128)}, u32[]{:S(2)}) copy-start(f32[1,1024]{1,0:T(1,128)} %get-tuple-element.78) | copy-start | bytes 12292
  455.7 118.0 %copy-start.16 = (f32[1,4096]{1,0:T(1,128)S(1)}, f32[1,4096]{1,0:T(1,128)}, u32[]{:S(2)}) copy-start(f32[1,4096]{1,0:T(1,128)} %get-tuple-element.79) | copy-start | bytes 49156
  455.7 118.7 %copy-start.19 = (f32[1,1024]{1,0:T(1,128)S(1)}, f32[1,1024]{1,0:T(1,128)}, u32[]{:S(2)}) copy-start(f32[1,1024]{1,0:T(1,128)} %get-tuple-element.80) | copy-start | bytes 12292
  455.8 120.4 %copy-start.10 = (f32[4,128,256]{2,1,0:T(8,128)S(1)}, f32[4,128,256]{2,1,0:T(8,128)}, u32[]{:S(2)}) copy-start(f32[4,128,256]{2,1,0:T(8,128)} %get-tuple-element.89) | copy-start | bytes 1572868
  455.8 122.8 %copy-start.5 = (f32[4,6,1024]{2,1,0:T(8,128)S(1)}, f32[4,6,1024]{2,1,0:T(8,128)}, u32[]{:S(2)}) copy-start(f32[4,6,1024]{2,1,0:T(8,128)} %copy-done.4) | copy-start | bytes 294916
  608.7 2.5 copy-start.7
  611.9 97.4 %copy-start.14 = (bf16[128,128]{1,0:T(8,128)(2,1)S(1)}, bf16[128,128]{1,0:T(8,128)(2,1)}, u32[]{:S(2)}) copy-start(bf16[128,128]{1,0:T(8,128)(2,1)} %get-tuple-element.91) | copy-start | bytes 98308
  707.9 6.1 copy-start.18
  707.9 7.3 copy-start.15
  707.9 7.3 copy-start.17
  707.9 7.9 %copy-start.9 = (f32[4,128,256]{2,1,0:T(8,128)S(1)}, f32[4,128,256]{2,1,0:T(8,128)}, u32[]{:S(2)}) copy-start(f32[4,128,256]{2,1,0:T(8,128)} %get-tuple-element.86) | copy-start | bytes 1572868
  717.3 7.5 %slice-start = ((s8[5570560]{0:T(1024)(128)(4,1)}), s8[4194304]{0:T(1024)(128)(4,1)S(1)}, s32[]{:S(2)}) async-start(s8[5570560]{0:T(1024)(128)(4,1)} %bitcast.105), calls=%async_computation.5 | async-start | bytes 8388608
  719.2 5.5 slice-start.1
  719.2 8.0 %copy-start.1 = (s32[16,680]{1,0:T(8,128)S(1)}, s32[16,680]{1,0:T(8,128)}, u32[]{:S(2)}) copy-start(s32[16,680]{1,0:T(8,128)} %param.17) | copy-start | bytes 130564
Sparse Core Ops, SparseCore 0:
  11.5 175.3 all-gather.2
  450.5 170.5 reduce-scatter.1
